TPU v7x, 32 devices: a whole 2x2x4 slice. The times are simulated.
32 devices in a mesh: fsdp: 8 (over y, x, core), seq: 4 (over z).
Axes of the slice: x: 2, y: 2, z: 4, core: 2. Of those that a mesh axis runs over, the one named last changes fastest.
Arguments:
- inputs: float32 [8, 3072, 768], P('fsdp', 'seq'), may hold values from -6 to 6
- conditioning: float32 [8, 128], P('fsdp'), may hold values from -6 to 6
- cotangent: float32 [8, 3072, 768], P('fsdp', 'seq'), may hold values from -6 to 6
- attn_gain: float32 [768], P('fsdp'), may hold values from 0.25 to 1.75
- mlp_gain: float32 [768], P('fsdp'), may hold values from 0.25 to 1.75
- qkv_weight: float32 [768, 2304], P('fsdp'), may hold values from -0.21875 to 0.21875
- out_weight: float32 [768, 768], P('fsdp'), may hold values from -3 to 3
- up_weight: float32 [768, 3072], P('fsdp'), may hold values from -0.21875 to 0.21875
- up_bias: float32 [3072], P('fsdp'), may hold values from -3 to 3
- down_weight: float32 [3072, 768], P('fsdp'), may hold values from -0.109375 to 0.109375
- down_bias: float32 [768], P('fsdp'), may hold values from -3 to 3
- mod_weight: float32 [128, 4608], P(None, 'fsdp'), may hold values from -0.375 to 0.375
- mod_bias: float32 [4608], P('fsdp'), may hold values from -2 to 2
Outputs:
- output: float32 [8, 3072, 768], P('fsdp', 'seq')
- inputs_grad: float32 [8, 3072, 768], P('fsdp', 'seq')
- conditioning_grad: float32 [8, 128], P('fsdp')
- attn_gain_grad: float32 [768], P('fsdp')
- mlp_gain_grad: float32 [768], P('fsdp')
- qkv_weight_grad: float32 [768, 2304], P('fsdp')
- out_weight_grad: float32 [768, 768], P('fsdp')
- up_weight_grad: float32 [768, 3072], P('fsdp')
- up_bias_grad: float32 [3072], P('fsdp')
- down_weight_grad: float32 [3072, 768], P('fsdp')
- down_bias_grad: float32 [768], P('fsdp')
- mod_weight_grad: float32 [128, 4608], P(None, 'fsdp')
- mod_bias_grad: float32 [4608], P('fsdp')
All inputs are finite; a program needn't handle non-finite values.
Results may differ from a plain program's by a relative error of at most 0.015.
The roundings to bfloat16 on the way count: a program that leaves them out, or rounds other values in their place, can miss the bound.
Values may be sent and summed in bfloat16 or wider, within the bound.
A program may use at most 192 MiB of HBM per device.

v0:
```python
from functools import partial
import math

import jax
import jax.numpy as jnp
from jax import lax
from jax.sharding import PartitionSpec as P

H = 12
HD = 64


HIGHEST = lax.Precision.HIGHEST
EPSILON = 1e-05


def normalize(values):
    centre = jnp.mean(values, axis=-1, keepdims=True)
    shifted = values - centre
    variance = jnp.mean(shifted * shifted, axis=-1, keepdims=True)
    inv_std = lax.rsqrt(variance + EPSILON)
    return (shifted * inv_std, inv_std)


def norm_back(grad_hat, normed_hat, inv_std):
    mean_grad = jnp.mean(grad_hat, axis=-1, keepdims=True)
    mean_mixed = jnp.mean(grad_hat * normed_hat, axis=-1, keepdims=True)
    return inv_std * (grad_hat - mean_grad - normed_hat * mean_mixed)


def rotary_tables(length, head_dim):
    half_dim = head_dim // 2
    inv_freq = jnp.exp(
        -math.log(10000.0) * jnp.arange(half_dim, dtype=jnp.float32) * (2.0 / head_dim)
    )
    angles = jnp.arange(length, dtype=jnp.float32)[:, None] * inv_freq[None, :]
    return (jnp.cos(angles), jnp.sin(angles))


def rotate(values, cosine_table, sine_table):
    half_dim = values.shape[-1] // 2
    first_half = values[..., :half_dim]
    second_half = values[..., half_dim:]
    cos_part = cosine_table[:, None, :]
    sin_part = sine_table[:, None, :]
    return jnp.concatenate(
        [
            first_half * cos_part - second_half * sin_part,
            second_half * cos_part + first_half * sin_part,
        ],
        axis=-1,
    )


def rotate_back(values, cosine_table, sine_table):
    half_dim = values.shape[-1] // 2
    first_half = values[..., :half_dim]
    second_half = values[..., half_dim:]
    cos_part = cosine_table[:, None, :]
    sin_part = sine_table[:, None, :]
    return jnp.concatenate(
        [
            first_half * cos_part + second_half * sin_part,
            second_half * cos_part - first_half * sin_part,
        ],
        axis=-1,
    )


def per_device(
    inputs,
    conditioning,
    cotangent,
    attn_gain,
    mlp_gain,
    qkv_weight,
    out_weight,
    up_weight,
    up_bias,
    down_weight,
    down_bias,
    mod_weight,
    mod_bias,
):
    qkv_full, out_full, up_full, down_full, mod_full = (
        lax.all_gather(qkv_weight.astype(jnp.bfloat16), "fsdp", axis=0, tiled=True),
        lax.all_gather(out_weight.astype(jnp.bfloat16), "fsdp", axis=0, tiled=True),
        lax.all_gather(up_weight.astype(jnp.bfloat16), "fsdp", axis=0, tiled=True),
        lax.all_gather(down_weight.astype(jnp.bfloat16), "fsdp", axis=0, tiled=True),
        lax.all_gather(mod_weight.astype(jnp.bfloat16), "fsdp", axis=1, tiled=True),
    )
    attn_gain_full, mlp_gain_full, up_bias_full, down_bias_full, mod_bias_full = (
        lax.all_gather(attn_gain, "fsdp", axis=0, tiled=True),
        lax.all_gather(mlp_gain, "fsdp", axis=0, tiled=True),
        lax.all_gather(up_bias, "fsdp", axis=0, tiled=True),
        lax.all_gather(down_bias, "fsdp", axis=0, tiled=True),
        lax.all_gather(mod_bias, "fsdp", axis=0, tiled=True),
    )
    seq_count = lax.axis_size("seq")
    tokens = inputs[0]
    tok_count = tokens.shape[0]
    model_width = tokens.shape[1]
    length = tok_count * seq_count
    group_heads = H // seq_count
    group_width = group_heads * HD
    scaling = 1.0 / math.sqrt(HD)
    block_rows = min(512, length)
    block_count = length // block_rows
    cond_act, silu_pull = jax.vjp(jax.nn.silu, conditioning[0])
    cond_low = cond_act.astype(jnp.bfloat16)
    modulation = (
        jnp.dot(cond_low[None, :], mod_full, preferred_element_type=jnp.float32)[0] + mod_bias_full
    )
    shift_attn, scale_attn, gate_attn, shift_mlp, scale_mlp, gate_mlp = jnp.split(modulation, 6)
    hat_attn, inv_attn = normalize(tokens)
    normed_attn = hat_attn * attn_gain_full
    attn_in = (normed_attn * (1.0 + scale_attn) + shift_attn).astype(jnp.bfloat16)
    qkv_tok = jnp.dot(attn_in, qkv_full, preferred_element_type=jnp.float32).astype(jnp.bfloat16)
    qkv_heads = lax.all_to_all(
        qkv_tok.reshape(tok_count, 3, seq_count, group_width),
        "seq",
        split_axis=2,
        concat_axis=0,
        tiled=True,
    )
    qkv_heads = qkv_heads.reshape(length, 3, group_heads, HD)
    cosine_table, sine_table = rotary_tables(length, HD)
    queries = rotate(qkv_heads[:, 0].astype(jnp.float32), cosine_table, sine_table).astype(
        jnp.bfloat16
    )
    keys_low = rotate(qkv_heads[:, 1].astype(jnp.float32), cosine_table, sine_table).astype(
        jnp.bfloat16
    )
    values_low = qkv_heads[:, 2]
    query_blocks = queries.reshape(block_count, block_rows, group_heads, HD)

    def attend(query_block):
        scores = (
            jnp.einsum("qgd,kgd->gqk", query_block, keys_low, preferred_element_type=jnp.float32)
            * scaling
        )
        row_max = jnp.max(scores, axis=-1, keepdims=True)
        exponent = jnp.exp(scores - row_max)
        row_total = jnp.sum(exponent, axis=-1, keepdims=True)
        probs_low = (exponent / row_total).astype(jnp.bfloat16)
        mixed_block = jnp.einsum(
            "gqk,kgd->qgd", probs_low, values_low, preferred_element_type=jnp.float32
        )
        return (mixed_block, (row_max + jnp.log(row_total))[..., 0])

    mixed_heads, log_totals = lax.map(attend, query_blocks)
    mixed_send = mixed_heads.reshape(length, 1, group_width).astype(jnp.bfloat16)
    mixed_tok = lax.all_to_all(mixed_send, "seq", split_axis=0, concat_axis=1, tiled=True).reshape(
        tok_count, model_width
    )
    attn_out = jnp.dot(mixed_tok, out_full, preferred_element_type=jnp.float32)
    hidden = tokens + gate_attn * attn_out
    hat_mlp, inv_mlp = normalize(hidden)
    normed_mlp = hat_mlp * mlp_gain_full
    mlp_in = (normed_mlp * (1.0 + scale_mlp) + shift_mlp).astype(jnp.bfloat16)
    pre_act = jnp.dot(mlp_in, up_full, preferred_element_type=jnp.float32) + up_bias_full
    gelu_act, gelu_pull = jax.vjp(partial(jax.nn.gelu, approximate=True), pre_act)
    up_act = gelu_act.astype(jnp.bfloat16)
    branch = jnp.dot(up_act, down_full, preferred_element_type=jnp.float32) + down_bias_full
    output = hidden + gate_mlp * branch
    grad_out = cotangent[0]
    grad_branch = gate_mlp * grad_out
    branch_low = grad_branch.astype(jnp.bfloat16)
    down_weight_grad = jnp.einsum(
        "tf,td->fd", up_act, branch_low, preferred_element_type=jnp.float32
    )
    grad_act = jnp.einsum("td,fd->tf", branch_low, down_full, preferred_element_type=jnp.float32)
    grad_pre = gelu_pull(grad_act)[0]
    pre_low = grad_pre.astype(jnp.bfloat16)
    up_weight_grad = jnp.einsum("td,tf->df", mlp_in, pre_low, preferred_element_type=jnp.float32)
    grad_mlp_in = jnp.einsum("tf,df->td", pre_low, up_full, preferred_element_type=jnp.float32)
    grad_normed_mlp = grad_mlp_in * (1.0 + scale_mlp)
    grad_hidden = grad_out + norm_back(grad_normed_mlp * mlp_gain_full, hat_mlp, inv_mlp)
    attn_low = (gate_attn * grad_hidden).astype(jnp.bfloat16)
    out_weight_grad = jnp.einsum(
        "td,te->de", mixed_tok, attn_low, preferred_element_type=jnp.float32
    )
    grad_mixed = jnp.einsum(
        "te,de->td", attn_low, out_full, preferred_element_type=jnp.float32
    ).astype(jnp.bfloat16)
    grad_heads = lax.all_to_all(
        grad_mixed.reshape(tok_count, seq_count, group_width),
        "seq",
        split_axis=1,
        concat_axis=0,
        tiled=True,
    )
    grad_heads = grad_heads.reshape(block_count, block_rows, group_heads, HD)

    def attend_back(running, block_items):
        keys_acc, values_acc = running
        query_block, grad_block, log_block = block_items
        scores = (
            jnp.einsum("qgd,kgd->gqk", query_block, keys_low, preferred_element_type=jnp.float32)
            * scaling
        )
        softmax_val = jnp.exp(scores - log_block[..., None])
        probs_low = softmax_val.astype(jnp.bfloat16)
        values_acc = values_acc + jnp.einsum(
            "gqk,qgd->kgd", probs_low, grad_block, preferred_element_type=jnp.float32
        )
        grad_probs = jnp.einsum(
            "qgd,kgd->gqk", grad_block, values_low, preferred_element_type=jnp.float32
        )
        centre = jnp.sum(grad_probs * softmax_val, axis=-1, keepdims=True)
        score_low = (softmax_val * (grad_probs - centre)).astype(jnp.bfloat16)
        query_grad = (
            jnp.einsum("gqk,kgd->qgd", score_low, keys_low, preferred_element_type=jnp.float32)
            * scaling
        )
        keys_acc = (
            keys_acc
            + jnp.einsum("gqk,qgd->kgd", score_low, query_block, preferred_element_type=jnp.float32)
            * scaling
        )
        return ((keys_acc, values_acc), query_grad)

    zero_block = jnp.zeros((length, group_heads, HD), jnp.float32)
    (keys_grad, values_grad), query_grads = lax.scan(
        attend_back, (zero_block, zero_block), (query_blocks, grad_heads, log_totals)
    )
    grad_stack = jnp.stack(
        [
            rotate_back(query_grads.reshape(length, group_heads, HD), cosine_table, sine_table),
            rotate_back(keys_grad, cosine_table, sine_table),
            values_grad,
        ],
        axis=1,
    )
    grad_send = grad_stack.reshape(length, 3, 1, group_width).astype(jnp.bfloat16)
    grad_qkv = lax.all_to_all(grad_send, "seq", split_axis=0, concat_axis=2, tiled=True).reshape(
        tok_count, 3 * model_width
    )
    qkv_weight_grad = jnp.einsum("td,te->de", attn_in, grad_qkv, preferred_element_type=jnp.float32)
    grad_attn_in = jnp.einsum("te,de->td", grad_qkv, qkv_full, preferred_element_type=jnp.float32)
    grad_normed_attn = grad_attn_in * (1.0 + scale_attn)
    inputs_grad = grad_hidden + norm_back(grad_normed_attn * attn_gain_full, hat_attn, inv_attn)
    grad_modulation = jnp.concatenate(
        [
            jnp.sum(grad_attn_in, axis=0),
            jnp.sum(grad_attn_in * normed_attn, axis=0),
            jnp.sum(grad_hidden * attn_out, axis=0),
            jnp.sum(grad_mlp_in, axis=0),
            jnp.sum(grad_mlp_in * normed_mlp, axis=0),
            jnp.sum(grad_out * branch, axis=0),
        ]
    )
    attn_gain_grad = jnp.sum(grad_normed_attn * hat_attn, axis=0)
    mlp_gain_grad = jnp.sum(grad_normed_mlp * hat_mlp, axis=0)
    up_bias_grad = jnp.sum(grad_pre, axis=0)
    down_bias_grad = jnp.sum(grad_branch, axis=0)
    mod_weight_grad = cond_low.astype(jnp.float32)[:, None] * grad_modulation[None, :]
    mod_wide = mod_full.astype(jnp.float32)
    grad_cond_act = lax.psum(jnp.dot(mod_wide, grad_modulation, precision=HIGHEST), "seq")
    conditioning_grad = silu_pull(grad_cond_act)[0]
    (
        part_attn_gain,
        part_mlp_gain,
        part_qkv,
        part_out,
        part_up,
        part_up_bias,
        part_down,
        part_down_bias,
        part_mod,
        part_mod_bias,
    ) = (
        lax.psum_scatter(attn_gain_grad, "fsdp", scatter_dimension=0, tiled=True),
        lax.psum_scatter(mlp_gain_grad, "fsdp", scatter_dimension=0, tiled=True),
        lax.psum_scatter(qkv_weight_grad, "fsdp", scatter_dimension=0, tiled=True),
        lax.psum_scatter(out_weight_grad, "fsdp", scatter_dimension=0, tiled=True),
        lax.psum_scatter(up_weight_grad, "fsdp", scatter_dimension=0, tiled=True),
        lax.psum_scatter(up_bias_grad, "fsdp", scatter_dimension=0, tiled=True),
        lax.psum_scatter(down_weight_grad, "fsdp", scatter_dimension=0, tiled=True),
        lax.psum_scatter(down_bias_grad, "fsdp", scatter_dimension=0, tiled=True),
        lax.psum_scatter(mod_weight_grad, "fsdp", scatter_dimension=1, tiled=True),
        lax.psum_scatter(grad_modulation, "fsdp", scatter_dimension=0, tiled=True),
    )
    owned_grads = (
        lax.psum(part_attn_gain.astype(jnp.bfloat16), "seq").astype(jnp.float32),
        lax.psum(part_mlp_gain.astype(jnp.bfloat16), "seq").astype(jnp.float32),
        lax.psum(part_qkv.astype(jnp.bfloat16), "seq").astype(jnp.float32),
        lax.psum(part_out.astype(jnp.bfloat16), "seq").astype(jnp.float32),
        lax.psum(part_up.astype(jnp.bfloat16), "seq").astype(jnp.float32),
        lax.psum(part_up_bias.astype(jnp.bfloat16), "seq").astype(jnp.float32),
        lax.psum(part_down.astype(jnp.bfloat16), "seq").astype(jnp.float32),
        lax.psum(part_down_bias.astype(jnp.bfloat16), "seq").astype(jnp.float32),
        lax.psum(part_mod.astype(jnp.bfloat16), "seq").astype(jnp.float32),
        lax.psum(part_mod_bias.astype(jnp.bfloat16), "seq").astype(jnp.float32),
    )
    return (output[None], inputs_grad[None], conditioning_grad[None]) + tuple(owned_grads)


def solution(mesh):
    in_specs = (
        P("fsdp", "seq", None),
        P("fsdp", None),
        P("fsdp", "seq", None),
        P("fsdp"),
        P("fsdp"),
        P("fsdp", None),
        P("fsdp", None),
        P("fsdp", None),
        P("fsdp"),
        P("fsdp", None),
        P("fsdp"),
        P(None, "fsdp"),
        P("fsdp"),
    )
    out_specs = (
        P("fsdp", "seq", None),
        P("fsdp", "seq", None),
        P("fsdp", None),
        P("fsdp"),
        P("fsdp"),
        P("fsdp", None),
        P("fsdp", None),
        P("fsdp", None),
        P("fsdp"),
        P("fsdp", None),
        P("fsdp"),
        P(None, "fsdp"),
        P("fsdp"),
    )
    return jax.shard_map(
        per_device, mesh=mesh, in_specs=in_specs, out_specs=out_specs, check_vma=False
    )
```

profile of v0, /device:TPU:0, one launch (start us, length us, event | category | flops | bytes accessed | tf_op | source)
XLA Modules:
  0.0 1490.2 jit_solution(8368317932655331914)
XLA Ops:
  17.7 25.7 %all-reduce.10 = (f32[4608]{0:T(1024)S(1)}, f32[768]{0:T(1024)S(1)}, f32[768]{0:T(1024)}, f32[768]{0:T(1024)}) all-reduce(f32[4608]{0:T(1024)S(1)} %dynamic-update-slice, f32[768]{0:T(1024)S(1)} %dynamic-update-slice.1, f32[768]{0:T(1024)S(1)} %dynamic-update-slice.2, ...), channel_id=1, replica_groups=mesh['fsdp'=8,'seq'=4] {'fsdp'}, use_global_device_ids=true, to_apply=%add | all-reduce | flops 6912 | bytes 55296
  46.2 27.4 %all-gather.9.cloned.1.call-done = bf16[768,2304]{1,0:T(8,128)(2,1)} async-done(((bf16[96,2304]{1,0:T(8,128)(2,1)}), bf16[768,2304]{1,0:T(8,128)(2,1)}) %all-gather.9.cloned.1.call-update) | async-done | bytes 3538960 | tf_op jit(solution)/shard_map/all_gather | solution.py:86
  96.3 74.7 %all-to-all-done = bf16[768,3,4,192]{0,3,1,2:T(8,128)(2,1)S(1)} async-done(((bf16[768,3,4,192]{0,3,1,2:T(8,128)(2,1)}), bf16[768,3,4,192]{0,3,1,2:T(8,128)(2,1)S(1)}, u32[]{:S(2)}, u32[]{:S(2)}) %all-to-all-start) | async-done | bytes 3538976 | tf_op jit(solution)/shard_map/all_to_all | solution.py:119
  189.8 163.7 %while.27 = (s32[]{:T(128)}, bf16[6,512,3,64]{1,3,2,0:T(8,128)(2,1)}, f32[6,3,512]{2,1,0:T(4,128)}, bf16[6,512,3,64]{1,3,2,0:T(8,128)(2,1)S(1)}, bf16[3072,3,64]...) while((s32[]{:T(128)}, bf16[6,512,3,64]{1,3,2,0:T(8,128)(2,1)}, ...), condition=%wide.region_5.6_spmd, body=%wide.region_2.5_spmd.sunk | while | flops 1250425344 | bytes 59624528 | solution.py:151
  359.2 13.0 reshape.332
  372.7 18.1 %reduce.3 = bf16[3072,192]{1,0:T(8,128)(2,1)S(1)} reduce(bf16[3072,1,192]{2,1,0:T(2,128)(2,1)} %reshape.332, bf16[]{:T(256)} %broadcast.238), dimensions={1}, to_apply=%reshape.332.reduce_sub_computation | reduce | bytes 2359298 | tf_op jit(solution)/shard_map/convert_element_type | solution.py:152
  406.2 19.2 %all-to-all-done.1 = bf16[4,2,73728]{2,1,0:T(2,128)(2,1)S(1)} async-done(((bf16[4,2,73728]{2,1,0:T(2,128)(2,1)}), bf16[4,2,73728]{2,1,0:T(2,128)(2,1)S(1)}, u32[]{:S(2)}, u32[]{:S(2)}) %all-to-all-start.1) | async-done | bytes 1179680 | tf_op jit(solution)/shard_map/all_to_all | solution.py:153
  460.4 14.1 fusion.97
  497.5 28.1 %all-to-all-done.2 = bf16[768,4,192]{0,2,1:T(8,128)(2,1)} async-done(((bf16[768,4,192]{0,2,1:T(8,128)(2,1)}), bf16[768,4,192]{0,2,1:T(8,128)(2,1)}, u32[]{:S(2)}, u32[]{:S(2)}) %all-to-all-start.2) | async-done | bytes 1179680 | tf_op jit(solution)/shard_map/all_to_all | solution.py:186
  535.2 403.9 %while.28 = (s32[]{:T(128)}, f32[3072,3,64]{0,2,1:T(8,128)S(1)}, f32[3072,3,64]{0,2,1:T(8,128)}, f32[6,512,3,64]{1,0,3,2:T(8,128)}, bf16[6,512,3,64]{1,3,2,0:T(8...) while((s32[]{:T(128)}, f32[3072,3,64]{0,2,1:T(8,128)S(1)}, ...), condition=%wide.region_12.13_spmd.clone, body=%wide.region_10.12_spmd.clone.sunk | while | flops 3079567872 | bytes 199798960 | solution.py:224
  557.7 13.4 multiply_convert_fusion.6
  624.3 13.4 multiply_convert_fusion.6
  679.1 12.6 multiply_reduce_fusion.14
  691.7 13.4 multiply_convert_fusion.6
  746.4 12.6 multiply_reduce_fusion.14
  759.0 13.4 multiply_convert_fusion.6
  826.3 13.4 multiply_convert_fusion.6
  893.6 13.4 multiply_convert_fusion.6
  963.5 133.9 %all-to-all-done.3 = bf16[3072,3,1,192]{3,1,2,0:T(4,128)(2,1)} async-done(((bf16[3072,3,1,192]{3,1,2,0:T(4,128)(2,1)}), bf16[3072,3,1,192]{3,1,2,0:T(4,128)(2,1)}, u32[]{:S(2)}, u32[]{:S(2)}) %all-to-all-start.3) | async-done | bytes 3538976 | tf_op jit(solution)/shard_map/all_to_all | solution.py:236
  1163.2 78.7 %reduce-scatter.10.cloned.1.call-done = f32[96,3072]{1,0:T(8,128)} async-done(((f32[768,3072]{1,0:T(8,128)}), f32[96,3072]{1,0:T(8,128)}) %reduce-scatter.10.cloned.1.call-update) | async-done | bytes 1179664 | tf_op jit(solution)/shard_map/reduce_scatter | solution.py:277
  1244.1 78.2 %reduce-scatter.12.cloned.1.call-done = f32[384,768]{1,0:T(8,128)} async-done(((f32[3072,768]{1,0:T(8,128)}), f32[384,768]{1,0:T(8,128)}) %reduce-scatter.12.cloned.1.call-update) | async-done | bytes 1179664 | tf_op jit(solution)/shard_map/reduce_scatter | solution.py:279
  1324.4 66.8 %reduce-scatter.6.cloned.1.call-done = f32[96,2304]{1,0:T(8,128)} async-done(((f32[768,2304]{1,0:T(8,128)}), f32[96,2304]{1,0:T(8,128)}) %reduce-scatter.6.cloned.1.call-update) | async-done | bytes 884752 | tf_op jit(solution)/shard_map/reduce_scatter | solution.py:275
  1396.5 25.7 %all-reduce.9 = (bf16[768]{0:T(1024)(128)(2,1)}, bf16[768]{0:T(1024)(128)(2,1)}, bf16[3072]{0:T(1024)(128)(2,1)}, bf16[768]{0:T(1024)(128)(2,1)}, bf16[4608]{0:T(1024)(128)(2,1)}) all-reduce(f32[768]{0:T(1024)} %get-tuple-element.193, f32[768]{0:T(1024)S(1)} %copy-done.58, ...), channel_id=2, replica_groups=mesh['fsdp'=8,'seq'=4] {'fsdp'}, use_global_device_ids=true, to_apply=%region_23.24.clone | all-reduce | flops 9984 | bytes 59904
  1463.1 13.5 all-reduce.15.cloned.1.call-done
  (374 shorter events, 748.0 us)
Async XLA Ops:
  7.2 36.7 %all-gather.7.cloned.1.call-start = ((), (), s32[]{:S(2)}) async-start(), calls=%async_computation.9 | async-start | bytes 1327104 | tf_op jit(solution)/shard_map/all_gather | solution.py:90
  9.0 64.6 %all-gather.9.cloned.1.call-start = ((), (), s32[]{:S(2)}) async-start(), calls=%async_computation.10 | async-start | bytes 3981312 | tf_op jit(solution)/shard_map/all_gather | solution.py:86
  11.2 431.2 %all-gather.11.cloned.1.call-start = ((), (), s32[]{:S(2)}) async-start(), calls=%async_computation.11 | async-start | bytes 1327104 | tf_op jit(solution)/shard_map/all_gather | solution.py:87
  13.0 435.5 %all-gather.13.cloned.1.call-start = ((), (), s32[]{:S(2)}) async-start(), calls=%async_computation.12 | async-start | bytes 5308416 | tf_op jit(solution)/shard_map/all_gather | solution.py:88
  43.4 30.2 %copy-start.47 = (f32[768]{0:T(1024)}, f32[768]{0:T(1024)S(1)}, u32[]{:S(2)}) copy-start(f32[768]{0:T(1024)S(1)} %get-tuple-element.238) | copy-start | bytes 9220
  43.4 30.2 %copy-start.39 = (f32[768]{0:T(1024)}, f32[768]{0:T(1024)S(1)}, u32[]{:S(2)}) copy-start(f32[768]{0:T(1024)S(1)} %broadcast_multiply_fusion.6) | copy-start | bytes 9220
  43.8 29.8 %copy-start.45 = (f32[768]{0:T(1024)}, f32[768]{0:T(1024)S(1)}, u32[]{:S(2)}) copy-start(f32[768]{0:T(1024)S(1)} %add_rsqrt_fusion.1) | copy-start | bytes 9220
  46.2 27.4 %copy-start.41 = (f32[768]{0:T(1024)}, f32[768]{0:T(1024)S(1)}, u32[]{:S(2)}) copy-start(f32[768]{0:T(1024)S(1)} %get-tuple-element.283) | copy-start | bytes 9220
  46.2 27.4 %copy-start.49 = (f32[768]{0:T(1024)}, f32[768]{0:T(1024)S(1)}, u32[]{:S(2)}) copy-start(f32[768]{0:T(1024)S(1)} %get-tuple-element.282) | copy-start | bytes 9220
  86.9 84.1 %all-to-all-start = ((bf16[768,3,4,192]{0,3,1,2:T(8,128)(2,1)}), bf16[768,3,4,192]{0,3,1,2:T(8,128)(2,1)S(1)}, u32[]{:S(2)}, u32[]{:S(2)}) async-start(bf16[768,3,4,192]{0,3,1,2:T(8,128)(2,1)} %copy.68), calls=%async_computation | async-start | bytes 7077888 | tf_op jit(solution)/shard_map/all_to_all | solution.py:119
  91.5 368.9 %all-gather.15.cloned.1.call-start = ((), (), s32[]{:S(2)}) async-start(), calls=%async_computation.13 | async-start | bytes 5308416 | tf_op jit(solution)/shard_map/all_gather | solution.py:89
  393.7 31.6 %all-to-all-start.1 = ((bf16[4,2,73728]{2,1,0:T(2,128)(2,1)}), bf16[4,2,73728]{2,1,0:T(2,128)(2,1)S(1)}, u32[]{:S(2)}, u32[]{:S(2)}) async-start(bf16[4,2,73728]{2,1,0:T(2,128)(2,1)} %reshape.339), calls=%async_computation.1 | async-start | bytes 2359296 | tf_op jit(solution)/shard_map/all_to_all | solution.py:153
  446.7 34.3 %copy-start.26 = (f32[768]{0:T(1024)}, f32[768]{0:T(1024)S(1)}, u32[]{:S(2)}) copy-start(f32[768]{0:T(1024)S(1)} %broadcast_multiply_fusion.5) | copy-start | bytes 9220
  448.5 32.5 %copy-start.32 = (f32[768]{0:T(1024)}, f32[768]{0:T(1024)S(1)}, u32[]{:S(2)}) copy-start(f32[768]{0:T(1024)S(1)} %add_rsqrt_fusion) | copy-start | bytes 9220
  493.2 32.4 %all-to-all-start.2 = ((bf16[768,4,192]{0,2,1:T(8,128)(2,1)}), bf16[768,4,192]{0,2,1:T(8,128)(2,1)}, u32[]{:S(2)}, u32[]{:S(2)}) async-start(bf16[768,4,192]{0,2,1:T(8,128)(2,1)} %bitcast.22), calls=%async_computation.2 | async-start | bytes 2359296 | tf_op jit(solution)/shard_map/all_to_all | solution.py:186
  954.2 143.2 %all-to-all-start.3 = ((bf16[3072,3,1,192]{3,1,2,0:T(4,128)(2,1)}), bf16[3072,3,1,192]{3,1,2,0:T(4,128)(2,1)}, u32[]{:S(2)}, u32[]{:S(2)}) async-start(bf16[3072,3,1,192]{3,1,2,0:T(4,128)(2,1)} %copy.79), calls=%async_computation.3 | async-start | bytes 12582912 | tf_op jit(solution)/shard_map/all_to_all | solution.py:236
  959.7 192.1 %reduce-scatter.8.cloned.1.call-start = ((), (), s32[]{:S(2)}) async-start(), calls=%async_computation.15 | async-start | bytes 2654208 | tf_op jit(solution)/shard_map/reduce_scatter | solution.py:276
  962.3 199.3 %reduce-scatter.14.cloned.1.call-start = ((), (), s32[]{:S(2)}) async-start(), calls=%async_computation.18 | async-start | bytes 2654208 | tf_op jit(solution)/shard_map/reduce_scatter | solution.py:281
  1121.0 120.9 %reduce-scatter.10.cloned.1.call-start = ((), (), s32[]{:S(2)}) async-start(), calls=%async_computation.16 | async-start | bytes 10616832 | tf_op jit(solution)/shard_map/reduce_scatter | solution.py:277
  1132.1 190.2 %reduce-scatter.12.cloned.1.call-start = ((), (), s32[]{:S(2)}) async-start(), calls=%async_computation.17 | async-start | bytes 10616832 | tf_op jit(solution)/shard_map/reduce_scatter | solution.py:279
  1143.4 247.8 %reduce-scatter.6.cloned.1.call-start = ((), (), s32[]{:S(2)}) async-start(), calls=%async_computation.14 | async-start | bytes 7962624 | tf_op jit(solution)/shard_map/reduce_scatter | solution.py:275
  1151.7 324.9 %all-reduce.15.cloned.1.call-start = ((), (), s32[]{:S(2)}) async-start(), calls=%async_computation.19 | async-start | bytes 3833856 | tf_op jit(solution)/shard_map/psum | solution.py:287
  1244.1 152.4 %copy-start.58 = (f32[768]{0:T(1024)S(1)}, f32[768]{0:T(1024)}, u32[]{:S(2)}) copy-start(f32[768]{0:T(1024)} %get-tuple-element.190) | copy-start | bytes 9220
  1244.1 202.4 %copy-start.10 = (bf16[128,4608]{0,1:T(8,128)(2,1)S(1)}, bf16[128,4608]{0,1:T(8,128)(2,1)}, u32[]{:S(2)}) copy-start(bf16[128,4608]{0,1:T(8,128)(2,1)} %all-gather.7.cloned.1.call-done) | copy-start | bytes 3538948
  (71 other events, 408.4 us)
Sparse Core Ops, SparseCore 0:
  10.5 26.7 all-gather.6
  39.7 33.8 all-gather.8
  76.1 23.9 all-gather.10
  102.3 38.7 all-gather.12
  142.9 38.7 all-gather.14
  963.5 42.7 reduce-scatter.7
  1121.1 40.4 reduce-scatter.13
  1165.1 76.8 reduce-scatter.9
  1245.4 76.8 reduce-scatter.11
  1325.6 65.4 reduce-scatter.5
  1395.1 81.4 all-reduce.14
where the time goes:
time: 1500 us; the launch traced here: 1490 us
  waiting for transfers between devices  529 us (35%)
  matrix products  452 us (30%)
  other arithmetic  212 us (14%)
  local copies, waits for them, and re-layouts  177 us (12%)
  blocking collectives  81.7 us (5%)
  starting transfers between devices  18.7 us (1%)
  between operations  18.2 us (1%)
    all_to_all x1, waiting for transfers between devices, per_device(): lax.all_to_all(grad_send, 'seq', split_axis=0, concat_axis=2, tiled=True)  134 us
    convert_element_type x6, other arithmetic, attend_back(): score_low = (softmax_val * (grad_probs - centre)).astype(jnp.bfloat16)  80.6 us
    reduce_scatter x1, waiting for transfers between devices, per_device(): lax.psum_scatter(up_weight_grad, 'fsdp', scatter_dimension=0, tiled=True)  78.7 us
    reduce_scatter x1, waiting for transfers between devices, per_device(): lax.psum_scatter(down_weight_grad, 'fsdp', scatter_dimension=0, tiled=True)  78.2 us
    dot_general x6, matrix products, attend_back(): jnp.einsum('qgd,kgd->gqk', grad_block, values_low, preferred_element_type...  75.6 us
    all_to_all x1, waiting for transfers between devices, per_device(): lax.all_to_all(qkv_tok.reshape(tok_count, 3, seq_count, group_width), 'se...  74.7 us
    dot_general x6, matrix products, attend_back(): jnp.einsum('gqk,qgd->kgd', probs_low, grad_block, preferred_element_type=...  72 us
    reduce_scatter x1, waiting for transfers between devices, per_device(): lax.psum_scatter(qkv_weight_grad, 'fsdp', scatter_dimension=0, tiled=True)  66.8 us
  transfers between devices with their start and end apart: 15, of which 10 were waited for; matrix products, arithmetic and copies ran while one was open for 24% of the time, Pallas kernels for 0%

commit v1 on v0

v1 whole, which is shorter than its diff:
```python
from functools import partial
import math

import jax
import jax.numpy as jnp
from jax import lax
from jax.experimental import pallas as pl
from jax.experimental.pallas import tpu as pltpu
from jax.sharding import PartitionSpec as P

H = 12
HD = 64
EPSILON = 1e-05
BF16 = jnp.bfloat16
F32 = jnp.float32
LOG2E = math.log2(math.e)
VMEM_LIMIT = 60 * 1024 * 1024


def mm(a, b, ca, cb):
    return lax.dot_general(a, b, (((ca,), (cb,)), ((), ())), preferred_element_type=F32)


def normalize(values):
    centre = jnp.mean(values, axis=-1, keepdims=True)
    shifted = values - centre
    variance = jnp.mean(shifted * shifted, axis=-1, keepdims=True)
    inv_std = lax.rsqrt(variance + EPSILON)
    return (shifted * inv_std, inv_std)


def norm_back(grad_hat, normed_hat, inv_std):
    mean_grad = jnp.mean(grad_hat, axis=-1, keepdims=True)
    mean_mixed = jnp.mean(grad_hat * normed_hat, axis=-1, keepdims=True)
    return inv_std * (grad_hat - mean_grad - normed_hat * mean_mixed)


def project_kernel(seq_count, w_ref, x_ref, cos_ref, sin_ref, out_ref):
    rows = mm(w_ref[...], x_ref[...], 0, 1).astype(BF16)
    cosine, sine = cos_ref[...], sin_ref[...]
    half = HD // 2
    for z in range(seq_count):
        for part in range(3):
            base = (z * 3 + part) * HD
            if part == 2:
                out_ref[z, part * HD : (part + 1) * HD, :] = rows[base : base + HD]
            else:
                a = rows[base : base + half].astype(F32)
                b = rows[base + half : base + HD].astype(F32)
                out_ref[z, part * HD : part * HD + half, :] = (a * cosine - b * sine).astype(BF16)
                out_ref[z, part * HD + half : (part + 1) * HD, :] = (b * cosine + a * sine).astype(BF16)


def project(weight, attn_in, cosine, sine, seq_count):
    tok = attn_in.shape[0]
    return pl.pallas_call(
        partial(project_kernel, seq_count),
        out_shape=jax.ShapeDtypeStruct((seq_count, 3 * HD, tok), BF16),
        compiler_params=pltpu.CompilerParams(vmem_limit_bytes=VMEM_LIMIT),
        cost_estimate=pl.CostEstimate(
            flops=2 * tok * weight.size, bytes_accessed=2 * weight.size * 3, transcendentals=0
        ),
        name="project",
    )(weight, attn_in, cosine, sine)


def attend_kernel(n, tok, sub, x_ref, o_ref, lse_ref, k_ref):
    step = pl.program_id(0)

    @pl.when(step == 0)
    def _():
        for c in range(n):
            k_ref[c * tok : (c + 1) * tok, :] = x_ref[c, HD : 2 * HD, :].T

    scale = LOG2E / math.sqrt(HD)
    width = tok // sub

    def score(i):
        q = x_ref[step, 0:HD, i * width : (i + 1) * width]
        return mm(k_ref[...], q, 1, 0)

    def soft(s):
        top = jnp.max(s, axis=0, keepdims=True) * scale
        p = jnp.exp2(s * scale - top)
        total = jnp.sum(p, axis=0, keepdims=True)
        return top, total, p.astype(BF16)

    def mix(i, top, total, p):
        o = None
        for c in range(n):
            part = mm(x_ref[c, 2 * HD : 3 * HD, :], p[c * tok : (c + 1) * tok], 1, 0)
            o = part if o is None else o + part
        o_ref[0, :, i * width : (i + 1) * width] = (o / total).astype(BF16)
        lse_ref[0, :, i * width : (i + 1) * width] = top + jnp.log2(total)

    scores = [score(0)]
    pending = None
    for i in range(sub):
        if i + 1 < sub:
            scores.append(score(i + 1))
        done = soft(scores[i])
        if pending is not None:
            mix(i - 1, *pending)
        pending = done
    mix(sub - 1, *pending)


def attend(x):
    n, _, tok = x.shape
    length = n * tok
    return pl.pallas_call(
        partial(attend_kernel, n, tok, 2),
        grid=(n,),
        in_specs=[pl.BlockSpec(x.shape, lambda i: (0, 0, 0))],
        out_specs=[
            pl.BlockSpec((1, HD, tok), lambda i: (i, 0, 0)),
            pl.BlockSpec((1, 1, tok), lambda i: (i, 0, 0)),
        ],
        out_shape=[
            jax.ShapeDtypeStruct((n, HD, tok), BF16),
            jax.ShapeDtypeStruct((n, 1, tok), F32),
        ],
        scratch_shapes=[pltpu.VMEM((length, HD), BF16)],
        compiler_params=pltpu.CompilerParams(vmem_limit_bytes=VMEM_LIMIT),
        cost_estimate=pl.CostEstimate(
            flops=16 * length * length * HD, bytes_accessed=8 * length * HD, transcendentals=length * length
        ),
        name="attend",
    )(x)


def attend_back_kernel(
    n, tok, sub, x_ref, g_ref, o_ref, lse_ref, cos_ref, sin_ref, out_ref, k_ref, v_ref, dk_ref, dv_ref
):
    step = pl.program_id(0)
    half = HD // 2

    @pl.when(step == 0)
    def _():
        for c in range(n):
            k_ref[c * tok : (c + 1) * tok, :] = x_ref[c, HD : 2 * HD, :].T
            v_ref[c * tok : (c + 1) * tok, :] = x_ref[c, 2 * HD : 3 * HD, :].T
        dk_ref[...] = jnp.zeros_like(dk_ref)
        dv_ref[...] = jnp.zeros_like(dv_ref)

    scale = LOG2E / math.sqrt(HD)
    width = tok // sub

    def turn_back(grad, cosine, sine):
        a, b = grad[:half], grad[half:]
        return (a * cosine + b * sine).astype(BF16), (b * cosine - a * sine).astype(BF16)

    for i in range(sub):
        cols = slice(i * width, (i + 1) * width)
        q = x_ref[step, 0:HD, cols]
        g = g_ref[step, :, cols]
        o = o_ref[step, :, cols]
        centre = jnp.sum(g.astype(F32) * o.astype(F32), axis=0, keepdims=True)
        s = mm(k_ref[...], q, 1, 0)
        dp = mm(v_ref[...], g, 1, 0)
        p = jnp.exp2(s * scale - lse_ref[step, :, cols])
        p_low = p.astype(BF16)
        ds = (p * (dp - centre)).astype(BF16)
        dv_ref[...] += mm(g, p_low, 1, 1)
        dk_ref[...] += mm(q, ds, 1, 1)
        dq = None
        for c in range(n):
            part = mm(x_ref[c, HD : 2 * HD, :], ds[c * tok : (c + 1) * tok], 1, 0)
            dq = part if dq is None else dq + part
        dq = dq * (1.0 / math.sqrt(HD))
        a, b = turn_back(dq, cos_ref[step, :, cols], sin_ref[step, :, cols])
        out_ref[step, 0:half, cols] = a
        out_ref[step, half:HD, cols] = b

    @pl.when(step == n - 1)
    def _():
        for c in range(n):
            dk = dk_ref[:, c * tok : (c + 1) * tok] * (1.0 / math.sqrt(HD))
            a, b = turn_back(dk, cos_ref[c], sin_ref[c])
            out_ref[c, HD : HD + half, :] = a
            out_ref[c, HD + half : 2 * HD, :] = b
            out_ref[c, 2 * HD : 3 * HD, :] = dv_ref[:, c * tok : (c + 1) * tok].astype(BF16)


def attend_back(x, g, o, lse, cosine, sine):
    n, _, tok = x.shape
    length = n * tok
    whole = lambda a: pl.BlockSpec(a.shape, lambda i: (0,) * a.ndim)
    return pl.pallas_call(
        partial(attend_back_kernel, n, tok, 2),
        grid=(n,),
        in_specs=[whole(a) for a in (x, g, o, lse, cosine, sine)],
        out_specs=whole(x),
        out_shape=jax.ShapeDtypeStruct(x.shape, BF16),
        scratch_shapes=[
            pltpu.VMEM((length, HD), BF16),
            pltpu.VMEM((length, HD), BF16),
            pltpu.VMEM((HD, length), F32),
            pltpu.VMEM((HD, length), F32),
        ],
        compiler_params=pltpu.CompilerParams(vmem_limit_bytes=VMEM_LIMIT),
        cost_estimate=pl.CostEstimate(
            flops=40 * length * length * HD, bytes_accessed=16 * length * HD, transcendentals=length * length
        ),
        name="attend_back",
    )(x, g, o, lse, cosine, sine)


def per_device(
    inputs,
    conditioning,
    cotangent,
    attn_gain,
    mlp_gain,
    qkv_weight,
    out_weight,
    up_weight,
    up_bias,
    down_weight,
    down_bias,
    mod_weight,
    mod_bias,
):
    n = lax.axis_size("seq")
    fs = lax.axis_size("fsdp")
    z = lax.axis_index("seq")
    me = lax.axis_index("fsdp")
    tokens = inputs[0]
    tok, width = tokens.shape
    slots = H // n
    gather = lambda a: lax.all_gather(a, "fsdp", axis=0, tiled=True)

    smalls = [attn_gain, mlp_gain, up_bias, down_bias, conditioning[0]]
    sizes = [a.shape[0] for a in smalls]
    packed = lax.all_gather(jnp.concatenate(smalls), "fsdp", axis=0)
    offsets = [sum(sizes[:i]) for i in range(len(sizes))]
    attn_gain_full, mlp_gain_full, up_bias_full, down_bias_full = (
        packed[:, o : o + s].reshape(-1) for o, s in zip(offsets[:4], sizes[:4])
    )
    cond_all = packed[:, offsets[4] :]
    cond_act_all = jax.nn.silu(cond_all)
    cond_low_all = cond_act_all.astype(BF16)
    mod_low = mod_weight.astype(BF16)
    mod_own = mm(cond_low_all, mod_low, 1, 0) + mod_bias[None, :]
    modulation = lax.all_to_all(mod_own, "fsdp", split_axis=0, concat_axis=0, tiled=True).reshape(-1)
    shift_attn, scale_attn, gate_attn, shift_mlp, scale_mlp, gate_mlp = jnp.split(modulation, 6)

    shard = qkv_weight.shape[0]
    qkv_low = qkv_weight.astype(BF16).reshape(shard, 3, n, slots, HD)
    qkv_slots = [
        gather(qkv_low[:, :, :, s].transpose(0, 2, 1, 3).reshape(shard, n * 3 * HD)) for s in range(slots)
    ]
    out_full = gather(out_weight.astype(BF16))
    up_full = gather(up_weight.astype(BF16))
    down_full = gather(down_weight.astype(BF16))

    inv_freq = jnp.exp(-math.log(10000.0) * jnp.arange(HD // 2, dtype=F32) * (2.0 / HD))
    angles = inv_freq[:, None] * jnp.arange(tok * n, dtype=F32)[None, :]
    cos_all = jnp.cos(angles).reshape(HD // 2, n, tok).transpose(1, 0, 2)
    sin_all = jnp.sin(angles).reshape(HD // 2, n, tok).transpose(1, 0, 2)
    cos_own = lax.dynamic_index_in_dim(cos_all, z, 0, keepdims=False)
    sin_own = lax.dynamic_index_in_dim(sin_all, z, 0, keepdims=False)

    hat_attn, inv_attn = normalize(tokens)
    normed_attn = hat_attn * attn_gain_full
    attn_in = (normed_attn * (1.0 + scale_attn) + shift_attn).astype(BF16)
    swap = lambda a: lax.all_to_all(a, "seq", split_axis=0, concat_axis=0, tiled=True)
    heads = [swap(project(w, attn_in, cos_own, sin_own, n)) for w in qkv_slots]
    mixed_heads, log_totals, mixed_back = [], [], []
    for x in heads:
        o, lse = attend(x)
        mixed_heads.append(o)
        log_totals.append(lse)
        mixed_back.append(swap(o))
    mixed = jnp.stack(mixed_back, axis=1).reshape(width, tok)

    attn_out = mm(mixed, out_full, 0, 0)
    hidden = tokens + gate_attn * attn_out
    hat_mlp, inv_mlp = normalize(hidden)
    normed_mlp = hat_mlp * mlp_gain_full
    mlp_in = (normed_mlp * (1.0 + scale_mlp) + shift_mlp).astype(BF16)
    pre_act = jnp.dot(mlp_in, up_full, preferred_element_type=F32) + up_bias_full
    gelu_act, gelu_pull = jax.vjp(partial(jax.nn.gelu, approximate=True), pre_act)
    up_act = gelu_act.astype(BF16)
    branch = jnp.dot(up_act, down_full, preferred_element_type=F32) + down_bias_full
    output = hidden + gate_mlp * branch
    grad_out = cotangent[0]
    grad_branch = gate_mlp * grad_out
    branch_low = grad_branch.astype(BF16)
    down_weight_grad = mm(up_act, branch_low, 0, 0)
    grad_act = mm(branch_low, down_full, 1, 1)
    grad_pre = gelu_pull(grad_act)[0]
    pre_low = grad_pre.astype(BF16)
    up_weight_grad = mm(mlp_in, pre_low, 0, 0)
    grad_mlp_in = mm(pre_low, up_full, 1, 1)
    grad_normed_mlp = grad_mlp_in * (1.0 + scale_mlp)
    grad_hidden = grad_out + norm_back(grad_normed_mlp * mlp_gain_full, hat_mlp, inv_mlp)
    attn_low = (gate_attn * grad_hidden).astype(BF16)
    out_weight_grad = mm(mixed, attn_low, 1, 0)
    grad_mixed = mm(out_full, attn_low, 1, 1).astype(BF16)
    grad_split = grad_mixed.reshape(n, slots, HD, tok)

    grad_slots = []
    for s in range(slots):
        g = swap(grad_split[:, s])
        grad_slots.append(swap(attend_back(heads[s], g, mixed_heads[s], log_totals[s], cos_all, sin_all)))

    scatter = lambda a: lax.psum_scatter(a.astype(BF16), "fsdp", scatter_dimension=0, tiled=True)
    qkv_parts = []
    grad_attn_in = None
    for s in range(slots):
        rows = grad_slots[s].reshape(n * 3 * HD, tok)
        qkv_parts.append(scatter(mm(attn_in, rows, 0, 1)))
        part = mm(rows, qkv_slots[s], 0, 1)
        grad_attn_in = part if grad_attn_in is None else grad_attn_in + part
    grad_normed_attn = grad_attn_in * (1.0 + scale_attn)
    inputs_grad = grad_hidden + norm_back(grad_normed_attn * attn_gain_full, hat_attn, inv_attn)

    part_down = scatter(down_weight_grad)
    part_up = scatter(up_weight_grad)
    part_out = scatter(out_weight_grad)
    vectors = jnp.concatenate(
        [
            jnp.sum(grad_attn_in, axis=0),
            jnp.sum(grad_attn_in * normed_attn, axis=0),
            jnp.sum(grad_hidden * attn_out, axis=0),
            jnp.sum(grad_mlp_in, axis=0),
            jnp.sum(grad_mlp_in * normed_mlp, axis=0),
            jnp.sum(grad_out * branch, axis=0),
            jnp.sum(grad_normed_attn * hat_attn, axis=0),
            jnp.sum(grad_normed_mlp * hat_mlp, axis=0),
            jnp.sum(grad_pre, axis=0),
            jnp.sum(grad_branch, axis=0),
        ]
    )
    summed = lax.all_gather(lax.psum(vectors, "seq"), "fsdp", axis=0)
    ff = up_bias.shape[0] * fs
    total = jnp.sum(summed, axis=0)
    own = lambda v: lax.dynamic_index_in_dim(v.reshape(fs, -1), me, 0, keepdims=False)
    mods = 6 * width
    attn_gain_grad = own(total[mods : mods + width])
    mlp_gain_grad = own(total[mods + width : mods + 2 * width])
    up_bias_grad = own(total[mods + 2 * width : mods + 2 * width + ff])
    down_bias_grad = own(total[mods + 2 * width + ff :])
    mod_bias_grad = own(total[:mods])
    own_mod = lax.dynamic_slice_in_dim(summed[:, :mods], me * (mods // fs), mods // fs, axis=1)
    mod_weight_grad = lax.dot_general(
        cond_low_all.astype(F32), own_mod, (((0,), (0,)), ((), ())), precision=lax.Precision.HIGHEST
    )
    cond_part = lax.dot_general(
        own_mod, mod_low.astype(F32), (((1,), (1,)), ((), ())), precision=lax.Precision.HIGHEST
    )
    grad_cond_act = lax.psum_scatter(cond_part, "fsdp", scatter_dimension=0, tiled=True)
    _, silu_pull = jax.vjp(jax.nn.silu, conditioning)
    conditioning_grad = silu_pull(grad_cond_act)[0]

    qkv_sum = lax.psum(jnp.stack(qkv_parts, axis=0), "seq").astype(F32)
    qkv_weight_grad = (
        qkv_sum.reshape(slots, shard, n, 3, HD).transpose(1, 3, 2, 0, 4).reshape(shard, 3 * width)
    )
    out_sum = lax.psum(part_out, "seq").astype(F32)
    up_sum = lax.psum(part_up, "seq").astype(F32)
    down_sum = lax.psum(part_down, "seq").astype(F32)
    return (
        output[None],
        inputs_grad[None],
        conditioning_grad,
        attn_gain_grad,
        mlp_gain_grad,
        qkv_weight_grad,
        out_sum,
        up_sum,
        up_bias_grad,
        down_sum,
        down_bias_grad,
        mod_weight_grad,
        mod_bias_grad,
    )


def solution(mesh):
    specs = (
        P("fsdp", "seq", None),
        P("fsdp", None),
        P("fsdp", "seq", None),
        P("fsdp"),
        P("fsdp"),
        P("fsdp", None),
        P("fsdp", None),
        P("fsdp", None),
        P("fsdp"),
        P("fsdp", None),
        P("fsdp"),
        P(None, "fsdp"),
        P("fsdp"),
    )
    out_specs = (specs[0], specs[0], specs[1]) + specs[3:]
    return jax.shard_map(per_device, mesh=mesh, in_specs=specs, out_specs=out_specs, check_vma=False)
```

time: 1500 us -> 765 us (0.51)
  matrix products: 452 us -> 95.4 us
  waiting for transfers between devices: 529 us -> 320 us
  other arithmetic: 212 us -> 24.5 us
  local copies, waits for them, and re-layouts: 177 us -> 29.3 us
  Pallas kernels: 0 us -> 147 us
  starting transfers between devices: 18.7 us -> 59.4 us
  blocking collectives: 81.7 us -> 64.6 us
    dot_general x56 -> x18, matrix products: 452 us -> 95.4 us  [the longest x14 70.8 us: mm(): lax.dot_general(a, b, (((ca,), (cb,)), ((), ())), preferred_element_type=...]
    pallas_call x0 -> x9, Pallas kernels: none -> 147 us  [the longest x3 85.3 us: attend_back(): pl.pallas_call(partial(attend_back_kernel, n, tok, 2), grid=(n,), in_spec...]
    all_to_all x4 -> x13, waiting for transfers between devices: 256 us -> 118 us  [the longest x12 115 us: per_device(): lax.all_to_all(a, 'seq', split_axis=0, concat_axis=0, tiled=True)]
    convert_element_type x28 -> x8, other arithmetic: 130 us -> 12.1 us  [the longest x2 3.75 us: per_device(): attn_in = (normed_attn * (1.0 + scale_attn) + shift_attn).astype(BF16)]
    reduce_scatter x5 -> x6, waiting for transfers between devices: 232 us -> 141 us  [per_device(): lax.psum_scatter(a.astype(BF16), 'fsdp', scatter_dimension=0, tiled=True)]
    dynamic_update_slice x12 -> x0, local copies, waits for them, and re-layouts: 60.5 us -> none  [per_device(): mixed_heads, log_totals = lax.map(attend, query_blocks)]
    reduce_sum x6 -> x1, other arithmetic: 57.3 us -> 0.88 us  [per_device(): total = jnp.sum(summed, axis=0)]
    psum x1, waiting for transfers between devices: 13.5 us -> 61.4 us  [per_device(): qkv_sum = lax.psum(jnp.stack(qkv_parts, axis=0), 'seq').astype(F32)]
  transfers between devices with their start and end apart: 15 -> 26, of which waited for: 10 -> 12; matrix products, arithmetic and copies ran while one was open for 24% -> 13% of each run, Pallas kernels for 0% -> 19%
where the time goes in v1:
time: 765 us; the launch traced here: 755 us
  waiting for transfers between devices  320 us (42%)
  Pallas kernels  147 us (19%)
  matrix products  95.4 us (12%)
  blocking collectives  64.6 us (8%)
  starting transfers between devices  59.4 us (8%)
  local copies, waits for them, and re-layouts  29.3 us (4%)
  other arithmetic  24.5 us (3%)
  between operations  15.7 us (2%)
    reduce_scatter x6, waiting for transfers between devices, per_device(): lax.psum_scatter(a.astype(BF16), 'fsdp', scatter_dimension=0, tiled=True)  141 us
    all_to_all x12, waiting for transfers between devices, per_device(): lax.all_to_all(a, 'seq', split_axis=0, concat_axis=0, tiled=True)  115 us
    pallas_call x3, Pallas kernels, attend_back(): pl.pallas_call(partial(attend_back_kernel, n, tok, 2), grid=(n,), in_spec...  85.3 us
    dot_general x14, matrix products, mm(): lax.dot_general(a, b, (((ca,), (cb,)), ((), ())), preferred_element_type=...  70.8 us
    psum x1, waiting for transfers between devices, per_device(): qkv_sum = lax.psum(jnp.stack(qkv_parts, axis=0), 'seq').astype(F32)  61.4 us
    all_to_all x12, starting transfers between devices, per_device(): lax.all_to_all(a, 'seq', split_axis=0, concat_axis=0, tiled=True)  55.2 us
    pallas_call x3, Pallas kernels, attend(): pl.pallas_call(partial(attend_kernel, n, tok, 2), grid=(n,), in_specs=[pl...  49.7 us
    unnamed x2, blocking collectives  38.3 us
  transfers between devices with their start and end apart: 26, of which 12 were waited for; matrix products, arithmetic and copies ran while one was open for 13% of the time, Pallas kernels for 19%

profile of v1, /device:TPU:0, one launch (start us, length us, event | category | flops | bytes accessed | tf_op | source)
XLA Modules:
  0.0 755.2 jit_solution(332266203091122483)
XLA Ops:
  19.8 25.8 %all-reduce = f32[6400]{0:T(1024)S(1)} all-reduce(f32[6400]{0:T(1024)S(1)} %dynamic-update-slice), channel_id=2, replica_groups=mesh['fsdp'=8,'seq'=4] {'fsdp'}, use_global_device_ids=true, to_apply=%add | all-reduce | flops 6400 | bytes 51200
  70.5 24.7 %all-to-all-done.5.x_ref = bf16[4,192,768]{2,1,0:T(8,128)(2,1)} async-done(((bf16[4,192,768]{2,1,0:T(8,128)(2,1)}), bf16[4,192,768]{2,1,0:T(8,128)(2,1)}, u32[]{:S(2)}, u32[]{:S(2)}) %all-to-all-start.5) | async-done | bytes 1179680 | tf_op jit(solution)/shard_map/all_to_all | solution.py:267
  104.3 23.4 %all-to-all-done.3.x_ref = bf16[4,192,768]{2,1,0:T(8,128)(2,1)} async-done(((bf16[4,192,768]{2,1,0:T(8,128)(2,1)}), bf16[4,192,768]{2,1,0:T(8,128)(2,1)}, u32[]{:S(2)}, u32[]{:S(2)}) %all-to-all-start.3) | async-done | bytes 1179680 | tf_op jit(solution)/shard_map/all_to_all | solution.py:267
  131.2 16.6 %attend.5 = (bf16[4,64,768]{2,1,0:T(8,128)(2,1)}, f32[4,1,768]{2,1,0:T(1,128)}) custom-call(bf16[4,192,768]{2,1,0:T(8,128)(2,1)} %all-to-all-done.5.x_ref), custom_call_target="tpu_custom_call" | custom-call | flops 9663676416 | bytes 1572864 | tf_op jit(solution)/shard_map/attend/pallas_call | solution.py:111
  147.8 11.5 %all-to-all-done.1.x_ref = bf16[4,192,768]{2,1,0:T(8,128)(2,1)S(1)} async-done(((bf16[4,192,768]{2,1,0:T(8,128)(2,1)}), bf16[4,192,768]{2,1,0:T(8,128)(2,1)S(1)}, u32[]{:S(2)}, u32[]{:S(2)}) %all-to-all-start.1) | async-done | bytes 1179680 | tf_op jit(solution)/shard_map/all_to_all | solution.py:267
  163.9 16.6 %attend.4 = (bf16[4,64,768]{2,1,0:T(8,128)(2,1)}, f32[4,1,768]{2,1,0:T(1,128)}) custom-call(bf16[4,192,768]{2,1,0:T(8,128)(2,1)} %all-to-all-done.3.x_ref), custom_call_target="tpu_custom_call" | custom-call | flops 9663676416 | bytes 1572864 | tf_op jit(solution)/shard_map/attend/pallas_call | solution.py:111
  185.6 16.6 %attend.3 = (bf16[4,64,768]{2,1,0:T(8,128)(2,1)}, f32[4,1,768]{2,1,0:T(1,128)}) custom-call(bf16[4,192,768]{2,1,0:T(8,128)(2,1)} %copy-done.10), custom_call_target="tpu_custom_call" | custom-call | flops 9663676416 | bytes 1572864 | tf_op jit(solution)/shard_map/attend/pallas_call | solution.py:111
  224.4 11.8 %multiply_convert_fusion = (bf16[768,3072]{1,0:T(8,128)(2,1)}, f32[768,3072]{1,0:T(8,128)}) fusion(f32[3072]{0:T(1024)} %add.168, bf16[768,3072]{1,0:T(8,128)(2,1)} %all-gather.17.cloned.1.call-done, f32[768,768]{1,0:T(8,128)} %copy-done.1, f32[768]{0:T(1024)} %get-tuple-element.89, f32[768]{0:T(1024)} %get-tuple-element.90, f32[768]{0:T(1024)} %mul.392, ...), kind=kOutput, calls=%fused_computation.8 | convolution fusion | flops 3651010560 | bytes 21261312 | tf_op jit(solution)/shard_map/dot_general | solution.py:282
  236.3 14.1 %fusion.42 = (f32[3072]{0:T(1024)}, bf16[768,3072]{1,0:T(8,128)(2,1)S(1)}) fusion(f32[768,3072]{1,0:T(8,128)} %get-tuple-element.100, f32[3072]{0:T(1024)} %add.168, bf16[3072,768]{1,0:T(8,128)(2,1)} %all-gather.19.cloned.1.call-done, f32[1,768,768]{2,1,0:T(8,128)} %param.15, f32[768]{0:T(1024)} %get-tuple-element.88), kind=kOutput, calls=%fused_computation.117 | convolution fusion | flops 3676959744 | bytes 21261312 | tf_op jit(solution)/shard_map/dot_general | solution.py:21
  256.9 10.0 %fusion.11 = (f32[768]{0:T(1024)}, f32[768]{0:T(1024)}, f32[1,768,768]{2,1,0:T(8,128)}, f32[768]{0:T(1024)}, f32[768,768]{1,0:T(8,128)S(1)}) fusion(f32[1,768,768]{2,1,0:T(8,128)S(1)} %copy-done.54, f32[768]{0:T(1024)S(1)} %copy-done.33, f32[768]{0:T(1024)S(1)} %copy-done.46, f32[768,768]{1,0:T(8,128)S(1)} %copy-done.2, f32[768,768]{1,0:T(8,128)S(1)} %copy-done.4, ...), kind=kOutput, calls=%fused_computation.37 | convolution fusion | flops 3634493184 | bytes 23626752 | tf_op jit(solution)/shard_map/dot_general | solution.py:285
  287.1 28.3 %attend_back.5 = bf16[4,192,768]{2,1,0:T(8,128)(2,1)} custom-call(bf16[4,192,768]{2,1,0:T(8,128)(2,1)} %all-to-all-done.5.x_ref, bf16[4,64,768]{2,1,0:T(8,128)(2,1)} %all-to-all-done.11.g_ref, bf16[4,64,768]{2,1,0:T(8,128)(2,1)} %get-tuple-element.21.o_ref, f32[4,1,768]{2,1,0:T(1,128)} %get-tuple-element.24.lse_ref, ...), custom_call_target="tpu_custom_call" | custom-call | flops 24159191040 | bytes 3145728 | tf_op jit(solution)/shard_map/attend_back/pallas_call | solution.py:189
  322.7 22.7 %all-to-all-done.12 = bf16[4,192,768]{2,1,0:T(8,128)(2,1)} async-done(((bf16[4,192,768]{2,1,0:T(8,128)(2,1)}), bf16[4,192,768]{2,1,0:T(8,128)(2,1)}, u32[]{:S(2)}, u32[]{:S(2)}) %all-to-all-start.12) | async-done | bytes 1179680 | tf_op jit(solution)/shard_map/all_to_all | solution.py:267
  349.6 28.6 %attend_back.4 = bf16[4,192,768]{2,1,0:T(8,128)(2,1)} custom-call(bf16[4,192,768]{2,1,0:T(8,128)(2,1)} %all-to-all-done.3.x_ref, bf16[4,64,768]{2,1,0:T(8,128)(2,1)} %all-to-all-done.9.g_ref, bf16[4,64,768]{2,1,0:T(8,128)(2,1)} %get-tuple-element.20.o_ref, f32[4,1,768]{2,1,0:T(1,128)} %get-tuple-element.23.lse_ref, f32[4,32,768]{2,1,0:T(8,128)} %get-tuple-element.95.cos_ref, ...), custom_call_target="tpu_custom_call" | custom-call | flops 24159191040 | bytes 3145728 | tf_op jit(solution)/shard_map/attend_back/pallas_call | solution.py:189
  387.5 28.4 %attend_back.3 = bf16[4,192,768]{2,1,0:T(8,128)(2,1)} custom-call(bf16[4,192,768]{2,1,0:T(8,128)(2,1)} %copy-done.10, bf16[4,64,768]{2,1,0:T(8,128)(2,1)} %all-to-all-done.7.g_ref, bf16[4,64,768]{2,1,0:T(8,128)(2,1)} %get-tuple-element.19.o_ref, f32[4,1,768]{2,1,0:T(1,128)} %get-tuple-element.22.lse_ref, f32[4,32,768]{2,1,0:T(8,128)} %get-tuple-element.95.cos_ref, ...), custom_call_target="tpu_custom_call" | custom-call | flops 24159191040 | bytes 3145728 | tf_op jit(solution)/shard_map/attend_back/pallas_call | solution.py:189
  424.9 22.2 %all-to-all-done.8 = bf16[4,192,768]{2,1,0:T(8,128)(2,1)} async-done(((bf16[4,192,768]{2,1,0:T(8,128)(2,1)}), bf16[4,192,768]{2,1,0:T(8,128)(2,1)}, u32[]{:S(2)}, u32[]{:S(2)}) %all-to-all-start.8) | async-done | bytes 1179680 | tf_op jit(solution)/shard_map/all_to_all | solution.py:267
  455.0 9.4 %convolution_convert_fusion.1 = bf16[768,3072]{1,0:T(8,128)(2,1)} fusion(bf16[768,3072]{1,0:T(8,128)(2,1)} %copy-done.55, f32[768,768]{1,0:T(8,128)} %copy-done.1, f32[768]{0:T(1024)} %get-tuple-element.89, f32[768]{0:T(1024)} %get-tuple-element.90, f32[768]{0:T(1024)} %mul.392, f32[768]{0:T(1024)} %add_rsqrt_fusion, f32[768]{0:T(1024)} %copy-done.28), kind=kOutput, calls=%fused_computation.10 | convolution fusion | flops 3629776896 | bytes 11811840 | tf_op jit(solution)/shard_map/dot_general | solution.py:21
  465.1 9.2 %convolution_convert_fusion = bf16[3072,768]{1,0:T(8,128)(2,1)} fusion(bf16[768,3072]{1,0:T(8,128)(2,1)} %get-tuple-element.99, f32[1,768,768]{2,1,0:T(8,128)} %param.15, f32[768]{0:T(1024)S(1)} %copy-done.34), kind=kOutput, calls=%fused_computation.9 | convolution fusion | flops 3627417600 | bytes 11799552 | tf_op jit(solution)/shard_map/dot_general | solution.py:21
  486.4 17.6 %psum.35 = f32[1,9984]{1,0:T(1,128)S(1)} all-reduce(f32[1,9984]{1,0:T(1,128)S(1)} %all_gather.38), channel_id=1, replica_groups=mesh['fsdp'=8,'seq'=4] {'seq'}, use_global_device_ids=true, to_apply=%region_18.19 | all-reduce | flops 9984 | bytes 79872 | tf_op jit(solution)/shard_map/psum | solution.py:336
  504.0 8.7 %all-gather.1 = f32[8,1,9984]{2,1,0:T(1,128)S(1)} all-gather(f32[1,1,9984]{2,1,0:T(1,128)S(1)} %bitcast.142), channel_id=1, replica_groups=mesh['fsdp'=8,'seq'=4] {'fsdp'}, dimensions={0}, use_global_device_ids=true | all-gather | bytes 359424 | tf_op jit(solution)/shard_map/all_gather | solution.py:336
  516.9 26.2 %reduce-scatter.13.cloned.1.call-done = bf16[96,768]{1,0:T(8,128)(2,1)} async-done(((bf16[768,768]{1,0:T(8,128)(2,1)}), bf16[96,768]{1,0:T(8,128)(2,1)}) %reduce-scatter.13.cloned.1.call-update) | async-done | bytes 147472 | tf_op jit(solution)/shard_map/reduce_scatter | solution.py:308
  543.0 57.3 %reduce-scatter.15.cloned.1.call-done = bf16[96,3072]{1,0:T(8,128)(2,1)} async-done(((bf16[768,3072]{1,0:T(8,128)(2,1)}), bf16[96,3072]{1,0:T(8,128)(2,1)}) %reduce-scatter.15.cloned.1.call-update) | async-done | bytes 589840 | tf_op jit(solution)/shard_map/reduce_scatter | solution.py:308
  600.3 57.1 %reduce-scatter.17.cloned.1.call-done = bf16[384,768]{1,0:T(8,128)(2,1)} async-done(((bf16[3072,768]{1,0:T(8,128)(2,1)}), bf16[384,768]{1,0:T(8,128)(2,1)}) %reduce-scatter.17.cloned.1.call-update) | async-done | bytes 589840 | tf_op jit(solution)/shard_map/reduce_scatter | solution.py:308
  659.0 12.5 %all-reduce.1 = f32[8,128]{1,0:T(8,128)S(1)} all-reduce(f32[8,128]{1,0:T(8,128)S(1)} %copy-done.30), channel_id=3, replica_groups=mesh['fsdp'=8,'seq'=4] {'fsdp'}, use_global_device_ids=true, to_apply=%region_19.20.clone | all-reduce | flops 1024 | bytes 8192
  679.9 61.4 %all-reduce.5.cloned.1.call-done = (bf16[96,2304]{0,1:T(8,128)(2,1)}, bf16[96,768]{1,0:T(8,128)(2,1)}, bf16[96,3072]{1,0:T(8,128)(2,1)}, bf16[384,768]{1,0:T(8,128)(2,1)}) async-done(((bf16[96,2304]{0,1:T(8,128)(2,1)}, bf16[96,768]{1,0:T(8,128)(2,1)}, bf16[96,3072]{1,0:T(8,128)(2,1)}, bf16[384,768]{1,0:T(8,128)(2,1)}), (bf16[96,2304]{0,1:T(8,128)(2,1)}, bf16[96,768]{1,0:T(8,128)(2,1)}, ...) | async-done | bytes 1769488 | tf_op jit(solution)/shard_map/psum | solution.py:357
  (269 shorter events, 179.1 us)
Async XLA Ops:
  7.2 50.7 %all-gather.13.cloned.1.call-start = ((), (), s32[]{:S(2)}) async-start(), calls=%async_computation.21 | async-start | bytes 1327104 | tf_op jit(solution)/shard_map/all_gather | solution.py:231
  10.3 56.4 %all-gather.11.cloned.1.call-start = ((), (), s32[]{:S(2)}) async-start(), calls=%async_computation.20 | async-start | bytes 1327104 | tf_op jit(solution)/shard_map/all_gather | solution.py:231
  11.2 89.2 %all-gather.9.cloned.1.call-start = ((), (), s32[]{:S(2)}) async-start(), calls=%async_computation.19 | async-start | bytes 1327104 | tf_op jit(solution)/shard_map/all_gather | solution.py:231
  14.8 203.2 %all-gather.15.cloned.1.call-start = ((), (), s32[]{:S(2)}) async-start(), calls=%async_computation.22 | async-start | bytes 1327104 | tf_op jit(solution)/shard_map/all_gather | solution.py:231
  16.5 207.9 %all-gather.17.cloned.1.call-start = ((), (), s32[]{:S(2)}) async-start(), calls=%async_computation.23 | async-start | bytes 5308416 | tf_op jit(solution)/shard_map/all_gather | solution.py:231
  61.7 33.5 %all-to-all-start.5 = ((bf16[4,192,768]{2,1,0:T(8,128)(2,1)}), bf16[4,192,768]{2,1,0:T(8,128)(2,1)}, u32[]{:S(2)}, u32[]{:S(2)}) async-start(bf16[4,192,768]{2,1,0:T(8,128)(2,1)} %project.5), calls=%async_computation.5 | async-start | bytes 2359296 | tf_op jit(solution)/shard_map/all_to_all | solution.py:267
  95.2 32.4 %all-to-all-start.3 = ((bf16[4,192,768]{2,1,0:T(8,128)(2,1)}), bf16[4,192,768]{2,1,0:T(8,128)(2,1)}, u32[]{:S(2)}, u32[]{:S(2)}) async-start(bf16[4,192,768]{2,1,0:T(8,128)(2,1)} %project.4), calls=%async_computation.3 | async-start | bytes 2359296 | tf_op jit(solution)/shard_map/all_to_all | solution.py:267
  99.5 136.8 %all-gather.19.cloned.1.call-start = ((), (), s32[]{:S(2)}) async-start(), calls=%async_computation.24 | async-start | bytes 5308416 | tf_op jit(solution)/shard_map/all_gather | solution.py:231
  127.6 31.6 %all-to-all-start.1 = ((bf16[4,192,768]{2,1,0:T(8,128)(2,1)}), bf16[4,192,768]{2,1,0:T(8,128)(2,1)S(1)}, u32[]{:S(2)}, u32[]{:S(2)}) async-start(bf16[4,192,768]{2,1,0:T(8,128)(2,1)} %project.3), calls=%async_computation.1 | async-start | bytes 2359296 | tf_op jit(solution)/shard_map/all_to_all | solution.py:267
  160.2 20.3 %all-to-all-start.6 = ((bf16[4,64,768]{2,1,0:T(8,128)(2,1)}), bf16[4,64,768]{2,1,0:T(8,128)(2,1)S(1)}, u32[]{:S(2)}, u32[]{:S(2)}) async-start(bf16[4,64,768]{2,1,0:T(8,128)(2,1)} %get-tuple-element.21.o_ref), calls=%async_computation.6 | async-start | bytes 786432 | tf_op jit(solution)/shard_map/all_to_all | solution.py:267
  180.5 21.6 %all-to-all-start.4 = ((bf16[4,64,768]{2,1,0:T(8,128)(2,1)}), bf16[4,64,768]{2,1,0:T(8,128)(2,1)S(1)}, u32[]{:S(2)}, u32[]{:S(2)}) async-start(bf16[4,64,768]{2,1,0:T(8,128)(2,1)} %get-tuple-element.20.o_ref), calls=%async_computation.4 | async-start | bytes 786432 | tf_op jit(solution)/shard_map/all_to_all | solution.py:267
  202.2 15.6 %all-to-all-start.2 = ((bf16[4,64,768]{2,1,0:T(8,128)(2,1)}), bf16[4,64,768]{2,1,0:T(8,128)(2,1)S(1)}, u32[]{:S(2)}, u32[]{:S(2)}) async-start(bf16[4,64,768]{2,1,0:T(8,128)(2,1)} %get-tuple-element.19.o_ref), calls=%async_computation.2 | async-start | bytes 786432 | tf_op jit(solution)/shard_map/all_to_all | solution.py:267
  282.7 32.7 %all-to-all-start.9 = ((bf16[4,64,768]{2,1,0:T(8,128)(2,1)}), bf16[4,64,768]{2,1,0:T(8,128)(2,1)}, u32[]{:S(2)}, u32[]{:S(2)}) async-start(bf16[4,64,768]{2,1,0:T(8,128)(2,1)} %get-tuple-element.75), calls=%async_computation.9 | async-start | bytes 786432 | tf_op jit(solution)/shard_map/all_to_all | solution.py:267
  315.4 30.0 %all-to-all-start.12 = ((bf16[4,192,768]{2,1,0:T(8,128)(2,1)}), bf16[4,192,768]{2,1,0:T(8,128)(2,1)}, u32[]{:S(2)}, u32[]{:S(2)}) async-start(bf16[4,192,768]{2,1,0:T(8,128)(2,1)} %attend_back.5), calls=%async_computation.12 | async-start | bytes 2359296 | tf_op jit(solution)/shard_map/all_to_all | solution.py:267
  345.4 36.6 %all-to-all-start.7 = ((bf16[4,64,768]{2,1,0:T(8,128)(2,1)}), bf16[4,64,768]{2,1,0:T(8,128)(2,1)}, u32[]{:S(2)}, u32[]{:S(2)}) async-start(bf16[4,64,768]{2,1,0:T(8,128)(2,1)} %get-tuple-element.76), calls=%async_computation.7 | async-start | bytes 786432 | tf_op jit(solution)/shard_map/all_to_all | solution.py:267
  349.6 164.9 %reduce-scatter.11.cloned.1.call-start = ((), (), s32[]{:S(2)}) async-start(), calls=%async_computation.27 | async-start | bytes 1327104 | tf_op jit(solution)/shard_map/reduce_scatter | solution.py:308
  382.1 33.8 %all-to-all-start.10 = ((bf16[4,192,768]{2,1,0:T(8,128)(2,1)}), bf16[4,192,768]{2,1,0:T(8,128)(2,1)}, u32[]{:S(2)}, u32[]{:S(2)}) async-start(bf16[4,192,768]{2,1,0:T(8,128)(2,1)} %attend_back.4), calls=%async_computation.10 | async-start | bytes 2359296 | tf_op jit(solution)/shard_map/all_to_all | solution.py:267
  415.9 31.2 %all-to-all-start.8 = ((bf16[4,192,768]{2,1,0:T(8,128)(2,1)}), bf16[4,192,768]{2,1,0:T(8,128)(2,1)}, u32[]{:S(2)}, u32[]{:S(2)}) async-start(bf16[4,192,768]{2,1,0:T(8,128)(2,1)} %attend_back.3), calls=%async_computation.8 | async-start | bytes 2359296 | tf_op jit(solution)/shard_map/all_to_all | solution.py:267
  421.0 93.4 %reduce-scatter.9.cloned.1.call-start = ((), (), s32[]{:S(2)}) async-start(), calls=%async_computation.26 | async-start | bytes 1327104 | tf_op jit(solution)/shard_map/reduce_scatter | solution.py:308
  424.8 89.6 %reduce-scatter.7.cloned.1.call-start = ((), (), s32[]{:S(2)}) async-start(), calls=%async_computation.25 | async-start | bytes 1327104 | tf_op jit(solution)/shard_map/reduce_scatter | solution.py:308
  450.9 92.1 %reduce-scatter.13.cloned.1.call-start = ((), (), s32[]{:S(2)}) async-start(), calls=%async_computation.28 | async-start | bytes 1327104 | tf_op jit(solution)/shard_map/reduce_scatter | solution.py:308
  454.8 145.5 %reduce-scatter.15.cloned.1.call-start = ((), (), s32[]{:S(2)}) async-start(), calls=%async_computation.29 | async-start | bytes 5308416 | tf_op jit(solution)/shard_map/reduce_scatter | solution.py:308
  464.4 193.0 %reduce-scatter.17.cloned.1.call-start = ((), (), s32[]{:S(2)}) async-start(), calls=%async_computation.30 | async-start | bytes 5308416 | tf_op jit(solution)/shard_map/reduce_scatter | solution.py:308
  474.3 267.0 %all-reduce.5.cloned.1.call-start = ((), (), s32[]{:S(2)}) async-start(), calls=%async_computation.31 | async-start | bytes 3833856 | tf_op jit(solution)/shard_map/psum | solution.py:357
  (60 other events, 1976.7 us)
Sparse Core Ops, SparseCore 0:
  10.4 26.7 all-gather.12
  39.7 23.9 all-gather.10
  66.1 23.9 all-gather.8
  92.4 23.9 all-gather.14
  118.6 38.7 all-gather.16
  159.7 38.7 all-gather.18
  382.2 36.8 reduce-scatter.10
  425.6 37.0 reduce-scatter.8
  466.5 36.6 reduce-scatter.6
  506.3 36.6 reduce-scatter.12
  546.5 53.7 reduce-scatter.14
  603.6 53.7 reduce-scatter.16
  660.6 80.6 all-reduce.4

commit v2 on v1

--- a/solution.py
+++ b/solution.py
@@ -204,6 +204,155 @@
         ),
         name="attend_back",
     )(x, g, o, lse, cosine, sine)
+
+
+GELU_C = math.sqrt(2.0 / math.pi)
+GELU_A = 0.044715
+
+
+def middle_kernel(
+    n,
+    slots,
+    blocks,
+    tokens_ref,
+    cot_ref,
+    vec_ref,
+    bias_ref,
+    up_ref,
+    down_ref,
+    out_w_ref,
+    *refs,
+):
+    mixed_refs, refs = refs[:slots], refs[slots:]
+    output_ref, grad_hidden_ref, sums_ref, bias_grad_ref, g_down_ref, g_pack_ref, *refs = refs
+    grad_mixed_refs, (mixed_ref, attn_out_ref, mlp_in_ref, low_ref, back_ref) = refs[:slots], refs[slots:]
+    j = pl.program_id(0)
+    tok, width = tokens_ref.shape
+    gate_attn, shift, scale, gate, gain, down_bias = (vec_ref[i : i + 1, :] for i in range(6))
+    piece = min(256, tok)
+    pieces = tok // piece
+
+    @pl.when(j == 0)
+    def _():
+        for s in range(slots):
+            for c in range(n):
+                head = c * slots + s
+                mixed_ref[head * HD : (head + 1) * HD, :] = mixed_refs[s][c]
+        attn_out_ref[...] = mm(mixed_ref[...], out_w_ref[...], 0, 0)
+
+        def prepare(i, _):
+            rows = pl.ds(pl.multiple_of(i * piece, piece), piece)
+            hidden = tokens_ref[rows, :] + gate_attn * attn_out_ref[rows, :]
+            grad_hidden_ref[rows, :] = hidden
+            hat, _ = normalize(hidden)
+            mlp_in_ref[rows, :] = (hat * gain * (1.0 + scale) + shift).astype(BF16)
+            low_ref[rows, :] = (gate * cot_ref[rows, :]).astype(BF16)
+            return 0
+
+        lax.fori_loop(0, pieces, prepare, 0)
+        output_ref[...] = jnp.zeros_like(output_ref)
+        back_ref[...] = jnp.zeros_like(back_ref)
+
+    @pl.when(j < blocks)
+    def _():
+        mlp_in, low = mlp_in_ref[...], low_ref[...]
+        x = mm(mlp_in, up_ref[...], 1, 0) + bias_ref[0]
+        grad_act = mm(low, down_ref[...], 1, 1)
+        square = x * x
+        t = jnp.tanh(x * (GELU_C + GELU_C * GELU_A * square))
+        half = 0.5 + 0.5 * t
+        act = (x * half).astype(BF16)
+        slope = half + x * (0.5 - 0.5 * t * t) * (GELU_C + 3.0 * GELU_C * GELU_A * square)
+        grad_pre = grad_act * slope
+        bias_grad_ref[0] = jnp.sum(grad_pre, axis=0, keepdims=True)
+        pre_low = grad_pre.astype(BF16)
+        output_ref[...] += mm(act, down_ref[...], 1, 0)
+        back_ref[...] += mm(pre_low, up_ref[...], 1, 1)
+        g_down_ref[...] = mm(act, low, 0, 0).astype(BF16)
+        g_pack_ref[...] = mm(mlp_in, pre_low, 0, 0).astype(BF16)
+
+    @pl.when(j == blocks)
+    def _():
+        def finish(i, sums):
+            rows = pl.ds(pl.multiple_of(i * piece, piece), piece)
+            cot = cot_ref[rows, :]
+            branch = output_ref[rows, :] + down_bias
+            hidden = grad_hidden_ref[rows, :]
+            output_ref[rows, :] = hidden + gate * branch
+            hat, inv = normalize(hidden)
+            back = back_ref[rows, :]
+            grad_hidden = cot + norm_back(back * ((1.0 + scale) * gain), hat, inv)
+            grad_hidden_ref[rows, :] = grad_hidden
+            low_ref[rows, :] = (gate_attn * grad_hidden).astype(BF16)
+            adds = (grad_hidden * attn_out_ref[rows, :], back, back * hat, cot * branch, cot)
+            return tuple(a + jnp.sum(v, axis=0, keepdims=True) for a, v in zip(sums, adds))
+
+        zero = jnp.zeros((1, width), F32)
+        sums = lax.fori_loop(0, pieces, finish, (zero,) * 5)
+        for i in range(5):
+            sums_ref[i : i + 1, :] = sums[i]
+        attn_low = low_ref[...]
+        g_pack_ref[...] = mm(mixed_ref[...], attn_low, 1, 0).astype(BF16)
+        grad_mixed = mm(out_w_ref[...], attn_low, 1, 1).astype(BF16)
+        for s in range(slots):
+            for c in range(n):
+                head = c * slots + s
+                grad_mixed_refs[s][c] = grad_mixed[head * HD : (head + 1) * HD]
+
+
+def middle(tokens, cot, vectors, up_bias, w_pack, w_down, mixed):
+    tok, width = tokens.shape
+    ff = w_down.shape[0]
+    blocks = ff // width
+    slots = len(mixed)
+    n = mixed[0].shape[0]
+    whole = lambda shape: pl.BlockSpec(shape, lambda j: (0,) * len(shape), pipeline_mode=pl.Buffered(1))
+    fixed = lambda shape: pl.BlockSpec(shape, lambda j: (0,) * len(shape))
+    last = blocks - 1
+    head_shape = mixed[0].shape
+    flops = 2 * tok * width * (6 * ff + 3 * width)
+    return pl.pallas_call(
+        partial(middle_kernel, n, slots, blocks),
+        grid=(blocks + 1,),
+        in_specs=[
+            whole(tokens.shape),
+            whole(cot.shape),
+            whole(vectors.shape),
+            pl.BlockSpec((1, 1, width), lambda j: (jnp.minimum(j, last), 0, 0)),
+            pl.BlockSpec((width, width), lambda j: (0, jnp.minimum(j, last))),
+            pl.BlockSpec((width, width), lambda j: (jnp.minimum(j, last), 0)),
+            pl.BlockSpec((width, width), lambda j: (0, blocks), pipeline_mode=pl.Buffered(1)),
+        ]
+        + [whole(head_shape)] * slots,
+        out_specs=[
+            fixed((tok, width)),
+            fixed((tok, width)),
+            fixed((8, width)),
+            pl.BlockSpec((1, 1, width), lambda j: (jnp.minimum(j, last), 0, 0)),
+            pl.BlockSpec((width, width), lambda j: (jnp.minimum(j, last), 0)),
+            pl.BlockSpec((width, width), lambda j: (0, j)),
+        ]
+        + [fixed(head_shape)] * slots,
+        out_shape=[
+            jax.ShapeDtypeStruct((tok, width), F32),
+            jax.ShapeDtypeStruct((tok, width), F32),
+            jax.ShapeDtypeStruct((8, width), F32),
+            jax.ShapeDtypeStruct((blocks, 1, width), F32),
+            jax.ShapeDtypeStruct((ff, width), BF16),
+            jax.ShapeDtypeStruct((width, ff + width), BF16),
+        ]
+        + [jax.ShapeDtypeStruct(head_shape, BF16)] * slots,
+        scratch_shapes=[
+            pltpu.VMEM((width, tok), BF16),
+            pltpu.VMEM((tok, width), F32),
+            pltpu.VMEM((tok, width), BF16),
+            pltpu.VMEM((tok, width), BF16),
+            pltpu.VMEM((tok, width), F32),
+        ],
+        compiler_params=pltpu.CompilerParams(vmem_limit_bytes=VMEM_LIMIT),
+        cost_estimate=pl.CostEstimate(flops=flops, bytes_accessed=6 * ff * width * 2, transcendentals=tok * ff),
+        name="middle",
+    )(tokens, cot, vectors, up_bias.reshape(blocks, 1, width), w_pack, w_down, w_pack, *mixed)
 
 
 def per_device(
@@ -250,8 +399,7 @@
     qkv_slots = [
         gather(qkv_low[:, :, :, s].transpose(0, 2, 1, 3).reshape(shard, n * 3 * HD)) for s in range(slots)
     ]
-    out_full = gather(out_weight.astype(BF16))
-    up_full = gather(up_weight.astype(BF16))
+    w_pack = gather(jnp.concatenate([up_weight.astype(BF16), out_weight.astype(BF16)], axis=1))
     down_full = gather(down_weight.astype(BF16))
 
     inv_freq = jnp.exp(-math.log(10000.0) * jnp.arange(HD // 2, dtype=F32) * (2.0 / HD))
@@ -272,65 +420,46 @@
         mixed_heads.append(o)
         log_totals.append(lse)
         mixed_back.append(swap(o))
-    mixed = jnp.stack(mixed_back, axis=1).reshape(width, tok)
-
-    attn_out = mm(mixed, out_full, 0, 0)
-    hidden = tokens + gate_attn * attn_out
-    hat_mlp, inv_mlp = normalize(hidden)
-    normed_mlp = hat_mlp * mlp_gain_full
-    mlp_in = (normed_mlp * (1.0 + scale_mlp) + shift_mlp).astype(BF16)
-    pre_act = jnp.dot(mlp_in, up_full, preferred_element_type=F32) + up_bias_full
-    gelu_act, gelu_pull = jax.vjp(partial(jax.nn.gelu, approximate=True), pre_act)
-    up_act = gelu_act.astype(BF16)
-    branch = jnp.dot(up_act, down_full, preferred_element_type=F32) + down_bias_full
-    output = hidden + gate_mlp * branch
-    grad_out = cotangent[0]
-    grad_branch = gate_mlp * grad_out
-    branch_low = grad_branch.astype(BF16)
-    down_weight_grad = mm(up_act, branch_low, 0, 0)
-    grad_act = mm(branch_low, down_full, 1, 1)
-    grad_pre = gelu_pull(grad_act)[0]
-    pre_low = grad_pre.astype(BF16)
-    up_weight_grad = mm(mlp_in, pre_low, 0, 0)
-    grad_mlp_in = mm(pre_low, up_full, 1, 1)
-    grad_normed_mlp = grad_mlp_in * (1.0 + scale_mlp)
-    grad_hidden = grad_out + norm_back(grad_normed_mlp * mlp_gain_full, hat_mlp, inv_mlp)
-    attn_low = (gate_attn * grad_hidden).astype(BF16)
-    out_weight_grad = mm(mixed, attn_low, 1, 0)
-    grad_mixed = mm(out_full, attn_low, 1, 1).astype(BF16)
-    grad_split = grad_mixed.reshape(n, slots, HD, tok)
+    vectors = jnp.stack(
+        [gate_attn, shift_mlp, scale_mlp, gate_mlp, mlp_gain_full, down_bias_full, gate_mlp, gate_mlp], axis=0
+    )
+    output, grad_hidden, sums, up_bias_sum, g_down, g_pack, *grad_mixed = middle(
+        tokens, cotangent[0], vectors, up_bias_full, w_pack, down_full, mixed_back
+    )
+    scatter = lambda a: lax.psum_scatter(a, "fsdp", scatter_dimension=0, tiled=True)
+    part_pack = scatter(g_pack)
+    part_down = scatter(g_down)
 
     grad_slots = []
     for s in range(slots):
-        g = swap(grad_split[:, s])
+        g = swap(grad_mixed[s])
         grad_slots.append(swap(attend_back(heads[s], g, mixed_heads[s], log_totals[s], cos_all, sin_all)))
 
-    scatter = lambda a: lax.psum_scatter(a.astype(BF16), "fsdp", scatter_dimension=0, tiled=True)
     qkv_parts = []
     grad_attn_in = None
     for s in range(slots):
         rows = grad_slots[s].reshape(n * 3 * HD, tok)
-        qkv_parts.append(scatter(mm(attn_in, rows, 0, 1)))
+        qkv_parts.append(mm(attn_in, rows, 0, 1).astype(BF16))
         part = mm(rows, qkv_slots[s], 0, 1)
         grad_attn_in = part if grad_attn_in is None else grad_attn_in + part
     grad_normed_attn = grad_attn_in * (1.0 + scale_attn)
     inputs_grad = grad_hidden + norm_back(grad_normed_attn * attn_gain_full, hat_attn, inv_attn)
 
-    part_down = scatter(down_weight_grad)
-    part_up = scatter(up_weight_grad)
-    part_out = scatter(out_weight_grad)
+    part_qkv = scatter(jnp.concatenate(qkv_parts, axis=1))
+    back_sum = jnp.sum(grad_attn_in, axis=0)
+    hat_sum = jnp.sum(grad_attn_in * hat_attn, axis=0)
     vectors = jnp.concatenate(
         [
-            jnp.sum(grad_attn_in, axis=0),
-            jnp.sum(grad_attn_in * normed_attn, axis=0),
-            jnp.sum(grad_hidden * attn_out, axis=0),
-            jnp.sum(grad_mlp_in, axis=0),
-            jnp.sum(grad_mlp_in * normed_mlp, axis=0),
-            jnp.sum(grad_out * branch, axis=0),
-            jnp.sum(grad_normed_attn * hat_attn, axis=0),
-            jnp.sum(grad_normed_mlp * hat_mlp, axis=0),
-            jnp.sum(grad_pre, axis=0),
-            jnp.sum(grad_branch, axis=0),
+            back_sum,
+            hat_sum * attn_gain_full,
+            sums[0],
+            sums[1],
+            sums[2] * mlp_gain_full,
+            sums[3],
+            hat_sum * (1.0 + scale_attn),
+            sums[2] * (1.0 + scale_mlp),
+            up_bias_sum.reshape(-1),
+            sums[4] * gate_mlp,
         ]
     )
     summed = lax.all_gather(lax.psum(vectors, "seq"), "fsdp", axis=0)
@@ -354,13 +483,13 @@
     _, silu_pull = jax.vjp(jax.nn.silu, conditioning)
     conditioning_grad = silu_pull(grad_cond_act)[0]
 
-    qkv_sum = lax.psum(jnp.stack(qkv_parts, axis=0), "seq").astype(F32)
+    qkv_sum = lax.psum(part_qkv, "seq").astype(F32)
     qkv_weight_grad = (
-        qkv_sum.reshape(slots, shard, n, 3, HD).transpose(1, 3, 2, 0, 4).reshape(shard, 3 * width)
-    )
-    out_sum = lax.psum(part_out, "seq").astype(F32)
-    up_sum = lax.psum(part_up, "seq").astype(F32)
+        qkv_sum.reshape(shard, slots, n, 3, HD).transpose(0, 3, 2, 1, 4).reshape(shard, 3 * width)
+    )
+    pack_sum = lax.psum(part_pack, "seq").astype(F32)
     down_sum = lax.psum(part_down, "seq").astype(F32)
+    out_sum, up_sum = pack_sum[:, ff:], pack_sum[:, :ff]
     return (
         output[None],
         inputs_grad[None],

time: 765 us -> 692 us (0.905)
  matrix products: 95.4 us -> 17.3 us
  Pallas kernels: 147 us -> 186 us
  waiting for transfers between devices: 320 us -> 285 us
  blocking collectives: 64.6 us -> 77.4 us
    dot_general x14 -> x7, matrix products: 70.8 us -> 15.2 us  [mm(): lax.dot_general(a, b, (((ca,), (cb,)), ((), ())), preferred_element_type=...]
    pallas_call x0 -> x1, Pallas kernels: none -> 39.5 us  [middle(): pl.pallas_call(partial(middle_kernel, n, slots, blocks), grid=(blocks + 1...]
    reduce_scatter x6 -> x2, waiting for transfers between devices: 141 us -> 118 us  [per_device(): lax.psum_scatter(a, 'fsdp', scatter_dimension=0, tiled=True)]
    dot_general x2 -> x0, matrix products: 21.8 us -> none  [the longest x1 11.8 us: per_device(): jnp.dot(mlp_in, up_full, preferred_element_type=F32) + up_bias_full]
    all_to_all x12 -> x11, waiting for transfers between devices: 115 us -> 94.3 us  [per_device(): lax.all_to_all(a, 'seq', split_axis=0, concat_axis=0, tiled=True)]
    all_to_all x0 -> x1, blocking collectives: none -> 13.5 us  [per_device(): lax.all_to_all(a, 'seq', split_axis=0, concat_axis=0, tiled=True)]
    all_to_all x12 -> x11, starting transfers between devices: 55.2 us -> 48.9 us  [per_device(): lax.all_to_all(a, 'seq', split_axis=0, concat_axis=0, tiled=True)]
  transfers between devices with their start and end apart: 26 -> 21, of which waited for: 12 -> 12; matrix products, arithmetic and copies ran while one was open for 13% -> 7% of each run, Pallas kernels for 19% -> 21%
where the time goes in v2:
time: 692 us; the launch traced here: 682 us
  waiting for transfers between devices  285 us (41%)
  Pallas kernels  186 us (27%)
  blocking collectives  77.4 us (11%)
  starting transfers between devices  52.8 us (8%)
  local copies, waits for them, and re-layouts  31.2 us (5%)
  other arithmetic  17.3 us (2%)
  matrix products  17.3 us (2%)
  between operations  15.7 us (2%)
    reduce_scatter x2, waiting for transfers between devices, per_device(): lax.psum_scatter(a, 'fsdp', scatter_dimension=0, tiled=True)  118 us
    all_to_all x11, waiting for transfers between devices, per_device(): lax.all_to_all(a, 'seq', split_axis=0, concat_axis=0, tiled=True)  94.3 us
    pallas_call x3, Pallas kernels, attend_back(): pl.pallas_call(partial(attend_back_kernel, n, tok, 2), grid=(n,), in_spec...  85 us
    psum x1, waiting for transfers between devices, per_device(): qkv_sum = lax.psum(part_qkv, 'seq').astype(F32)  61.6 us
    pallas_call x3, Pallas kernels, attend(): pl.pallas_call(partial(attend_kernel, n, tok, 2), grid=(n,), in_specs=[pl...  49.8 us
    all_to_all x11, starting transfers between devices, per_device(): lax.all_to_all(a, 'seq', split_axis=0, concat_axis=0, tiled=True)  48.9 us
    pallas_call x1, Pallas kernels, middle(): pl.pallas_call(partial(middle_kernel, n, slots, blocks), grid=(blocks + 1...  39.5 us
    unnamed x2, blocking collectives  38.3 us
  transfers between devices with their start and end apart: 21, of which 12 were waited for; matrix products, arithmetic and copies ran while one was open for 7% of the time, Pallas kernels for 21%

profile of v2, /device:TPU:0, one launch (start us, length us, event | category | flops | bytes accessed | tf_op | source)
XLA Modules:
  0.0 682.3 jit_solution(785813915497360643)
XLA Ops:
  17.2 25.8 %all-reduce = f32[6400]{0:T(1024)S(1)} all-reduce(f32[6400]{0:T(1024)S(1)} %dynamic-update-slice), channel_id=2, replica_groups=mesh['fsdp'=8,'seq'=4] {'fsdp'}, use_global_device_ids=true, to_apply=%add | all-reduce | flops 6400 | bytes 51200
  67.7 23.1 %all-to-all-done.1.x_ref = bf16[4,192,768]{2,1,0:T(8,128)(2,1)S(1)} async-done(((bf16[4,192,768]{2,1,0:T(8,128)(2,1)}), bf16[4,192,768]{2,1,0:T(8,128)(2,1)S(1)}, u32[]{:S(2)}, u32[]{:S(2)}) %all-to-all-start.1) | async-done | bytes 1179680 | tf_op jit(solution)/shard_map/all_to_all | solution.py:415
  98.2 24.2 %all-to-all-done.3.x_ref = bf16[4,192,768]{2,1,0:T(8,128)(2,1)S(1)} async-done(((bf16[4,192,768]{2,1,0:T(8,128)(2,1)}), bf16[4,192,768]{2,1,0:T(8,128)(2,1)S(1)}, u32[]{:S(2)}, u32[]{:S(2)}) %all-to-all-start.3) | async-done | bytes 1179680 | tf_op jit(solution)/shard_map/all_to_all | solution.py:415
  125.9 16.6 %attend.3 = (bf16[4,64,768]{2,1,0:T(8,128)(2,1)}, f32[4,1,768]{2,1,0:T(1,128)}) custom-call(bf16[4,192,768]{2,1,0:T(8,128)(2,1)} %copy-done.8), custom_call_target="tpu_custom_call" | custom-call | flops 9663676416 | bytes 1572864 | tf_op jit(solution)/shard_map/attend/pallas_call | solution.py:111
  142.6 11.4 %all-to-all-done.5.x_ref = bf16[4,192,768]{2,1,0:T(8,128)(2,1)S(1)} async-done(((bf16[4,192,768]{2,1,0:T(8,128)(2,1)}), bf16[4,192,768]{2,1,0:T(8,128)(2,1)S(1)}, u32[]{:S(2)}, u32[]{:S(2)}) %all-to-all-start.5) | async-done | bytes 1179680 | tf_op jit(solution)/shard_map/all_to_all | solution.py:415
  157.7 16.6 %attend.4 = (bf16[4,64,768]{2,1,0:T(8,128)(2,1)}, f32[4,1,768]{2,1,0:T(1,128)}) custom-call(bf16[4,192,768]{2,1,0:T(8,128)(2,1)} %copy-done.10), custom_call_target="tpu_custom_call" | custom-call | flops 9663676416 | bytes 1572864 | tf_op jit(solution)/shard_map/attend/pallas_call | solution.py:111
  179.4 16.6 %attend.5 = (bf16[4,64,768]{2,1,0:T(8,128)(2,1)}, f32[4,1,768]{2,1,0:T(1,128)}) custom-call(bf16[4,192,768]{2,1,0:T(8,128)(2,1)} %copy-done.9), custom_call_target="tpu_custom_call" | custom-call | flops 9663676416 | bytes 1572864 | tf_op jit(solution)/shard_map/attend/pallas_call | solution.py:111
  196.0 5.5 all-to-all-start.6
  203.0 8.9 %all-to-all-done.6.refs_2_ = bf16[4,64,768]{2,1,0:T(8,128)(2,1)S(1)} async-done(((bf16[4,64,768]{2,1,0:T(8,128)(2,1)}), bf16[4,64,768]{2,1,0:T(8,128)(2,1)S(1)}, u32[]{:S(2)}, u32[]{:S(2)}) %all-to-all-start.6) | async-done | bytes 393248 | tf_op jit(solution)/shard_map/all_to_all | solution.py:415
  212.7 39.5 %middle.1 = (f32[768,768]{1,0:T(8,128)}, f32[768,768]{1,0:T(8,128)}, f32[8,768]{1,0:T(8,128)}, f32[4,1,768]{2,1,0:T(1,128)}, bf16[3072,768]{1,0:T(8,128)(2,1)}, ...) custom-call(f32[768,768]{1,0:T(8,128)} %bitcast.68, ...), custom_call_target="tpu_custom_call" | custom-call | flops 24461180928 | bytes 28311552 | tf_op jit(solution)/shard_map/middle/pallas_call | solution.py:314
  252.2 13.5 %all_to_all.69.g_ref = bf16[4,64,768]{2,1,0:T(8,128)(2,1)} all-to-all(bf16[4,64,768]{2,1,0:T(8,128)(2,1)} %get-tuple-element.35), channel_id=1, replica_groups=mesh['fsdp'=8,'seq'=4] {'seq'}, dimensions={0} | all-to-all | bytes 786432 | tf_op jit(solution)/shard_map/all_to_all | solution.py:415
  271.5 7.3 %all-to-all-done.7.g_ref = bf16[4,64,768]{2,1,0:T(8,128)(2,1)S(1)} async-done(((bf16[4,64,768]{2,1,0:T(8,128)(2,1)}), bf16[4,64,768]{2,1,0:T(8,128)(2,1)S(1)}, u32[]{:S(2)}, u32[]{:S(2)}) %all-to-all-start.7) | async-done | bytes 393248 | tf_op jit(solution)/shard_map/all_to_all | solution.py:415
  282.4 28.4 %attend_back.4 = bf16[4,192,768]{2,1,0:T(8,128)(2,1)} custom-call(bf16[4,192,768]{2,1,0:T(8,128)(2,1)} %copy-done.10, bf16[4,64,768]{2,1,0:T(8,128)(2,1)} %all_to_all.69.g_ref, bf16[4,64,768]{2,1,0:T(8,128)(2,1)} %get-tuple-element.29.o_ref, f32[4,1,768]{2,1,0:T(1,128)} %get-tuple-element.36.lse_ref, f32[4,32,768]{2,1,0:T(8,128)} %get-tuple-element.99.cos_ref, ...), custom_call_target="tpu_custom_call" | custom-call | flops 24159191040 | bytes 3145728 | tf_op jit(solution)/shard_map/attend_back/pallas_call | solution.py:189
  315.9 28.3 %attend_back.3 = bf16[4,192,768]{2,1,0:T(8,128)(2,1)} custom-call(bf16[4,192,768]{2,1,0:T(8,128)(2,1)} %copy-done.8, bf16[4,64,768]{2,1,0:T(8,128)(2,1)} %copy-done.25, bf16[4,64,768]{2,1,0:T(8,128)(2,1)} %get-tuple-element.28.o_ref, f32[4,1,768]{2,1,0:T(1,128)} %get-tuple-element.34.lse_ref, f32[4,32,768]{2,1,0:T(8,128)} %get-tuple-element.99.cos_ref, ...), custom_call_target="tpu_custom_call" | custom-call | flops 24159191040 | bytes 3145728 | tf_op jit(solution)/shard_map/attend_back/pallas_call | solution.py:189
  344.2 5.3 all-to-all-start.8
  349.6 28.3 %attend_back.5 = bf16[4,192,768]{2,1,0:T(8,128)(2,1)} custom-call(bf16[4,192,768]{2,1,0:T(8,128)(2,1)} %copy-done.9, bf16[4,64,768]{2,1,0:T(8,128)(2,1)} %copy-done.24, bf16[4,64,768]{2,1,0:T(8,128)(2,1)} %get-tuple-element.30.o_ref, f32[4,1,768]{2,1,0:T(1,128)} %get-tuple-element.38.lse_ref, f32[4,32,768]{2,1,0:T(8,128)} %get-tuple-element.99.cos_ref, ...), custom_call_target="tpu_custom_call" | custom-call | flops 24159191040 | bytes 3145728 | tf_op jit(solution)/shard_map/attend_back/pallas_call | solution.py:189
  389.7 19.3 %all-to-all-done.12 = bf16[4,192,768]{2,1,0:T(8,128)(2,1)S(1)} async-done(((bf16[4,192,768]{2,1,0:T(8,128)(2,1)}), bf16[4,192,768]{2,1,0:T(8,128)(2,1)S(1)}, u32[]{:S(2)}, u32[]{:S(2)}) %all-to-all-start.12) | async-done | bytes 1179680 | tf_op jit(solution)/shard_map/all_to_all | solution.py:415
  413.5 5.8 copy.49
  432.3 17.4 %psum.28 = f32[1,9984]{1,0:T(1,128)S(1)} all-reduce(f32[1,9984]{1,0:T(1,128)S(1)} %all_gather.34), channel_id=1, replica_groups=mesh['fsdp'=8,'seq'=4] {'seq'}, use_global_device_ids=true, to_apply=%region_6.7 | all-reduce | flops 9984 | bytes 79872 | tf_op jit(solution)/shard_map/psum | solution.py:465
  449.7 8.2 %all-gather.1 = f32[8,1,9984]{2,1,0:T(1,128)S(1)} all-gather(f32[1,1,9984]{2,1,0:T(1,128)S(1)} %bitcast.82), channel_id=1, replica_groups=mesh['fsdp'=8,'seq'=4] {'fsdp'}, dimensions={0}, use_global_device_ids=true | all-gather | bytes 359424 | tf_op jit(solution)/shard_map/all_gather | solution.py:465
  467.1 55.1 %reduce-scatter.8.cloned.1.call-done = bf16[384,768]{1,0:T(8,128)(2,1)} async-done(((bf16[3072,768]{1,0:T(8,128)(2,1)}), bf16[384,768]{1,0:T(8,128)(2,1)}) %reduce-scatter.8.cloned.1.call-update) | async-done | bytes 589840 | tf_op jit(solution)/shard_map/reduce_scatter | solution.py:429
  522.2 63.2 %reduce-scatter.6.cloned.1.call-done = bf16[96,3840]{1,0:T(8,128)(2,1)} async-done(((bf16[768,3840]{1,0:T(8,128)(2,1)}), bf16[96,3840]{1,0:T(8,128)(2,1)}) %reduce-scatter.6.cloned.1.call-update) | async-done | bytes 737296 | tf_op jit(solution)/shard_map/reduce_scatter | solution.py:429
  587.1 12.5 %all-reduce.1 = f32[8,128]{1,0:T(8,128)S(1)} all-reduce(f32[8,128]{1,0:T(8,128)S(1)} %fusion.3), channel_id=3, replica_groups=mesh['fsdp'=8,'seq'=4] {'fsdp'}, use_global_device_ids=true, to_apply=%region_7.8.clone | all-reduce | flops 1024 | bytes 8192
  607.6 61.6 %all-reduce.5.cloned.1.call-done = (bf16[96,2304]{0,1:T(8,128)(2,1)}, bf16[96,3840]{1,0:T(8,128)(2,1)}, bf16[384,768]{1,0:T(8,128)(2,1)}) async-done(((bf16[96,2304]{0,1:T(8,128)(2,1)}, bf16[96,3840]{1,0:T(8,128)(2,1)}, bf16[384,768]{1,0:T(8,128)(2,1)}), (bf16[96,2304]{0,1:T(8,128)(2,1)}, bf16[96,3840]{1,0:T(8,128)(2,1)}, bf16[384,768]{1,0:T(8,128)(2,1)})) %all-reduce.5.cloned.1.call-update) | async-done | bytes 1769488 | tf_op jit(solution)/shard_map/psum | solution.py:486
  (216 shorter events, 124.1 us)
Async XLA Ops:
  7.2 46.6 %all-gather.12.cloned.1.call-start = ((), (), s32[]{:S(2)}) async-start(), calls=%async_computation.18 | async-start | bytes 1327104 | tf_op jit(solution)/shard_map/all_gather | solution.py:380
  9.7 54.2 %all-gather.14.cloned.1.call-start = ((), (), s32[]{:S(2)}) async-start(), calls=%async_computation.19 | async-start | bytes 1327104 | tf_op jit(solution)/shard_map/all_gather | solution.py:380
  10.6 83.8 %all-gather.16.cloned.1.call-start = ((), (), s32[]{:S(2)}) async-start(), calls=%async_computation.20 | async-start | bytes 1327104 | tf_op jit(solution)/shard_map/all_gather | solution.py:380
  11.5 200.4 %all-gather.10.cloned.1.call-start = ((), (), s32[]{:S(2)}) async-start(), calls=%async_computation.17 | async-start | bytes 5308416 | tf_op jit(solution)/shard_map/all_gather | solution.py:380
  12.6 199.4 %all-gather.8.cloned.1.call-start = ((), (), s32[]{:S(2)}) async-start(), calls=%async_computation.16 | async-start | bytes 6635520 | tf_op jit(solution)/shard_map/all_gather | solution.py:380
  43.1 158.4 %copy-start.28 = (f32[8,800]{1,0:T(8,128)}, f32[8,800]{1,0:T(8,128)S(1)}, u32[]{:S(2)}) copy-start(f32[8,800]{1,0:T(8,128)S(1)} %reshape.282) | copy-start | bytes 76804
  43.9 8.2 %all-to-all-start = ((f32[8,1,576]{2,1,0:T(1,128)}), f32[8,1,576]{2,1,0:T(1,128)S(1)}, u32[]{:S(2)}, u32[]{:S(2)}) async-start(f32[8,1,576]{2,1,0:T(1,128)} %copy.39), calls=%async_computation | async-start | bytes 40960 | tf_op jit(solution)/shard_map/all_to_all | solution.py:394
  48.0 153.6 %copy-start.30 = (f32[8,96]{1,0:T(8,128)}, f32[8,96]{1,0:T(8,128)S(1)}, u32[]{:S(2)}) copy-start(f32[8,96]{1,0:T(8,128)S(1)} %get-tuple-element.91) | copy-start | bytes 9220
  57.6 33.2 %all-to-all-start.1 = ((bf16[4,192,768]{2,1,0:T(8,128)(2,1)}), bf16[4,192,768]{2,1,0:T(8,128)(2,1)S(1)}, u32[]{:S(2)}, u32[]{:S(2)}) async-start(bf16[4,192,768]{2,1,0:T(8,128)(2,1)} %project.3), calls=%async_computation.1 | async-start | bytes 2359296 | tf_op jit(solution)/shard_map/all_to_all | solution.py:415
  90.8 31.6 %all-to-all-start.3 = ((bf16[4,192,768]{2,1,0:T(8,128)(2,1)}), bf16[4,192,768]{2,1,0:T(8,128)(2,1)S(1)}, u32[]{:S(2)}, u32[]{:S(2)}) async-start(bf16[4,192,768]{2,1,0:T(8,128)(2,1)} %project.4), calls=%async_computation.3 | async-start | bytes 2359296 | tf_op jit(solution)/shard_map/all_to_all | solution.py:415
  122.4 31.6 %all-to-all-start.5 = ((bf16[4,192,768]{2,1,0:T(8,128)(2,1)}), bf16[4,192,768]{2,1,0:T(8,128)(2,1)S(1)}, u32[]{:S(2)}, u32[]{:S(2)}) async-start(bf16[4,192,768]{2,1,0:T(8,128)(2,1)} %project.5), calls=%async_computation.5 | async-start | bytes 2359296 | tf_op jit(solution)/shard_map/all_to_all | solution.py:415
  154.0 20.3 %all-to-all-start.2 = ((bf16[4,64,768]{2,1,0:T(8,128)(2,1)}), bf16[4,64,768]{2,1,0:T(8,128)(2,1)S(1)}, u32[]{:S(2)}, u32[]{:S(2)}) async-start(bf16[4,64,768]{2,1,0:T(8,128)(2,1)} %get-tuple-element.28.o_ref), calls=%async_computation.2 | async-start | bytes 786432 | tf_op jit(solution)/shard_map/all_to_all | solution.py:415
  174.3 21.6 %all-to-all-start.4 = ((bf16[4,64,768]{2,1,0:T(8,128)(2,1)}), bf16[4,64,768]{2,1,0:T(8,128)(2,1)S(1)}, u32[]{:S(2)}, u32[]{:S(2)}) async-start(bf16[4,64,768]{2,1,0:T(8,128)(2,1)} %get-tuple-element.29.o_ref), calls=%async_computation.4 | async-start | bytes 786432 | tf_op jit(solution)/shard_map/all_to_all | solution.py:415
  196.0 16.0 %all-to-all-start.6 = ((bf16[4,64,768]{2,1,0:T(8,128)(2,1)}), bf16[4,64,768]{2,1,0:T(8,128)(2,1)S(1)}, u32[]{:S(2)}, u32[]{:S(2)}) async-start(bf16[4,64,768]{2,1,0:T(8,128)(2,1)} %get-tuple-element.30.o_ref), calls=%async_computation.6 | async-start | bytes 786432 | tf_op jit(solution)/shard_map/all_to_all | solution.py:415
  265.7 13.1 %all-to-all-start.7 = ((bf16[4,64,768]{2,1,0:T(8,128)(2,1)}), bf16[4,64,768]{2,1,0:T(8,128)(2,1)S(1)}, u32[]{:S(2)}, u32[]{:S(2)}) async-start(bf16[4,64,768]{2,1,0:T(8,128)(2,1)} %get-tuple-element.33), calls=%async_computation.7 | async-start | bytes 786432 | tf_op jit(solution)/shard_map/all_to_all | solution.py:415
  278.8 32.0 %all-to-all-start.11 = ((bf16[4,64,768]{2,1,0:T(8,128)(2,1)}), bf16[4,64,768]{2,1,0:T(8,128)(2,1)S(1)}, u32[]{:S(2)}, u32[]{:S(2)}) async-start(bf16[4,64,768]{2,1,0:T(8,128)(2,1)} %get-tuple-element.37), calls=%async_computation.11 | async-start | bytes 786432 | tf_op jit(solution)/shard_map/all_to_all | solution.py:415
  310.8 33.4 %all-to-all-start.10 = ((bf16[4,192,768]{2,1,0:T(8,128)(2,1)}), bf16[4,192,768]{2,1,0:T(8,128)(2,1)S(1)}, u32[]{:S(2)}, u32[]{:S(2)}) async-start(bf16[4,192,768]{2,1,0:T(8,128)(2,1)} %attend_back.4), calls=%async_computation.10 | async-start | bytes 2359296 | tf_op jit(solution)/shard_map/all_to_all | solution.py:415
  344.2 33.7 %all-to-all-start.8 = ((bf16[4,192,768]{2,1,0:T(8,128)(2,1)}), bf16[4,192,768]{2,1,0:T(8,128)(2,1)S(1)}, u32[]{:S(2)}, u32[]{:S(2)}) async-start(bf16[4,192,768]{2,1,0:T(8,128)(2,1)} %attend_back.3), calls=%async_computation.8 | async-start | bytes 2359296 | tf_op jit(solution)/shard_map/all_to_all | solution.py:415
  379.0 30.0 %all-to-all-start.12 = ((bf16[4,192,768]{2,1,0:T(8,128)(2,1)}), bf16[4,192,768]{2,1,0:T(8,128)(2,1)S(1)}, u32[]{:S(2)}, u32[]{:S(2)}) async-start(bf16[4,192,768]{2,1,0:T(8,128)(2,1)} %attend_back.5), calls=%async_computation.12 | async-start | bytes 2359296 | tf_op jit(solution)/shard_map/all_to_all | solution.py:415
  384.2 80.7 %reduce-scatter.10.cloned.1.call-start = ((), (), s32[]{:S(2)}) async-start(), calls=%async_computation.23 | async-start | bytes 3981312
  419.4 102.8 %reduce-scatter.8.cloned.1.call-start = ((), (), s32[]{:S(2)}) async-start(), calls=%async_computation.22 | async-start | bytes 5308416 | tf_op jit(solution)/shard_map/reduce_scatter | solution.py:429
  420.2 165.2 %reduce-scatter.6.cloned.1.call-start = ((), (), s32[]{:S(2)}) async-start(), calls=%async_computation.21 | async-start | bytes 6635520 | tf_op jit(solution)/shard_map/reduce_scatter | solution.py:429
  420.9 248.3 %all-reduce.5.cloned.1.call-start = ((), (), s32[]{:S(2)}) async-start(), calls=%async_computation.24 | async-start | bytes 3833856 | tf_op jit(solution)/shard_map/psum | solution.py:486
  459.9 142.0 %copy-start.32 = (f32[768]{0:T(1024)S(1)}, f32[768]{0:T(1024)}, u32[]{:S(2)}) copy-start(f32[768]{0:T(1024)} %get-tuple-element.70) | copy-start | bytes 9220
  (38 other events, 742.2 us)
Sparse Core Ops, SparseCore 0:
  10.5 26.7 all-gather.11
  39.7 24.1 all-gather.13
  66.4 23.9 all-gather.15
  92.1 38.7 all-gather.9
  133.2 43.7 all-gather.7
  419.5 45.3 reduce-scatter.9
  468.4 53.7 reduce-scatter.7
  525.7 59.6 reduce-scatter.5
  588.5 80.6 all-reduce.4

commit v3 on v2

--- a/solution.py
+++ b/solution.py
@@ -355,6 +355,430 @@
     )(tokens, cot, vectors, up_bias.reshape(blocks, 1, width), w_pack, w_down, w_pack, *mixed)
 
 
+MESH = pl.DeviceIdType.MESH
+HIGHEST = lax.Precision.HIGHEST
+
+
+def add_low(a, b):
+    return (a.astype(F32) + b.astype(F32)).astype(BF16)
+
+
+def remote(src, dst, s, r, **where):
+    return pltpu.make_async_remote_copy(
+        src_ref=src, dst_ref=dst, send_sem=s, recv_sem=r, device_id=where, device_id_type=MESH
+    )
+
+
+def each(count, body):
+    lax.fori_loop(0, count, lambda i, _: (body(i), 0)[1], 0)
+
+
+def greet(me, z, fs, nz):
+    barrier = pltpu.get_barrier_semaphore()
+
+    def hello_fsdp(i):
+        peer = {"fsdp": lax.rem(me + 1 + i, fs)}
+        pl.semaphore_signal(barrier, inc=1, device_id=peer, device_id_type=MESH)
+
+    def hello_seq(i):
+        peer = {"seq": lax.rem(z + 1 + i, nz)}
+        pl.semaphore_signal(barrier, inc=1, device_id=peer, device_id_type=MESH)
+
+    each(fs - 1, hello_fsdp)
+    each(nz - 1, hello_seq)
+    pl.semaphore_wait(barrier, fs + nz - 2)
+
+
+def reduce_kernel(fs, nz, slots, counts, lengths, *refs):
+    row_refs, w_refs, refs = refs[:slots], refs[slots : 2 * slots], refs[2 * slots :]
+    attn_in_ref, tokens_hbm, hidden_hbm, vec_in_ref, sums_ref, up_bias_ref, *refs = refs
+    bulk_refs, (mod_t_ref, cond_ref), refs = refs[:2], refs[2:4], refs[4:]
+    inputs_out, qkv_out, pack_out, down_out, total_out, mod_w_out, cond_out = refs[:7]
+    (
+        w_buf,
+        tokens_buf,
+        hidden_buf,
+        g_buf,
+        pair_buf,
+        sum_buf,
+        recv_buf,
+        own_buf,
+        up_pack,
+        up_down,
+        up_qkv,
+        part_pack,
+        part_down,
+        part_qkv,
+        twin_pack,
+        twin_down,
+        twin_qkv,
+        tot_pack,
+        tot_down,
+        tot_qkv,
+        vec_buf,
+        vec_z,
+        vec_own,
+        vec_all,
+        cond_send,
+        cond_recv,
+        local_s,
+        pair_s,
+        pair_r,
+        peer_s,
+        peer_r,
+        up_s,
+        up_r,
+        twin_s,
+        twin_r,
+        tot_s,
+        tot_r,
+        vecz_s,
+        vecz_r,
+        vec_s,
+        vec_r,
+        cond_s,
+        cond_r,
+    ) = refs[7:]
+    me = lax.axis_index("fsdp")
+    z = lax.axis_index("seq")
+    pairs = fs // 2
+    k, c = me // 2, lax.rem(me, 2)
+    partner = me + 1 - 2 * c
+    inner = jnp.logical_or(z == nz // 2 - 1, z == nz // 2)
+    outer = jnp.logical_not(inner)
+    twin = nz - 1 - z
+    mate = z + 1 - 2 * lax.rem(z, 2)
+    tok, width = tokens_buf.shape
+    shard = g_buf.shape[3]
+    groups = width // 128
+
+    loads = [pltpu.make_async_copy(w_refs[s], w_buf.at[s], local_s.at[s]) for s in range(slots)]
+    loads.append(pltpu.make_async_copy(tokens_hbm, tokens_buf, local_s.at[slots]))
+    loads.append(pltpu.make_async_copy(hidden_hbm, hidden_buf, local_s.at[slots + 1]))
+    for load in loads:
+        load.start()
+    greet(me, z, fs, nz)
+
+    bulk = [
+        (src, up, part, other, tot, i)
+        for src, up, part, other, tot, count in (
+            (bulk_refs[0], up_pack, part_pack, twin_pack, tot_pack, counts[0]),
+            (bulk_refs[1], up_down, part_down, twin_down, tot_down, counts[1]),
+        )
+        for i in range(count)
+    ]
+    last = [(own_buf, up_qkv, part_qkv, twin_qkv, tot_qkv, s) for s in range(slots)]
+    chain = list(enumerate(bulk + last))
+    early, late = chain[: len(bulk)], chain[len(bulk) :]
+
+    def up_copy(n, item):
+        src, up, _, _, _, i = item
+        return remote(src.at[i], up.at[i], up_s.at[n], up_r.at[n], seq=mate)
+
+    def twin_copy(n, item):
+        _, _, part, other, _, i = item
+        return remote(part.at[i], other.at[i], twin_s.at[n], twin_r.at[n], seq=twin)
+
+    def tot_copy(n, item):
+        tot, i = item[4], item[5]
+        return remote(tot.at[i], tot.at[i], tot_s.at[n], tot_r.at[n], seq=mate)
+
+    def chain_in(n, item):
+        src, up, part, _, _, i = item
+        up_copy(n, item).wait_recv()
+        part[i] = add_low(src[i], up[i])
+        twin_copy(n, item).start()
+
+    def chain_out(n, item):
+        _, _, part, other, tot, i = item
+        twin_copy(n, item).wait_recv()
+        tot[i] = add_low(part[i], other[i])
+        tot_copy(n, item).start()
+
+    def plan(items):
+        steps = [(chain_in, items[0])]
+        for before, item in zip(items[:-1], items[1:]):
+            steps += [(chain_in, item), (chain_out, before)]
+        return steps + [(chain_out, items[-1])]
+
+    steps = plan(early)
+
+    def advance(count):
+        todo = [steps.pop(0) for _ in range(min(count, len(steps)))]
+        if todo:
+
+            @pl.when(inner)
+            def _():
+                for step, (n, item) in todo:
+                    step(n, item)
+
+    half = len(early) // 2
+
+    @pl.when(outer)
+    def _():
+        for n, item in early[:half]:
+            up_copy(n, item).start()
+
+    def pair_copy(s, j):
+        return remote(g_buf.at[s, j, 1 - c], pair_buf.at[s, j], pair_s.at[s, j], pair_r.at[s, j], fsdp=partner)
+
+    def peer_copy(s, j):
+        return remote(sum_buf.at[s, j], recv_buf.at[s, k], peer_s.at[s, j], peer_r.at[s, k], fsdp=2 * j + c)
+
+    def peer_arrival(s, j):
+        return remote(sum_buf.at[s, j], recv_buf.at[s, j], peer_s.at[s, j], peer_r.at[s, j], fsdp=2 * j + c)
+
+    for s in range(slots):
+        grad = mm(attn_in_ref[...], row_refs[s][...], 0, 1).astype(BF16)
+        for i in range(fs):
+            g_buf[s, i // 2, i % 2] = grad[i * shard : (i + 1) * shard]
+        each(pairs, lambda i: pair_copy(s, lax.rem(k + 1 + i, pairs)).start())
+
+    advance(1)
+
+    def forward(i):
+        j = lax.rem(k + 1 + i, pairs)
+        for s in range(slots):
+            pair_copy(s, j).wait_recv()
+            sum_buf[s, j] = add_low(g_buf[s, j, c], pair_buf[s, j])
+            peer_copy(s, j).start()
+
+    each(pairs - 1, forward)
+    for load in loads:
+        load.wait()
+
+    scale_mlp, gate_mlp, mlp_gain = (vec_in_ref[i : i + 1, :] for i in (2, 3, 4))
+    attn_gain, scale_attn = (vec_in_ref[i : i + 1, :] for i in (6, 7))
+    piece = min(256, tok)
+    back_sum = hat_sum = jnp.zeros((1, width), F32)
+    for i in range(tok // piece):
+        rows = slice(i * piece, (i + 1) * piece)
+        grad = None
+        for s in range(slots):
+            part = mm(row_refs[s][:, rows], w_buf[s], 0, 1)
+            grad = part if grad is None else grad + part
+        hat, inv = normalize(tokens_buf[rows, :])
+        scaled = grad * ((1.0 + scale_attn) * attn_gain)
+        inputs_out[rows, :] = hidden_buf[rows, :] + norm_back(scaled, hat, inv)
+        back_sum = back_sum + jnp.sum(grad, axis=0, keepdims=True)
+        hat_sum = hat_sum + jnp.sum(grad * hat, axis=0, keepdims=True)
+        advance(2)
+
+    sums = [sums_ref[i : i + 1, :] for i in range(5)]
+    vectors = [back_sum, hat_sum * attn_gain, sums[0], sums[1], sums[2] * mlp_gain, sums[3]]
+    vectors += [hat_sum * (1.0 + scale_attn), sums[2] * (1.0 + scale_mlp)]
+    vectors += [up_bias_ref[i] for i in range(up_bias_ref.shape[0])]
+    vectors.append(sums[4] * gate_mlp)
+    for p, v in enumerate(vectors):
+        for i in range(groups):
+            vec_buf[p * groups + i : p * groups + i + 1, :] = v[:, i * 128 : (i + 1) * 128]
+    used = len(vectors) * groups
+    vec_buf[used:, :] = jnp.zeros((vec_buf.shape[0] - used, 128), F32)
+    vec_z[z] = vec_buf[...]
+
+    def vecz_copy(i):
+        return remote(vec_buf, vec_z.at[z], vecz_s.at[i], vecz_r.at[z], seq=lax.rem(z + 1 + i, nz))
+
+    def vecz_arrival(i):
+        peer = lax.rem(z + 1 + i, nz)
+        return remote(vec_buf, vec_z.at[peer], vecz_s.at[i], vecz_r.at[peer], seq=peer)
+
+    each(nz - 1, lambda i: vecz_copy(i).start())
+
+    @pl.when(outer)
+    def _():
+        for n, item in early[half:]:
+            up_copy(n, item).start()
+
+    advance(2)
+    each(nz - 1, lambda i: vecz_arrival(i).wait_recv())
+    summed = vec_z[0]
+    for i in range(1, nz):
+        summed = summed + vec_z[i]
+    vec_own[...] = summed
+    vec_all[me] = summed
+
+    def vec_copy(i):
+        return remote(vec_own, vec_all.at[me], vec_s.at[i], vec_r.at[me], fsdp=lax.rem(me + 1 + i, fs))
+
+    def vec_arrival(i):
+        peer = lax.rem(me + 1 + i, fs)
+        return remote(vec_own, vec_all.at[peer], vec_s.at[i], vec_r.at[peer], fsdp=peer)
+
+    each(fs - 1, lambda i: vec_copy(i).start())
+    advance(len(steps))
+
+    for s in range(slots):
+        pair_copy(s, k).wait_recv()
+        own = g_buf[s, k, c].astype(F32) + pair_buf[s, k].astype(F32)
+
+        def gather_in(i, acc):
+            j = lax.rem(k + 1 + i, pairs)
+            peer_arrival(s, j).wait_recv()
+            return acc + recv_buf[s, j].astype(F32)
+
+        own_buf[s] = lax.fori_loop(0, pairs - 1, gather_in, own).astype(BF16)
+
+        @pl.when(outer)
+        def _():
+            up_copy(*late[s]).start()
+
+    each(fs - 1, lambda i: vec_arrival(i).wait_recv())
+    lane_from = lax.broadcasted_iota(jnp.int32, (256, 128), 0)
+    lane_to = lax.broadcasted_iota(jnp.int32, (256, 128), 1)
+    part, first, place = None, 0, 0
+    for which, length in enumerate(lengths):
+        block = length // fs
+        for i in range(-(-block // 128)):
+            offset = me * block + 128 * i
+            row = first + offset // 128
+            select = (lane_from == lane_to + lax.rem(offset, 128)).astype(F32)
+            both = jnp.concatenate([vec_all[:, pl.ds(row, 1), :][:, 0], vec_all[:, pl.ds(row + 1, 1), :][:, 0]], axis=1)
+            rows = lax.dot_general(
+                both, select, (((1,), (0,)), ((), ())), precision=HIGHEST, preferred_element_type=F32
+            )
+            total_out[place : place + 1, :] = jnp.sum(rows, axis=0, keepdims=True)
+            place += 1
+            if which > 0:
+                continue
+            share = lax.dot_general(
+                rows, mod_t_ref[i], (((1,), (0,)), ((), ())), precision=HIGHEST, preferred_element_type=F32
+            )
+            part = share if part is None else part + share
+            outer_product = lax.dot_general(
+                cond_ref[...], rows, (((0,), (0,)), ((), ())), precision=HIGHEST, preferred_element_type=F32
+            )
+            wide = min(128, block - i * 128)
+            mod_w_out[:, i * 128 : i * 128 + wide] = outer_product[:, :wide]
+        first += length // 128
+    cond_send[...] = jnp.broadcast_to(part[:, None, :], cond_send.shape)
+
+    def cond_copy(i):
+        peer = lax.rem(me + 1 + i, fs)
+        return remote(cond_send.at[peer], cond_recv.at[me], cond_s.at[i], cond_r.at[me], fsdp=peer)
+
+    def cond_arrival(i):
+        peer = lax.rem(me + 1 + i, fs)
+        return remote(cond_send.at[peer], cond_recv.at[peer], cond_s.at[i], cond_r.at[peer], fsdp=peer)
+
+    each(fs - 1, lambda i: cond_copy(i).start())
+    steps.extend(plan(late))
+    advance(len(steps))
+    cond_recv[me] = cond_send[me]
+    each(fs - 1, lambda i: cond_arrival(i).wait_recv())
+    cond_out[...] = jnp.sum(cond_recv[...], axis=0)
+
+    @pl.when(outer)
+    def _():
+        for n, item in chain:
+            tot_copy(n, item).wait_recv()
+            up_copy(n, item).wait_send()
+
+    pack_out[...] = tot_pack[...]
+    down_out[...] = tot_down[...]
+    qkv_out[...] = tot_qkv[...]
+
+    @pl.when(inner)
+    def _():
+        for n, item in chain:
+            twin_copy(n, item).wait_send()
+            tot_copy(n, item).wait_send()
+
+    def drain_peers(i):
+        vec_copy(i).wait_send()
+        cond_copy(i).wait_send()
+
+    def drain_pairs(i):
+        for s in range(slots):
+            pair_copy(s, i).wait_send()
+
+    def drain_sums(i):
+        for s in range(slots):
+            peer_copy(s, lax.rem(k + 1 + i, pairs)).wait_send()
+
+    each(fs - 1, drain_peers)
+    each(pairs, drain_pairs)
+    each(pairs - 1, drain_sums)
+    each(nz - 1, lambda i: vecz_copy(i).wait_send())
+
+
+def reduce_all(
+    grad_rows, weights, attn_in, tokens, grad_hidden, vectors, sums, up_bias_sum, part_pack, part_down, mod_t, cond, mod_cols, fs, nz
+):
+    slots = len(grad_rows)
+    tok, width = tokens.shape
+    shard = width // fs
+    count = lambda a: 3 if a.shape[0] % 48 == 0 else 1
+    counts = (count(part_pack), count(part_down))
+    split = lambda a, n: a.reshape(n, a.shape[0] // n, a.shape[1])
+    pack, down = split(part_pack, counts[0]), split(part_down, counts[1])
+    pairs = fs // 2
+    items = sum(counts) + slots
+    ff = up_bias_sum.size
+    lengths = (6 * width, width, width, ff, width)
+    rows = sum(lengths) // 128 + 2
+    places = sum(-(-v // fs // 128) for v in lengths)
+    vmem = pl.BlockSpec(memory_space=pltpu.VMEM)
+    hbm = pl.BlockSpec(memory_space=pl.ANY)
+    low = lambda *shape: pltpu.VMEM(shape, BF16)
+    wide = lambda *shape: pltpu.VMEM(shape, F32)
+    dma = lambda *shape: pltpu.SemaphoreType.DMA(shape)
+    qkv_shape = (slots, shard, width)
+    triple = [low(*pack.shape), low(*down.shape), low(*qkv_shape)]
+    cols = grad_rows[0].shape[0]
+    inputs_grad, qkv_sum, pack_sum, down_sum, total, mod_w, cond_grad = pl.pallas_call(
+        partial(reduce_kernel, fs, nz, slots, counts, lengths),
+        in_specs=[vmem] * slots + [hbm] * slots + [vmem, hbm, hbm] + [vmem] * 7,
+        out_specs=[vmem] * 7,
+        out_shape=[
+            jax.ShapeDtypeStruct((tok, width), F32),
+            jax.ShapeDtypeStruct(qkv_shape, BF16),
+            jax.ShapeDtypeStruct(pack.shape, BF16),
+            jax.ShapeDtypeStruct(down.shape, BF16),
+            jax.ShapeDtypeStruct((places, 128), F32),
+            jax.ShapeDtypeStruct((cond.shape[1], mod_cols), F32),
+            jax.ShapeDtypeStruct((8, 128), F32),
+        ],
+        scratch_shapes=[
+            low(slots, width, cols),
+            wide(tok, width),
+            wide(tok, width),
+            low(slots, pairs, 2, shard, width),
+            low(slots, pairs, shard, width),
+            low(slots, pairs, shard, width),
+            low(slots, pairs, shard, width),
+            low(*qkv_shape),
+        ]
+        + triple * 4
+        + [
+            wide(rows, 128),
+            wide(nz, rows, 128),
+            wide(rows, 128),
+            wide(fs, rows, 128),
+            wide(fs, 8, 128),
+            wide(fs, 8, 128),
+            dma(slots + 2),
+            dma(slots, pairs),
+            dma(slots, pairs),
+            dma(slots, pairs),
+            dma(slots, pairs),
+        ]
+        + [dma(items)] * 6
+        + [dma(nz - 1), dma(nz), dma(fs - 1), dma(fs), dma(fs - 1), dma(fs)],
+        compiler_params=pltpu.CompilerParams(vmem_limit_bytes=VMEM_LIMIT, collective_id=1, has_side_effects=True),
+        cost_estimate=pl.CostEstimate(flops=12 * tok * width * cols, bytes_accessed=10**8, transcendentals=0),
+        name="reduce_all",
+    )(*grad_rows, *weights, attn_in, tokens, grad_hidden, vectors, sums, up_bias_sum, pack, down, mod_t, cond)
+    blocks, place = [], 0
+    for v in lengths:
+        n = -(-v // fs // 128)
+        blocks.append(total[place : place + n].reshape(-1)[: v // fs])
+        place += n
+    return (
+        inputs_grad, qkv_sum, pack_sum.reshape(part_pack.shape), down_sum.reshape(part_down.shape), blocks, mod_w, cond_grad
+    )
+
+
 def per_device(
     inputs,
     conditioning,
@@ -421,74 +845,50 @@
         log_totals.append(lse)
         mixed_back.append(swap(o))
     vectors = jnp.stack(
-        [gate_attn, shift_mlp, scale_mlp, gate_mlp, mlp_gain_full, down_bias_full, gate_mlp, gate_mlp], axis=0
+        [gate_attn, shift_mlp, scale_mlp, gate_mlp, mlp_gain_full, down_bias_full, attn_gain_full, scale_attn], axis=0
     )
     output, grad_hidden, sums, up_bias_sum, g_down, g_pack, *grad_mixed = middle(
         tokens, cotangent[0], vectors, up_bias_full, w_pack, down_full, mixed_back
     )
     scatter = lambda a: lax.psum_scatter(a, "fsdp", scatter_dimension=0, tiled=True)
+    part_down = scatter(g_down)
     part_pack = scatter(g_pack)
-    part_down = scatter(g_down)
 
     grad_slots = []
     for s in range(slots):
         g = swap(grad_mixed[s])
+        if s == 1:
+            g, part_down = lax.optimization_barrier((g, part_down))
         grad_slots.append(swap(attend_back(heads[s], g, mixed_heads[s], log_totals[s], cos_all, sin_all)))
-
-    qkv_parts = []
-    grad_attn_in = None
-    for s in range(slots):
-        rows = grad_slots[s].reshape(n * 3 * HD, tok)
-        qkv_parts.append(mm(attn_in, rows, 0, 1).astype(BF16))
-        part = mm(rows, qkv_slots[s], 0, 1)
-        grad_attn_in = part if grad_attn_in is None else grad_attn_in + part
-    grad_normed_attn = grad_attn_in * (1.0 + scale_attn)
-    inputs_grad = grad_hidden + norm_back(grad_normed_attn * attn_gain_full, hat_attn, inv_attn)
-
-    part_qkv = scatter(jnp.concatenate(qkv_parts, axis=1))
-    back_sum = jnp.sum(grad_attn_in, axis=0)
-    hat_sum = jnp.sum(grad_attn_in * hat_attn, axis=0)
-    vectors = jnp.concatenate(
-        [
-            back_sum,
-            hat_sum * attn_gain_full,
-            sums[0],
-            sums[1],
-            sums[2] * mlp_gain_full,
-            sums[3],
-            hat_sum * (1.0 + scale_attn),
-            sums[2] * (1.0 + scale_mlp),
-            up_bias_sum.reshape(-1),
-            sums[4] * gate_mlp,
-        ]
+    grad_slots[-1], part_pack = lax.optimization_barrier((grad_slots[-1], part_pack))
+
+    mod_cols = mod_weight.shape[1]
+    mod_t = jnp.pad(mod_low.T.astype(F32), ((0, -mod_cols % 128), (0, 0))).reshape(-1, 128, mod_weight.shape[0])
+    inputs_grad, qkv_sum, pack_sum, down_sum, blocks, mod_weight_grad, cond_grad = reduce_all(
+        [g.reshape(n * 3 * HD, tok) for g in grad_slots],
+        qkv_slots,
+        attn_in,
+        tokens,
+        grad_hidden,
+        vectors,
+        sums,
+        up_bias_sum,
+        part_pack,
+        part_down,
+        mod_t,
+        cond_low_all.astype(F32),
+        mod_cols,
+        fs,
+        n,
     )
-    summed = lax.all_gather(lax.psum(vectors, "seq"), "fsdp", axis=0)
+    mod_bias_grad, attn_gain_grad, mlp_gain_grad, up_bias_grad, down_bias_grad = blocks
+    _, silu_pull = jax.vjp(jax.nn.silu, conditioning)
+    conditioning_grad = silu_pull(cond_grad[:1])[0]
+    qkv_weight_grad = (
+        qkv_sum.astype(F32).reshape(slots, shard, n, 3, HD).transpose(1, 3, 2, 0, 4).reshape(shard, 3 * width)
+    )
+    pack_sum, down_sum = pack_sum.astype(F32), down_sum.astype(F32)
     ff = up_bias.shape[0] * fs
-    total = jnp.sum(summed, axis=0)
-    own = lambda v: lax.dynamic_index_in_dim(v.reshape(fs, -1), me, 0, keepdims=False)
-    mods = 6 * width
-    attn_gain_grad = own(total[mods : mods + width])
-    mlp_gain_grad = own(total[mods + width : mods + 2 * width])
-    up_bias_grad = own(total[mods + 2 * width : mods + 2 * width + ff])
-    down_bias_grad = own(total[mods + 2 * width + ff :])
-    mod_bias_grad = own(total[:mods])
-    own_mod = lax.dynamic_slice_in_dim(summed[:, :mods], me * (mods // fs), mods // fs, axis=1)
-    mod_weight_grad = lax.dot_general(
-        cond_low_all.astype(F32), own_mod, (((0,), (0,)), ((), ())), precision=lax.Precision.HIGHEST
-    )
-    cond_part = lax.dot_general(
-        own_mod, mod_low.astype(F32), (((1,), (1,)), ((), ())), precision=lax.Precision.HIGHEST
-    )
-    grad_cond_act = lax.psum_scatter(cond_part, "fsdp", scatter_dimension=0, tiled=True)
-    _, silu_pull = jax.vjp(jax.nn.silu, conditioning)
-    conditioning_grad = silu_pull(grad_cond_act)[0]
-
-    qkv_sum = lax.psum(part_qkv, "seq").astype(F32)
-    qkv_weight_grad = (
-        qkv_sum.reshape(shard, slots, n, 3, HD).transpose(0, 3, 2, 1, 4).reshape(shard, 3 * width)
-    )
-    pack_sum = lax.psum(part_pack, "seq").astype(F32)
-    down_sum = lax.psum(part_down, "seq").astype(F32)
     out_sum, up_sum = pack_sum[:, ff:], pack_sum[:, :ff]
     return (
         output[None],

time: 692 us -> 503 us (0.73)
  waiting for transfers between devices: 285 us -> 102 us
  Pallas kernels: 186 us -> 252 us
  blocking collectives: 77.4 us -> 38.9 us
  matrix products: 17.3 us -> 0.22 us
  local copies, waits for them, and re-layouts: 31.2 us -> 19.6 us
    reduce_scatter x2, waiting for transfers between devices: 118 us -> 0.01 us  [per_device(): lax.psum_scatter(a, 'fsdp', scatter_dimension=0, tiled=True)]
    pallas_call x0 -> x1, Pallas kernels: none -> 65.8 us  [reduce_all(): pl.pallas_call(partial(reduce_kernel, fs, nz, slots, counts, lengths), in...]
    psum x1 -> x0, waiting for transfers between devices: 61.6 us -> none  [per_device(): qkv_sum = lax.psum(part_qkv, 'seq').astype(F32)]
    psum x1 -> x0, blocking collectives: 17.4 us -> none  [per_device(): summed = lax.all_gather(lax.psum(vectors, 'seq'), 'fsdp', axis=0)]
    dot_general x7 -> x1, matrix products: 15.2 us -> 0.22 us  [mm(): lax.dot_general(a, b, (((ca,), (cb,)), ((), ())), preferred_element_type=...]
    unnamed x2 -> x1, blocking collectives: 38.3 us -> 25.9 us
    all_gather x1 -> x0, blocking collectives: 8.22 us -> none  [per_device(): summed = lax.all_gather(lax.psum(vectors, 'seq'), 'fsdp', axis=0)]
  transfers between devices with their start and end apart: 21 -> 19, of which waited for: 12 -> 8; matrix products, arithmetic and copies ran while one was open for 7% -> 3% of each run, Pallas kernels for 21% -> 30%
where the time goes in v3:
time: 503 us; the launch traced here: 493 us
  Pallas kernels  252 us (50%)
  waiting for transfers between devices  102 us (20%)
  starting transfers between devices  52.4 us (10%)
  blocking collectives  38.9 us (8%)
  local copies, waits for them, and re-layouts  19.6 us (4%)
  between operations  15.7 us (3%)
  other arithmetic  11.5 us (2%)
    all_to_all x11, waiting for transfers between devices, per_device(): lax.all_to_all(a, 'seq', split_axis=0, concat_axis=0, tiled=True)  96.5 us
    pallas_call x3, Pallas kernels, attend_back(): pl.pallas_call(partial(attend_back_kernel, n, tok, 2), grid=(n,), in_spec...  85.5 us
    pallas_call x1, Pallas kernels, reduce_all(): pl.pallas_call(partial(reduce_kernel, fs, nz, slots, counts, lengths), in...  65.8 us
    pallas_call x3, Pallas kernels, attend(): pl.pallas_call(partial(attend_kernel, n, tok, 2), grid=(n,), in_specs=[pl...  50.2 us
    all_to_all x11, starting transfers between devices, per_device(): lax.all_to_all(a, 'seq', split_axis=0, concat_axis=0, tiled=True)  48.4 us
    pallas_call x1, Pallas kernels, middle(): pl.pallas_call(partial(middle_kernel, n, slots, blocks), grid=(blocks + 1...  39.5 us
    unnamed x1, blocking collectives  25.9 us
    all_to_all x1, blocking collectives, per_device(): lax.all_to_all(a, 'seq', split_axis=0, concat_axis=0, tiled=True)  13 us
  transfers between devices with their start and end apart: 19, of which 8 were waited for; matrix products, arithmetic and copies ran while one was open for 3% of the time, Pallas kernels for 30%

profile of v3, /device:TPU:0, one launch (start us, length us, event | category | flops | bytes accessed | tf_op | source)
XLA Modules:
  0.0 493.3 jit_solution(13119523038281195989)
XLA Ops:
  16.1 25.9 %all-reduce.1 = f32[6400]{0:T(1024)S(1)} all-reduce(f32[6400]{0:T(1024)S(1)} %dynamic-update-slice), channel_id=2, replica_groups=mesh['fsdp'=8,'seq'=4] {'fsdp'}, use_global_device_ids=true, to_apply=%add.1 | all-reduce | flops 6400 | bytes 51200
  56.5 4.9 all-to-all-start.1
  63.8 3.8 project.4
  67.6 22.3 %all-to-all-done.1.x_ref = bf16[4,192,768]{2,1,0:T(8,128)(2,1)S(1)} async-done(((bf16[4,192,768]{2,1,0:T(8,128)(2,1)}), bf16[4,192,768]{2,1,0:T(8,128)(2,1)S(1)}, u32[]{:S(2)}, u32[]{:S(2)}) %all-to-all-start.1) | async-done | bytes 1179680 | tf_op jit(solution)/shard_map/all_to_all | solution.py:839
  93.4 3.8 project.5
  97.2 24.2 %all-to-all-done.3.x_ref = bf16[4,192,768]{2,1,0:T(8,128)(2,1)S(1)} async-done(((bf16[4,192,768]{2,1,0:T(8,128)(2,1)}), bf16[4,192,768]{2,1,0:T(8,128)(2,1)S(1)}, u32[]{:S(2)}, u32[]{:S(2)}) %all-to-all-start.3) | async-done | bytes 1179680 | tf_op jit(solution)/shard_map/all_to_all | solution.py:839
  125.0 16.6 %attend.3 = (bf16[4,64,768]{2,1,0:T(8,128)(2,1)}, f32[4,1,768]{2,1,0:T(1,128)}) custom-call(bf16[4,192,768]{2,1,0:T(8,128)(2,1)} %copy-done.5), custom_call_target="tpu_custom_call" | custom-call | flops 9663676416 | bytes 1572864 | tf_op jit(solution)/shard_map/attend/pallas_call | solution.py:111
  141.6 11.4 %all-to-all-done.5.x_ref = bf16[4,192,768]{2,1,0:T(8,128)(2,1)S(1)} async-done(((bf16[4,192,768]{2,1,0:T(8,128)(2,1)}), bf16[4,192,768]{2,1,0:T(8,128)(2,1)S(1)}, u32[]{:S(2)}, u32[]{:S(2)}) %all-to-all-start.5) | async-done | bytes 1179680 | tf_op jit(solution)/shard_map/all_to_all | solution.py:839
  156.7 17.0 %attend.4 = (bf16[4,64,768]{2,1,0:T(8,128)(2,1)}, f32[4,1,768]{2,1,0:T(1,128)}) custom-call(bf16[4,192,768]{2,1,0:T(8,128)(2,1)} %copy-done.4), custom_call_target="tpu_custom_call" | custom-call | flops 9663676416 | bytes 1572864 | tf_op jit(solution)/shard_map/attend/pallas_call | solution.py:111
  173.7 5.1 %all-to-all-start.4 = ((bf16[4,64,768]{2,1,0:T(8,128)(2,1)}), bf16[4,64,768]{2,1,0:T(8,128)(2,1)S(1)}, u32[]{:S(2)}, u32[]{:S(2)}) async-start(bf16[4,64,768]{2,1,0:T(8,128)(2,1)} %get-tuple-element.40.o_ref), calls=%async_computation.4 | async-start | bytes 786432 | tf_op jit(solution)/shard_map/all_to_all | solution.py:839
  178.8 16.6 %attend.5 = (bf16[4,64,768]{2,1,0:T(8,128)(2,1)}, f32[4,1,768]{2,1,0:T(1,128)}) custom-call(bf16[4,192,768]{2,1,0:T(8,128)(2,1)} %copy-done.6), custom_call_target="tpu_custom_call" | custom-call | flops 9663676416 | bytes 1572864 | tf_op jit(solution)/shard_map/attend/pallas_call | solution.py:111
  195.4 5.1 %all-to-all-start.6 = ((bf16[4,64,768]{2,1,0:T(8,128)(2,1)}), bf16[4,64,768]{2,1,0:T(8,128)(2,1)S(1)}, u32[]{:S(2)}, u32[]{:S(2)}) async-start(bf16[4,64,768]{2,1,0:T(8,128)(2,1)} %get-tuple-element.41.o_ref), calls=%async_computation.6 | async-start | bytes 786432 | tf_op jit(solution)/shard_map/all_to_all | solution.py:839
  202.5 7.7 %all-to-all-done.6.refs_2_ = bf16[4,64,768]{2,1,0:T(8,128)(2,1)S(1)} async-done(((bf16[4,64,768]{2,1,0:T(8,128)(2,1)}), bf16[4,64,768]{2,1,0:T(8,128)(2,1)S(1)}, u32[]{:S(2)}, u32[]{:S(2)}) %all-to-all-start.6) | async-done | bytes 393248 | tf_op jit(solution)/shard_map/all_to_all | solution.py:839
  211.0 39.5 %middle.1 = (f32[768,768]{1,0:T(8,128)}, f32[768,768]{1,0:T(8,128)}, f32[8,768]{1,0:T(8,128)}, f32[4,1,768]{2,1,0:T(1,128)}, bf16[3072,768]{1,0:T(8,128)(2,1)}, ...) custom-call(f32[768,768]{1,0:T(8,128)} %bitcast.60, ...), custom_call_target="tpu_custom_call" | custom-call | flops 24461180928 | bytes 28311552 | tf_op jit(solution)/shard_map/middle/pallas_call | solution.py:314
  251.5 13.0 %all_to_all.69.g_ref = bf16[4,64,768]{2,1,0:T(8,128)(2,1)} all-to-all(bf16[4,64,768]{2,1,0:T(8,128)(2,1)S(1)} %copy-done.18), channel_id=1, replica_groups=mesh['fsdp'=8,'seq'=4] {'seq'}, dimensions={0} | all-to-all | bytes 786432 | tf_op jit(solution)/shard_map/all_to_all | solution.py:839
  271.1 7.1 %all-to-all-done.9.g_ref = bf16[4,64,768]{2,1,0:T(8,128)(2,1)S(1)} async-done(((bf16[4,64,768]{2,1,0:T(8,128)(2,1)}), bf16[4,64,768]{2,1,0:T(8,128)(2,1)S(1)}, u32[]{:S(2)}, u32[]{:S(2)}) %all-to-all-start.9) | async-done | bytes 393248 | tf_op jit(solution)/shard_map/all_to_all | solution.py:839
  281.9 28.3 %attend_back.5 = bf16[4,192,768]{2,1,0:T(8,128)(2,1)} custom-call(bf16[4,192,768]{2,1,0:T(8,128)(2,1)} %copy-done.6, bf16[4,64,768]{2,1,0:T(8,128)(2,1)} %all_to_all.69.g_ref, bf16[4,64,768]{2,1,0:T(8,128)(2,1)} %get-tuple-element.41.o_ref, f32[4,1,768]{2,1,0:T(1,128)} %get-tuple-element.50.lse_ref, f32[4,32,768]{2,1,0:T(8,128)} %get-tuple-element.120.cos_ref, ...), custom_call_target="tpu_custom_call" | custom-call | flops 24159191040 | bytes 3145728 | tf_op jit(solution)/shard_map/attend_back/pallas_call | solution.py:189
  310.2 5.1 %all-to-all-start.12 = ((bf16[4,192,768]{2,1,0:T(8,128)(2,1)}), bf16[4,192,768]{2,1,0:T(8,128)(2,1)S(1)}, u32[]{:S(2)}, u32[]{:S(2)}) async-start(bf16[4,192,768]{2,1,0:T(8,128)(2,1)} %attend_back.5), calls=%async_computation.13 | async-start | bytes 2359296 | tf_op jit(solution)/shard_map/all_to_all | solution.py:839
  315.3 28.8 %attend_back.3 = bf16[4,192,768]{2,1,0:T(8,128)(2,1)} custom-call(bf16[4,192,768]{2,1,0:T(8,128)(2,1)} %copy-done.5, bf16[4,64,768]{2,1,0:T(8,128)(2,1)} %copy-done.17, bf16[4,64,768]{2,1,0:T(8,128)(2,1)} %get-tuple-element.39.o_ref, f32[4,1,768]{2,1,0:T(1,128)} %get-tuple-element.44.lse_ref, f32[4,32,768]{2,1,0:T(8,128)} %get-tuple-element.120.cos_ref, ...), custom_call_target="tpu_custom_call" | custom-call | flops 24159191040 | bytes 3145728 | tf_op jit(solution)/shard_map/attend_back/pallas_call | solution.py:189
  344.1 5.3 %all-to-all-start.8 = ((bf16[4,192,768]{2,1,0:T(8,128)(2,1)}), bf16[4,192,768]{2,1,0:T(8,128)(2,1)S(1)}, u32[]{:S(2)}, u32[]{:S(2)}) async-start(bf16[4,192,768]{2,1,0:T(8,128)(2,1)} %attend_back.3), calls=%async_computation.8 | async-start | bytes 2359296 | tf_op jit(solution)/shard_map/all_to_all | solution.py:839
  349.4 28.3 %attend_back.4 = bf16[4,192,768]{2,1,0:T(8,128)(2,1)} custom-call(bf16[4,192,768]{2,1,0:T(8,128)(2,1)} %copy-done.4, bf16[4,64,768]{2,1,0:T(8,128)(2,1)} %copy-done.15, bf16[4,64,768]{2,1,0:T(8,128)(2,1)} %get-tuple-element.40.o_ref, f32[4,1,768]{2,1,0:T(1,128)} %get-tuple-element.48.lse_ref, f32[4,32,768]{2,1,0:T(8,128)} %get-tuple-element.120.cos_ref, ...), custom_call_target="tpu_custom_call" | custom-call | flops 24159191040 | bytes 3145728 | tf_op jit(solution)/shard_map/attend_back/pallas_call | solution.py:189
  377.8 5.1 %all-to-all-start.10 = ((bf16[4,192,768]{2,1,0:T(8,128)(2,1)}), bf16[4,192,768]{2,1,0:T(8,128)(2,1)S(1)}, u32[]{:S(2)}, u32[]{:S(2)}) async-start(bf16[4,192,768]{2,1,0:T(8,128)(2,1)} %attend_back.4), calls=%async_computation.11 | async-start | bytes 2359296 | tf_op jit(solution)/shard_map/all_to_all | solution.py:839
  384.4 23.7 %all-to-all-done.10 = bf16[4,192,768]{2,1,0:T(8,128)(2,1)S(1)} async-done(((bf16[4,192,768]{2,1,0:T(8,128)(2,1)}), bf16[4,192,768]{2,1,0:T(8,128)(2,1)S(1)}, u32[]{:S(2)}, u32[]{:S(2)}) %all-to-all-start.10) | async-done | bytes 1179680 | tf_op jit(solution)/shard_map/all_to_all | solution.py:839
  409.1 65.8 %reduce_all.1 = (f32[768,768]{1,0:T(8,128)}, bf16[3,96,768]{2,1,0:T(8,128)(2,1)}, bf16[3,32,3840]{2,1,0:T(8,128)(2,1)}, bf16[3,128,768]{2,1,0:T(8,128)(2,1)}, f3...) custom-call(bf16[768,768]{1,0:T(8,128)(2,1)} %bitcast.67, bf16[768,768]{1,0:T(8,128)(2,1)} %bitcast.68, ...), custom_call_target="tpu_custom_call" | custom-call | flops 5435817984 | bytes 100000000 | tf_op jit(solution)/shard_map/reduce_all/pallas_call | solution.py:729
  (156 shorter events, 63.0 us)
Async XLA Ops:
  7.2 45.5 %all-gather.11.cloned.1.call-start = ((), (), s32[]{:S(2)}) async-start(), calls=%async_computation.17 | async-start | bytes 1327104 | tf_op jit(solution)/shard_map/all_gather | solution.py:804
  9.6 54.2 %all-gather.13.cloned.1.call-start = ((), (), s32[]{:S(2)}) async-start(), calls=%async_computation.18 | async-start | bytes 1327104 | tf_op jit(solution)/shard_map/all_gather | solution.py:804
  10.5 82.9 %all-gather.15.cloned.1.call-start = ((), (), s32[]{:S(2)}) async-start(), calls=%async_computation.19 | async-start | bytes 1327104 | tf_op jit(solution)/shard_map/all_gather | solution.py:804
  11.4 198.8 %all-gather.9.cloned.1.call-start = ((), (), s32[]{:S(2)}) async-start(), calls=%async_computation.16 | async-start | bytes 5308416 | tf_op jit(solution)/shard_map/all_gather | solution.py:804
  12.4 197.8 %all-gather.7.cloned.1.call-start = ((), (), s32[]{:S(2)}) async-start(), calls=%async_computation.15 | async-start | bytes 6635520 | tf_op jit(solution)/shard_map/all_gather | solution.py:804
  13.4 28.7 %copy-start.10 = (f32[128,576]{0,1:T(8,128)S(1)}, f32[128,576]{0,1:T(8,128)}, u32[]{:S(2)}) copy-start(f32[128,576]{0,1:T(8,128)} %param.24) | copy-start | bytes 884740
  13.4 28.7 %copy-start.22 = (f32[576]{0:T(1024)S(1)}, f32[576]{0:T(1024)}, u32[]{:S(2)}) copy-start(f32[576]{0:T(1024)} %param.25) | copy-start | bytes 6916
  13.5 32.8 %copy-start = (f32[1,768,768]{2,1,0:T(8,128)S(1)}, f32[1,768,768]{2,1,0:T(8,128)}, u32[]{:S(2)}) copy-start(f32[1,768,768]{2,1,0:T(8,128)} %param.13) | copy-start | bytes 7077892
  42.9 8.1 %all-to-all-start = ((f32[8,1,576]{2,1,0:T(1,128)}), f32[8,1,576]{2,1,0:T(1,128)S(1)}, u32[]{:S(2)}, u32[]{:S(2)}) async-start(f32[8,1,576]{2,1,0:T(1,128)} %copy.44), calls=%async_computation | async-start | bytes 40960 | tf_op jit(solution)/shard_map/all_to_all | solution.py:818
  56.5 33.4 %all-to-all-start.1 = ((bf16[4,192,768]{2,1,0:T(8,128)(2,1)}), bf16[4,192,768]{2,1,0:T(8,128)(2,1)S(1)}, u32[]{:S(2)}, u32[]{:S(2)}) async-start(bf16[4,192,768]{2,1,0:T(8,128)(2,1)} %project.3), calls=%async_computation.1 | async-start | bytes 2359296 | tf_op jit(solution)/shard_map/all_to_all | solution.py:839
  89.9 31.6 %all-to-all-start.3 = ((bf16[4,192,768]{2,1,0:T(8,128)(2,1)}), bf16[4,192,768]{2,1,0:T(8,128)(2,1)S(1)}, u32[]{:S(2)}, u32[]{:S(2)}) async-start(bf16[4,192,768]{2,1,0:T(8,128)(2,1)} %project.4), calls=%async_computation.3 | async-start | bytes 2359296 | tf_op jit(solution)/shard_map/all_to_all | solution.py:839
  121.5 31.6 %all-to-all-start.5 = ((bf16[4,192,768]{2,1,0:T(8,128)(2,1)}), bf16[4,192,768]{2,1,0:T(8,128)(2,1)S(1)}, u32[]{:S(2)}, u32[]{:S(2)}) async-start(bf16[4,192,768]{2,1,0:T(8,128)(2,1)} %project.5), calls=%async_computation.5 | async-start | bytes 2359296 | tf_op jit(solution)/shard_map/all_to_all | solution.py:839
  153.0 20.7 %all-to-all-start.2 = ((bf16[4,64,768]{2,1,0:T(8,128)(2,1)}), bf16[4,64,768]{2,1,0:T(8,128)(2,1)S(1)}, u32[]{:S(2)}, u32[]{:S(2)}) async-start(bf16[4,64,768]{2,1,0:T(8,128)(2,1)} %get-tuple-element.39.o_ref), calls=%async_computation.2 | async-start | bytes 786432 | tf_op jit(solution)/shard_map/all_to_all | solution.py:839
  173.7 21.6 %all-to-all-start.4 = ((bf16[4,64,768]{2,1,0:T(8,128)(2,1)}), bf16[4,64,768]{2,1,0:T(8,128)(2,1)S(1)}, u32[]{:S(2)}, u32[]{:S(2)}) async-start(bf16[4,64,768]{2,1,0:T(8,128)(2,1)} %get-tuple-element.40.o_ref), calls=%async_computation.4 | async-start | bytes 786432 | tf_op jit(solution)/shard_map/all_to_all | solution.py:839
  195.4 14.9 %all-to-all-start.6 = ((bf16[4,64,768]{2,1,0:T(8,128)(2,1)}), bf16[4,64,768]{2,1,0:T(8,128)(2,1)S(1)}, u32[]{:S(2)}, u32[]{:S(2)}) async-start(bf16[4,64,768]{2,1,0:T(8,128)(2,1)} %get-tuple-element.41.o_ref), calls=%async_computation.6 | async-start | bytes 786432 | tf_op jit(solution)/shard_map/all_to_all | solution.py:839
  200.5 143.6 %reduce-scatter.3.cloned.1.call-start = ((), (), s32[]{:S(2)}) async-start(), calls=%async_computation.20 | async-start | bytes 5308416 | tf_op jit(solution)/shard_map/reduce_scatter | solution.py:853
  264.6 13.7 %all-to-all-start.9 = ((bf16[4,64,768]{2,1,0:T(8,128)(2,1)}), bf16[4,64,768]{2,1,0:T(8,128)(2,1)S(1)}, u32[]{:S(2)}, u32[]{:S(2)}) async-start(bf16[4,64,768]{2,1,0:T(8,128)(2,1)} %get-tuple-element.45), calls=%async_computation.9 | async-start | bytes 786432 | tf_op jit(solution)/shard_map/all_to_all | solution.py:839
  268.0 116.3 %reduce-scatter.5.cloned.1.call-start = ((), (), s32[]{:S(2)}) async-start(), calls=%async_computation.21 | async-start | bytes 6635520 | tf_op jit(solution)/shard_map/reduce_scatter | solution.py:853
  278.2 32.0 %copy-start.15 = (bf16[4,64,768]{2,1,0:T(8,128)(2,1)}, bf16[4,64,768]{2,1,0:T(8,128)(2,1)S(1)}, u32[]{:S(2)}) copy-start(bf16[4,64,768]{2,1,0:T(8,128)(2,1)S(1)} %all-to-all-done.9.g_ref) | copy-start | bytes 1179652
  278.2 32.0 %all-to-all-start.7 = ((bf16[4,64,768]{2,1,0:T(8,128)(2,1)}), bf16[4,64,768]{2,1,0:T(8,128)(2,1)S(1)}, u32[]{:S(2)}, u32[]{:S(2)}) async-start(bf16[4,64,768]{2,1,0:T(8,128)(2,1)} %get-tuple-element.43), calls=%async_computation.7 | async-start | bytes 786432 | tf_op jit(solution)/shard_map/all_to_all | solution.py:839
  310.2 33.9 %all-to-all-start.12 = ((bf16[4,192,768]{2,1,0:T(8,128)(2,1)}), bf16[4,192,768]{2,1,0:T(8,128)(2,1)S(1)}, u32[]{:S(2)}, u32[]{:S(2)}) async-start(bf16[4,192,768]{2,1,0:T(8,128)(2,1)} %attend_back.5), calls=%async_computation.13 | async-start | bytes 2359296 | tf_op jit(solution)/shard_map/all_to_all | solution.py:839
  344.1 33.6 %copy-start.7 = (bf16[4,192,768]{2,1,0:T(8,128)(2,1)}, bf16[4,192,768]{2,1,0:T(8,128)(2,1)S(1)}, u32[]{:S(2)}) copy-start(bf16[4,192,768]{2,1,0:T(8,128)(2,1)S(1)} %all-to-all-done.12) | copy-start | bytes 3538948
  344.1 33.6 %all-to-all-start.8 = ((bf16[4,192,768]{2,1,0:T(8,128)(2,1)}), bf16[4,192,768]{2,1,0:T(8,128)(2,1)S(1)}, u32[]{:S(2)}, u32[]{:S(2)}) async-start(bf16[4,192,768]{2,1,0:T(8,128)(2,1)} %attend_back.3), calls=%async_computation.8 | async-start | bytes 2359296 | tf_op jit(solution)/shard_map/all_to_all | solution.py:839
  377.8 30.3 %all-to-all-start.10 = ((bf16[4,192,768]{2,1,0:T(8,128)(2,1)}), bf16[4,192,768]{2,1,0:T(8,128)(2,1)S(1)}, u32[]{:S(2)}, u32[]{:S(2)}) async-start(bf16[4,192,768]{2,1,0:T(8,128)(2,1)} %attend_back.4), calls=%async_computation.11 | async-start | bytes 2359296 | tf_op jit(solution)/shard_map/all_to_all | solution.py:839
  (25 other events, 130.3 us)
Sparse Core Ops, SparseCore 0:
  10.4 26.7 all-gather.10
  39.7 24.0 all-gather.12
  66.2 23.9 all-gather.14
  91.9 38.7 all-gather.8
  133.1 43.7 all-gather.6
  250.7 51.3 reduce-scatter.2
  305.6 59.6 reduce-scatter.4

commit v4 on v3

--- a/solution.py
+++ b/solution.py
@@ -35,33 +35,317 @@
     return inv_std * (grad_hat - mean_grad - normed_hat * mean_mixed)
 
 
-def project_kernel(seq_count, w_ref, x_ref, cos_ref, sin_ref, out_ref):
-    rows = mm(w_ref[...], x_ref[...], 0, 1).astype(BF16)
+MESH = pl.DeviceIdType.MESH
+HIGHEST = lax.Precision.HIGHEST
+
+
+def add_low(a, b):
+    return (a.astype(F32) + b.astype(F32)).astype(BF16)
+
+
+def remote(src, dst, s, r, **where):
+    return pltpu.make_async_remote_copy(
+        src_ref=src, dst_ref=dst, send_sem=s, recv_sem=r, device_id=where, device_id_type=MESH
+    )
+
+
+def each(count, body):
+    lax.fori_loop(0, count, lambda i, _: (body(i), 0)[1], 0)
+
+
+def greet(me, z, fs, nz):
+    barrier = pltpu.get_barrier_semaphore()
+
+    def hello_fsdp(i):
+        peer = {"fsdp": lax.rem(me + 1 + i, fs)}
+        pl.semaphore_signal(barrier, inc=1, device_id=peer, device_id_type=MESH)
+
+    def hello_seq(i):
+        peer = {"seq": lax.rem(z + 1 + i, nz)}
+        pl.semaphore_signal(barrier, inc=1, device_id=peer, device_id_type=MESH)
+
+    each(fs - 1, hello_fsdp)
+    each(nz - 1, hello_seq)
+    pl.semaphore_wait(barrier, fs + nz - 2)
+
+
+def start_kernel(fs, nz, slots, *refs):
+    (
+        qkv_ref,
+        tokens_hbm,
+        attn_gain_ref,
+        mlp_gain_ref,
+        up_bias_ref,
+        down_bias_ref,
+        cond_ref,
+        mod_w_ref,
+        mod_b_ref,
+        cos_ref,
+        sin_ref,
+    ) = refs[:11]
+    refs = refs[11:]
+    heads_ref, rest_refs, refs = refs[0], refs[1:slots], refs[slots:]
+    w_ref, attn_in_ref, vec_ref, bias_ref, cond_out = refs[:5]
+    (
+        tokens_buf,
+        w_own,
+        z_send,
+        narrow,
+        spread,
+        mod_wide,
+        small_send,
+        small_all,
+        mod_send,
+        mod_recv,
+        w_full,
+        local_s,
+        small_s,
+        small_r,
+        mod_s,
+        mod_r,
+        w_s,
+        w_f,
+        w_r,
+        z_s,
+        z_r,
+    ) = refs[5:]
+    me = lax.axis_index("fsdp")
+    z = lax.axis_index("seq")
+    pairs = fs // 2
+    k, c = me // 2, lax.rem(me, 2)
+    partner = me + 1 - 2 * c
+    tok, width = tokens_buf.shape
+    shard = w_own.shape[1]
+    ff = spread.shape[1]
+    block = nz * HD
+
+    load = pltpu.make_async_copy(tokens_hbm, tokens_buf, local_s)
+    load.start()
+    greet(me, z, fs, nz)
+
+    narrow[...] = jnp.zeros_like(narrow)
+    for i, piece in enumerate((attn_gain_ref, mlp_gain_ref, down_bias_ref)):
+        narrow[i : i + 1, :shard] = piece[...]
+    spread[...] = jnp.zeros_like(spread)
+    spread[0:1, : up_bias_ref.shape[1]] = up_bias_ref[...]
+    placed = pltpu.roll(narrow[...], me * shard, 1)
+    for i in range(3):
+        small_send[:, i * width : (i + 1) * width] = placed[i : i + 1]
+    placed = pltpu.roll(spread[...], me * up_bias_ref.shape[1], 1)
+    small_send[:, 3 * width : 3 * width + ff] = placed[0:1]
+    small_send[:, 3 * width + ff :] = cond_ref[...]
+    small_all[me] = small_send[...]
+
+    def small_copy(i):
+        return remote(small_send, small_all.at[me], small_s.at[i], small_r.at[me], fsdp=lax.rem(me + 1 + i, fs))
+
+    def small_arrival(i):
+        peer = lax.rem(me + 1 + i, fs)
+        return remote(small_send, small_all.at[peer], small_s.at[i], small_r.at[peer], fsdp=peer)
+
+    each(fs - 1, lambda i: small_copy(i).start())
+
+    for s in range(slots):
+        for part in range(3):
+            columns = slice(part * width + s * block, part * width + (s + 1) * block)
+            w_own[s, :, part * block : (part + 1) * block] = qkv_ref[:, columns].astype(BF16)
+        w_ref[s, me] = w_own[s]
+
+    def w_peer(s, i):
+        j = lax.rem(k + 1 + i, pairs)
+        return remote(w_own.at[s], w_ref.at[s, me], w_s.at[s, i], w_r.at[s, me], fsdp=2 * j + c)
+
+    def w_partner(s):
+        return remote(w_own.at[s], w_ref.at[s, me], w_s.at[s, pairs - 1], w_r.at[s, me], fsdp=partner)
+
+    def w_arrival(s, j):
+        return remote(w_own.at[s], w_ref.at[s, j], w_s.at[s, 0], w_r.at[s, j], fsdp=partner)
+
+    def w_pass(s, i):
+        j = 2 * lax.rem(k + 1 + i, pairs) + c
+        return remote(w_ref.at[s, j], w_ref.at[s, j], w_f.at[s, i], w_r.at[s, j], fsdp=partner)
+
+    def send_weight(s):
+        each(pairs - 1, lambda i: w_peer(s, i).start())
+        w_partner(s).start()
+
+    def pass_weight(s):
+        def step(i):
+            w_arrival(s, 2 * lax.rem(k + 1 + i, pairs) + c).wait_recv()
+            w_pass(s, i).start()
+
+        each(pairs - 1, step)
+
+    send_weight(0)
+    for s in range(1, slots - 1):
+        send_weight(s)
+
+    each(fs - 1, lambda i: small_arrival(i).wait_recv())
+    small_sum = jnp.sum(small_all[:, :, : 3 * width + ff], axis=0)
+    cond_all = small_all[:, 0, 3 * width + ff :]
+    cond_low = (cond_all / (1.0 + jnp.exp(-cond_all))).astype(BF16)
+    cond_out[...] = cond_low.astype(F32)
+    own_mod = mm(cond_low, mod_w_ref[...].astype(BF16), 1, 0) + mod_b_ref[...]
+    mod_wide[...] = jnp.zeros_like(mod_wide)
+    mod_wide[:, : own_mod.shape[1]] = own_mod
+    placed = pltpu.roll(mod_wide[...], me * own_mod.shape[1], 1)
+    for i in range(fs):
+        mod_send[i] = placed[i : i + 1]
+    mod_recv[me] = mod_send[me]
+
+    def mod_copy(i):
+        peer = lax.rem(me + 1 + i, fs)
+        return remote(mod_send.at[peer], mod_recv.at[me], mod_s.at[i], mod_r.at[me], fsdp=peer)
+
+    def mod_arrival(i):
+        peer = lax.rem(me + 1 + i, fs)
+        return remote(mod_send.at[peer], mod_recv.at[peer], mod_s.at[i], mod_r.at[peer], fsdp=peer)
+
+    each(fs - 1, lambda i: mod_copy(i).start())
+    send_weight(slots - 1)
+    pass_weight(0)
+
+    attn_gain, mlp_gain, down_bias = (small_sum[:, i * width : (i + 1) * width] for i in range(3))
+    for i in range(ff // width):
+        bias_ref[i] = small_sum[:, (3 + i) * width : (4 + i) * width]
+    load.wait()
+    piece = min(256, tok)
+    each(fs - 1, lambda i: mod_arrival(i).wait_recv())
+    modulation = jnp.sum(mod_recv[...], axis=0)
+    shift_attn, scale_attn, gate_attn, shift_mlp, scale_mlp, gate_mlp = (
+        modulation[:, i * width : (i + 1) * width] for i in range(6)
+    )
+    kept = (gate_attn, shift_mlp, scale_mlp, gate_mlp, mlp_gain, down_bias, attn_gain, scale_attn)
+    for i, v in enumerate(kept):
+        vec_ref[i : i + 1, :] = v
+    for i in range(tok // piece):
+        rows = slice(i * piece, (i + 1) * piece)
+        hat, _ = normalize(tokens_buf[rows, :])
+        attn_in_ref[rows, :] = (hat * attn_gain * (1.0 + scale_attn) + shift_attn).astype(BF16)
+
     cosine, sine = cos_ref[...], sin_ref[...]
     half = HD // 2
-    for z in range(seq_count):
-        for part in range(3):
-            base = (z * 3 + part) * HD
-            if part == 2:
-                out_ref[z, part * HD : (part + 1) * HD, :] = rows[base : base + HD]
-            else:
-                a = rows[base : base + half].astype(F32)
-                b = rows[base + half : base + HD].astype(F32)
-                out_ref[z, part * HD : part * HD + half, :] = (a * cosine - b * sine).astype(BF16)
-                out_ref[z, part * HD + half : (part + 1) * HD, :] = (b * cosine + a * sine).astype(BF16)
-
-
-def project(weight, attn_in, cosine, sine, seq_count):
-    tok = attn_in.shape[0]
-    return pl.pallas_call(
-        partial(project_kernel, seq_count),
-        out_shape=jax.ShapeDtypeStruct((seq_count, 3 * HD, tok), BF16),
-        compiler_params=pltpu.CompilerParams(vmem_limit_bytes=VMEM_LIMIT),
-        cost_estimate=pl.CostEstimate(
-            flops=2 * tok * weight.size, bytes_accessed=2 * weight.size * 3, transcendentals=0
-        ),
-        name="project",
-    )(weight, attn_in, cosine, sine)
+
+    def project(s, out_ref):
+        each(pairs, lambda j: w_arrival(s, 2 * j + 1 - c).wait_recv())
+        if shard % 16 == 0:
+            weight = w_ref[s].reshape(fs * shard, 3 * block)
+        else:
+            for i in range(fs):
+                w_full[i * shard : (i + 1) * shard, :] = w_ref[s, i].astype(F32)
+            weight = w_full[...].astype(BF16)
+        rows = mm(weight, attn_in_ref[...], 0, 1).astype(BF16)
+        for shard_of in range(nz):
+            for part in range(3):
+                base = (part * nz + shard_of) * HD
+                if part == 2:
+                    out_ref[shard_of, part * HD : (part + 1) * HD, :] = rows[base : base + HD]
+                else:
+                    a = rows[base : base + half].astype(F32)
+                    b = rows[base + half : base + HD].astype(F32)
+                    out_ref[shard_of, part * HD : part * HD + half, :] = (a * cosine - b * sine).astype(BF16)
+                    out_ref[shard_of, part * HD + half : (part + 1) * HD, :] = (b * cosine + a * sine).astype(BF16)
+
+    def z_copy(i):
+        peer = lax.rem(z + 1 + i, nz)
+        return remote(z_send.at[peer], heads_ref.at[z], z_s.at[i], z_r.at[z], seq=peer)
+
+    def z_arrival(i):
+        peer = lax.rem(z + 1 + i, nz)
+        return remote(z_send.at[peer], heads_ref.at[peer], z_s.at[i], z_r.at[peer], seq=peer)
+
+    project(0, z_send)
+    each(nz - 1, lambda i: z_copy(i).start())
+    heads_ref[z] = z_send[z]
+    for s in range(1, slots):
+        pass_weight(s)
+        project(s, rest_refs[s - 1])
+
+    each(nz - 1, lambda i: z_arrival(i).wait_recv())
+    each(nz - 1, lambda i: z_copy(i).wait_send())
+
+    def drain_peers(i):
+        small_copy(i).wait_send()
+        mod_copy(i).wait_send()
+
+    def drain_weights(i):
+        for s in range(slots):
+            w_peer(s, i).wait_send()
+            w_pass(s, i).wait_send()
+
+    each(fs - 1, drain_peers)
+    each(pairs - 1, drain_weights)
+    for s in range(slots):
+        w_partner(s).wait_send()
+
+
+def start(qkv_weight, tokens, gains, cond, mod_weight, mod_bias, cosine, sine, fs, nz):
+    slots = H // nz
+    tok, width = tokens.shape
+    shard = qkv_weight.shape[0]
+    pairs = fs // 2
+    row = lambda v: v.reshape(1, -1)
+    ff = gains[2].shape[0] * fs
+    vmem = pl.BlockSpec(memory_space=pltpu.VMEM)
+    hbm = pl.BlockSpec(memory_space=pl.ANY)
+    low = lambda *shape: pltpu.VMEM(shape, BF16)
+    wide = lambda *shape: pltpu.VMEM(shape, F32)
+    dma = lambda *shape: pltpu.SemaphoreType.DMA(shape)
+    head_shape = (nz, 3 * HD, tok)
+    cols = 3 * nz * HD
+    small = 3 * width + ff + cond.shape[-1]
+    outs = pl.pallas_call(
+        partial(start_kernel, fs, nz, slots),
+        in_specs=[vmem, hbm] + [vmem] * 9,
+        out_specs=[vmem] * (slots + 5),
+        out_shape=[jax.ShapeDtypeStruct(head_shape, BF16)] * slots
+        + [
+            jax.ShapeDtypeStruct((slots, fs, shard, cols), BF16),
+            jax.ShapeDtypeStruct((tok, width), BF16),
+            jax.ShapeDtypeStruct((8, width), F32),
+            jax.ShapeDtypeStruct((ff // width, 1, width), F32),
+            jax.ShapeDtypeStruct((fs, cond.shape[-1]), F32),
+        ],
+        scratch_shapes=[
+            wide(tok, width),
+            low(slots, shard, cols),
+            low(*head_shape),
+            wide(8, width),
+            wide(8, ff),
+            wide(fs, 6 * width),
+            wide(1, small),
+            wide(fs, 1, small),
+            wide(fs, 1, 6 * width),
+            wide(fs, 1, 6 * width),
+            wide(*((8, 128) if shard % 16 == 0 else (width, cols))),
+            pltpu.SemaphoreType.DMA,
+            dma(fs - 1),
+            dma(fs),
+            dma(fs - 1),
+            dma(fs),
+            dma(slots, pairs),
+            dma(slots, pairs),
+            dma(slots, fs),
+            dma(nz - 1),
+            dma(nz),
+        ],
+        compiler_params=pltpu.CompilerParams(vmem_limit_bytes=VMEM_LIMIT, collective_id=2, has_side_effects=True),
+        cost_estimate=pl.CostEstimate(flops=6 * tok * width * cols, bytes_accessed=10**8, transcendentals=0),
+        name="start",
+    )(
+        qkv_weight,
+        tokens,
+        row(gains[0]),
+        row(gains[1]),
+        row(gains[2]),
+        row(gains[3]),
+        cond.reshape(1, -1),
+        mod_weight,
+        row(mod_bias),
+        cosine,
+        sine,
+    )
+    return outs[:slots], *outs[slots:]
 
 
 def attend_kernel(n, tok, sub, x_ref, o_ref, lse_ref, k_ref):
@@ -236,7 +520,7 @@
     def _():
         for s in range(slots):
             for c in range(n):
-                head = c * slots + s
+                head = s * n + c
                 mixed_ref[head * HD : (head + 1) * HD, :] = mixed_refs[s][c]
         attn_out_ref[...] = mm(mixed_ref[...], out_w_ref[...], 0, 0)
 
@@ -296,7 +580,7 @@
         grad_mixed = mm(out_w_ref[...], attn_low, 1, 1).astype(BF16)
         for s in range(slots):
             for c in range(n):
-                head = c * slots + s
+                head = s * n + c
                 grad_mixed_refs[s][c] = grad_mixed[head * HD : (head + 1) * HD]
 
 
@@ -352,49 +636,16 @@
         compiler_params=pltpu.CompilerParams(vmem_limit_bytes=VMEM_LIMIT),
         cost_estimate=pl.CostEstimate(flops=flops, bytes_accessed=6 * ff * width * 2, transcendentals=tok * ff),
         name="middle",
-    )(tokens, cot, vectors, up_bias.reshape(blocks, 1, width), w_pack, w_down, w_pack, *mixed)
-
-
-MESH = pl.DeviceIdType.MESH
-HIGHEST = lax.Precision.HIGHEST
-
-
-def add_low(a, b):
-    return (a.astype(F32) + b.astype(F32)).astype(BF16)
-
-
-def remote(src, dst, s, r, **where):
-    return pltpu.make_async_remote_copy(
-        src_ref=src, dst_ref=dst, send_sem=s, recv_sem=r, device_id=where, device_id_type=MESH
-    )
-
-
-def each(count, body):
-    lax.fori_loop(0, count, lambda i, _: (body(i), 0)[1], 0)
-
-
-def greet(me, z, fs, nz):
-    barrier = pltpu.get_barrier_semaphore()
-
-    def hello_fsdp(i):
-        peer = {"fsdp": lax.rem(me + 1 + i, fs)}
-        pl.semaphore_signal(barrier, inc=1, device_id=peer, device_id_type=MESH)
-
-    def hello_seq(i):
-        peer = {"seq": lax.rem(z + 1 + i, nz)}
-        pl.semaphore_signal(barrier, inc=1, device_id=peer, device_id_type=MESH)
-
-    each(fs - 1, hello_fsdp)
-    each(nz - 1, hello_seq)
-    pl.semaphore_wait(barrier, fs + nz - 2)
+    )(tokens, cot, vectors, up_bias, w_pack, w_down, w_pack, *mixed)
 
 
 def reduce_kernel(fs, nz, slots, counts, lengths, *refs):
-    row_refs, w_refs, refs = refs[:slots], refs[slots : 2 * slots], refs[2 * slots :]
+    swapped_refs, w_refs, refs = refs[:slots], refs[slots : 2 * slots], refs[2 * slots :]
     attn_in_ref, tokens_hbm, hidden_hbm, vec_in_ref, sums_ref, up_bias_ref, *refs = refs
     bulk_refs, (mod_t_ref, cond_ref), refs = refs[:2], refs[2:4], refs[4:]
-    inputs_out, qkv_out, pack_out, down_out, total_out, mod_w_out, cond_out = refs[:7]
+    inputs_out, qkv_out, up_out, out_out, down_out, total_out, mod_w_out, cond_out = refs[:8]
     (
+        row_buf,
         w_buf,
         tokens_buf,
         hidden_buf,
@@ -438,7 +689,7 @@
         vec_r,
         cond_s,
         cond_r,
-    ) = refs[7:]
+    ) = refs[8:]
     me = lax.axis_index("fsdp")
     z = lax.axis_index("seq")
     pairs = fs // 2
@@ -529,7 +780,11 @@
         return remote(sum_buf.at[s, j], recv_buf.at[s, j], peer_s.at[s, j], peer_r.at[s, j], fsdp=2 * j + c)
 
     for s in range(slots):
-        grad = mm(attn_in_ref[...], row_refs[s][...], 0, 1).astype(BF16)
+        for head in range(nz):
+            for p in range(3):
+                base = (p * nz + head) * HD
+                row_buf[s, base : base + HD, :] = swapped_refs[s][head, p * HD : (p + 1) * HD, :]
+        grad = mm(attn_in_ref[...], row_buf[s], 0, 1).astype(BF16)
         for i in range(fs):
             g_buf[s, i // 2, i % 2] = grad[i * shard : (i + 1) * shard]
         each(pairs, lambda i: pair_copy(s, lax.rem(k + 1 + i, pairs)).start())
@@ -555,7 +810,7 @@
         rows = slice(i * piece, (i + 1) * piece)
         grad = None
         for s in range(slots):
-            part = mm(row_refs[s][:, rows], w_buf[s], 0, 1)
+            part = mm(row_buf[s, :, rows], w_buf[s], 0, 1)
             grad = part if grad is None else grad + part
         hat, inv = normalize(tokens_buf[rows, :])
         scaled = grad * ((1.0 + scale_attn) * attn_gain)
@@ -674,9 +929,18 @@
             tot_copy(n, item).wait_recv()
             up_copy(n, item).wait_send()
 
-    pack_out[...] = tot_pack[...]
-    down_out[...] = tot_down[...]
-    qkv_out[...] = tot_qkv[...]
+    block = nz * HD
+    ff = up_out.shape[1]
+    for i in range(counts[0]):
+        rows = slice(i * tot_pack.shape[1], (i + 1) * tot_pack.shape[1])
+        up_out[rows, :] = tot_pack[i, :, :ff].astype(F32)
+        out_out[rows, :] = tot_pack[i, :, ff:].astype(F32)
+    for i in range(counts[1]):
+        down_out[i * tot_down.shape[1] : (i + 1) * tot_down.shape[1], :] = tot_down[i].astype(F32)
+    for s in range(slots):
+        for p in range(3):
+            columns = slice(p * width + s * block, p * width + (s + 1) * block)
+            qkv_out[:, columns] = tot_qkv[s, :, p * block : (p + 1) * block].astype(F32)
 
     @pl.when(inner)
     def _():
@@ -725,21 +989,23 @@
     dma = lambda *shape: pltpu.SemaphoreType.DMA(shape)
     qkv_shape = (slots, shard, width)
     triple = [low(*pack.shape), low(*down.shape), low(*qkv_shape)]
-    cols = grad_rows[0].shape[0]
-    inputs_grad, qkv_sum, pack_sum, down_sum, total, mod_w, cond_grad = pl.pallas_call(
+    cols = grad_rows[0].shape[0] * grad_rows[0].shape[1]
+    inputs_grad, qkv_sum, up_sum, out_sum, down_sum, total, mod_w, cond_grad = pl.pallas_call(
         partial(reduce_kernel, fs, nz, slots, counts, lengths),
         in_specs=[vmem] * slots + [hbm] * slots + [vmem, hbm, hbm] + [vmem] * 7,
-        out_specs=[vmem] * 7,
+        out_specs=[vmem] * 8,
         out_shape=[
             jax.ShapeDtypeStruct((tok, width), F32),
-            jax.ShapeDtypeStruct(qkv_shape, BF16),
-            jax.ShapeDtypeStruct(pack.shape, BF16),
-            jax.ShapeDtypeStruct(down.shape, BF16),
+            jax.ShapeDtypeStruct((shard, 3 * width), F32),
+            jax.ShapeDtypeStruct((shard, ff), F32),
+            jax.ShapeDtypeStruct((shard, part_pack.shape[1] - ff), F32),
+            jax.ShapeDtypeStruct(part_down.shape, F32),
             jax.ShapeDtypeStruct((places, 128), F32),
             jax.ShapeDtypeStruct((cond.shape[1], mod_cols), F32),
             jax.ShapeDtypeStruct((8, 128), F32),
         ],
         scratch_shapes=[
+            low(slots, cols, tok),
             low(slots, width, cols),
             wide(tok, width),
             wide(tok, width),
@@ -774,9 +1040,7 @@
         n = -(-v // fs // 128)
         blocks.append(total[place : place + n].reshape(-1)[: v // fs])
         place += n
-    return (
-        inputs_grad, qkv_sum, pack_sum.reshape(part_pack.shape), down_sum.reshape(part_down.shape), blocks, mod_w, cond_grad
-    )
+    return inputs_grad, qkv_sum, up_sum, out_sum, down_sum, blocks, mod_w, cond_grad
 
 
 def per_device(
@@ -797,56 +1061,43 @@
     n = lax.axis_size("seq")
     fs = lax.axis_size("fsdp")
     z = lax.axis_index("seq")
-    me = lax.axis_index("fsdp")
     tokens = inputs[0]
     tok, width = tokens.shape
     slots = H // n
     gather = lambda a: lax.all_gather(a, "fsdp", axis=0, tiled=True)
 
-    smalls = [attn_gain, mlp_gain, up_bias, down_bias, conditioning[0]]
-    sizes = [a.shape[0] for a in smalls]
-    packed = lax.all_gather(jnp.concatenate(smalls), "fsdp", axis=0)
-    offsets = [sum(sizes[:i]) for i in range(len(sizes))]
-    attn_gain_full, mlp_gain_full, up_bias_full, down_bias_full = (
-        packed[:, o : o + s].reshape(-1) for o, s in zip(offsets[:4], sizes[:4])
+    inv_freq = jnp.exp(-math.log(10000.0) * jnp.arange(HD // 2, dtype=F32) * (2.0 / HD))
+    positions = jnp.arange(tok, dtype=F32)
+    own_angles = inv_freq[:, None] * (positions + (z * tok).astype(F32))[None, :]
+    starts = (jnp.arange(n) * tok).astype(F32)
+    all_angles = inv_freq[None, :, None] * (positions[None, :] + starts[:, None])[:, None, :]
+    cos_all, sin_all = jnp.cos(all_angles), jnp.sin(all_angles)
+
+    sent, qkv_slots, attn_in, vectors, up_bias_full, cond_low_all = start(
+        qkv_weight,
+        tokens,
+        (attn_gain, mlp_gain, up_bias, down_bias),
+        conditioning,
+        mod_weight,
+        mod_bias,
+        jnp.cos(own_angles),
+        jnp.sin(own_angles),
+        fs,
+        n,
     )
-    cond_all = packed[:, offsets[4] :]
-    cond_act_all = jax.nn.silu(cond_all)
-    cond_low_all = cond_act_all.astype(BF16)
-    mod_low = mod_weight.astype(BF16)
-    mod_own = mm(cond_low_all, mod_low, 1, 0) + mod_bias[None, :]
-    modulation = lax.all_to_all(mod_own, "fsdp", split_axis=0, concat_axis=0, tiled=True).reshape(-1)
-    shift_attn, scale_attn, gate_attn, shift_mlp, scale_mlp, gate_mlp = jnp.split(modulation, 6)
-
-    shard = qkv_weight.shape[0]
-    qkv_low = qkv_weight.astype(BF16).reshape(shard, 3, n, slots, HD)
-    qkv_slots = [
-        gather(qkv_low[:, :, :, s].transpose(0, 2, 1, 3).reshape(shard, n * 3 * HD)) for s in range(slots)
-    ]
-    w_pack = gather(jnp.concatenate([up_weight.astype(BF16), out_weight.astype(BF16)], axis=1))
-    down_full = gather(down_weight.astype(BF16))
-
-    inv_freq = jnp.exp(-math.log(10000.0) * jnp.arange(HD // 2, dtype=F32) * (2.0 / HD))
-    angles = inv_freq[:, None] * jnp.arange(tok * n, dtype=F32)[None, :]
-    cos_all = jnp.cos(angles).reshape(HD // 2, n, tok).transpose(1, 0, 2)
-    sin_all = jnp.sin(angles).reshape(HD // 2, n, tok).transpose(1, 0, 2)
-    cos_own = lax.dynamic_index_in_dim(cos_all, z, 0, keepdims=False)
-    sin_own = lax.dynamic_index_in_dim(sin_all, z, 0, keepdims=False)
-
-    hat_attn, inv_attn = normalize(tokens)
-    normed_attn = hat_attn * attn_gain_full
-    attn_in = (normed_attn * (1.0 + scale_attn) + shift_attn).astype(BF16)
     swap = lambda a: lax.all_to_all(a, "seq", split_axis=0, concat_axis=0, tiled=True)
-    heads = [swap(project(w, attn_in, cos_own, sin_own, n)) for w in qkv_slots]
+    heads = [sent[0]] + [swap(a) for a in sent[1:]]
+    pack_own = jnp.concatenate([up_weight.astype(BF16), out_weight.astype(BF16)], axis=1)
+    down_own = down_weight.astype(BF16)
+    attn_in, pack_own, down_own = lax.optimization_barrier((attn_in, pack_own, down_own))
+    w_pack, down_full = gather(pack_own), gather(down_own)
+
     mixed_heads, log_totals, mixed_back = [], [], []
     for x in heads:
         o, lse = attend(x)
         mixed_heads.append(o)
         log_totals.append(lse)
         mixed_back.append(swap(o))
-    vectors = jnp.stack(
-        [gate_attn, shift_mlp, scale_mlp, gate_mlp, mlp_gain_full, down_bias_full, attn_gain_full, scale_attn], axis=0
-    )
     output, grad_hidden, sums, up_bias_sum, g_down, g_pack, *grad_mixed = middle(
         tokens, cotangent[0], vectors, up_bias_full, w_pack, down_full, mixed_back
     )
@@ -863,10 +1114,10 @@
     grad_slots[-1], part_pack = lax.optimization_barrier((grad_slots[-1], part_pack))
 
     mod_cols = mod_weight.shape[1]
-    mod_t = jnp.pad(mod_low.T.astype(F32), ((0, -mod_cols % 128), (0, 0))).reshape(-1, 128, mod_weight.shape[0])
-    inputs_grad, qkv_sum, pack_sum, down_sum, blocks, mod_weight_grad, cond_grad = reduce_all(
-        [g.reshape(n * 3 * HD, tok) for g in grad_slots],
-        qkv_slots,
+    mod_t = jnp.pad(mod_weight.astype(BF16).T.astype(F32), ((0, -mod_cols % 128), (0, 0)))
+    inputs_grad, qkv_weight_grad, up_sum, out_sum, down_sum, blocks, mod_weight_grad, cond_grad = reduce_all(
+        grad_slots,
+        [qkv_slots[s].reshape(width, -1) for s in range(slots)],
         attn_in,
         tokens,
         grad_hidden,
@@ -875,8 +1126,8 @@
         up_bias_sum,
         part_pack,
         part_down,
-        mod_t,
-        cond_low_all.astype(F32),
+        mod_t.reshape(-1, 128, mod_weight.shape[0]),
+        cond_low_all,
         mod_cols,
         fs,
         n,
@@ -884,12 +1135,6 @@
     mod_bias_grad, attn_gain_grad, mlp_gain_grad, up_bias_grad, down_bias_grad = blocks
     _, silu_pull = jax.vjp(jax.nn.silu, conditioning)
     conditioning_grad = silu_pull(cond_grad[:1])[0]
-    qkv_weight_grad = (
-        qkv_sum.astype(F32).reshape(slots, shard, n, 3, HD).transpose(1, 3, 2, 0, 4).reshape(shard, 3 * width)
-    )
-    pack_sum, down_sum = pack_sum.astype(F32), down_sum.astype(F32)
-    ff = up_bias.shape[0] * fs
-    out_sum, up_sum = pack_sum[:, ff:], pack_sum[:, :ff]
     return (
         output[None],
         inputs_grad[None],

time: 503 us -> 502 us (level)
  waiting for transfers between devices: 102 us -> 41.8 us
  blocking collectives: 38.9 us -> 84.3 us
  Pallas kernels: 252 us -> 293 us
  starting transfers between devices: 52.4 us -> 30.2 us
    all_to_all x1 -> x4, blocking collectives: 13 us -> 84.3 us  [per_device(): lax.all_to_all(a, 'seq', split_axis=0, concat_axis=0, tiled=True)]
    all_to_all x11 -> x7, waiting for transfers between devices: 96.5 us -> 40.5 us  [per_device(): lax.all_to_all(a, 'seq', split_axis=0, concat_axis=0, tiled=True)]
    pallas_call x3 -> x1, Pallas kernels: 11.4 us -> 52.1 us  [start(): pl.pallas_call(partial(start_kernel, fs, nz, slots), in_specs=[vmem, hbm]...]
    unnamed x1 -> x0, blocking collectives: 25.9 us -> none
    all_to_all x11 -> x7, starting transfers between devices: 48.4 us -> 30.1 us  [per_device(): lax.all_to_all(a, 'seq', split_axis=0, concat_axis=0, tiled=True)]
    unnamed x67 -> x37, local copies, waits for them, and re-layouts: 9.54 us -> 12.6 us
  transfers between devices with their start and end apart: 19 -> 11, of which waited for: 8 -> 3; matrix products, arithmetic and copies ran while one was open for 3% -> 1% of each run, Pallas kernels for 30% -> 27%
where the time goes in v4:
time: 502 us; the launch traced here: 494 us
  Pallas kernels  293 us (58%)
  blocking collectives  84.3 us (17%)
  waiting for transfers between devices  41.8 us (8%)
  starting transfers between devices  30.2 us (6%)
  local copies, waits for them, and re-layouts  20.9 us (4%)
  between operations  14.4 us (3%)
  other arithmetic  9.55 us (2%)
    pallas_call x3, Pallas kernels, attend_back(): pl.pallas_call(partial(attend_back_kernel, n, tok, 2), grid=(n,), in_spec...  85.5 us
    all_to_all x4, blocking collectives, per_device(): lax.all_to_all(a, 'seq', split_axis=0, concat_axis=0, tiled=True)  84.3 us
    pallas_call x1, Pallas kernels, reduce_all(): pl.pallas_call(partial(reduce_kernel, fs, nz, slots, counts, lengths), in...  65.8 us
    pallas_call x1, Pallas kernels, start(): pl.pallas_call(partial(start_kernel, fs, nz, slots), in_specs=[vmem, hbm]...  52.1 us
    pallas_call x3, Pallas kernels, attend(): pl.pallas_call(partial(attend_kernel, n, tok, 2), grid=(n,), in_specs=[pl...  49.9 us
    all_to_all x7, waiting for transfers between devices, per_device(): lax.all_to_all(a, 'seq', split_axis=0, concat_axis=0, tiled=True)  40.5 us
    pallas_call x1, Pallas kernels, middle(): pl.pallas_call(partial(middle_kernel, n, slots, blocks), grid=(blocks + 1...  39.5 us
    all_to_all x7, starting transfers between devices, per_device(): lax.all_to_all(a, 'seq', split_axis=0, concat_axis=0, tiled=True)  30.1 us
  transfers between devices with their start and end apart: 11, of which 3 were waited for; matrix products, arithmetic and copies ran while one was open for 1% of the time, Pallas kernels for 27%

profile of v4, /device:TPU:0, one launch (start us, length us, event | category | flops | bytes accessed | tf_op | source)
XLA Modules:
  0.0 494.0 jit_solution(11429686658636036134)
XLA Ops:
  16.0 52.1 %start.1 = (bf16[4,192,768]{2,1,0:T(8,128)(2,1)}, bf16[4,192,768]{2,1,0:T(8,128)(2,1)}, bf16[4,192,768]{2,1,0:T(8,128)(2,1)}, bf16[3,8,96,768]{3,2,1,0:T(8,128)(...) custom-call(f32[96,2304]{1,0:T(8,128)} %refs_0_.1, ...), custom_call_target="tpu_custom_call" | custom-call | flops 2717908992 | bytes 100000000 | tf_op jit(solution)/shard_map/start/pallas_call | solution.py:297
  68.9 16.7 %attend.3 = (bf16[4,64,768]{2,1,0:T(8,128)(2,1)}, f32[4,1,768]{2,1,0:T(1,128)}) custom-call(bf16[4,192,768]{2,1,0:T(8,128)(2,1)} %get-tuple-element.56.x_ref), custom_call_target="tpu_custom_call" | custom-call | flops 9663676416 | bytes 1572864 | tf_op jit(solution)/shard_map/attend/pallas_call | solution.py:395
  85.6 22.2 %all_to_all.55.refs_0_ = bf16[4,64,768]{2,1,0:T(8,128)(2,1)} all-to-all(bf16[4,64,768]{2,1,0:T(8,128)(2,1)} %get-tuple-element.57.o_ref), channel_id=1, replica_groups=mesh['fsdp'=8,'seq'=4] {'seq'}, dimensions={0} | all-to-all | bytes 786432 | tf_op jit(solution)/shard_map/all_to_all | solution.py:1088
  107.9 32.2 %all_to_all.56.x_ref = bf16[4,192,768]{2,1,0:T(8,128)(2,1)} all-to-all(bf16[4,192,768]{2,1,0:T(8,128)(2,1)S(1)} %copy-done.6), channel_id=1, replica_groups=mesh['fsdp'=8,'seq'=4] {'seq'}, dimensions={0} | all-to-all | bytes 2359296 | tf_op jit(solution)/shard_map/all_to_all | solution.py:1088
  140.1 3.7 all-to-all-start.3
  143.9 16.6 %attend.4 = (bf16[4,64,768]{2,1,0:T(8,128)(2,1)}, f32[4,1,768]{2,1,0:T(1,128)}) custom-call(bf16[4,192,768]{2,1,0:T(8,128)(2,1)} %all_to_all.56.x_ref), custom_call_target="tpu_custom_call" | custom-call | flops 9663676416 | bytes 1572864 | tf_op jit(solution)/shard_map/attend/pallas_call | solution.py:395
  160.5 11.6 %all-to-all-done.3.x_ref = bf16[4,192,768]{2,1,0:T(8,128)(2,1)S(1)} async-done(((bf16[4,192,768]{2,1,0:T(8,128)(2,1)}), bf16[4,192,768]{2,1,0:T(8,128)(2,1)S(1)}, u32[]{:S(2)}, u32[]{:S(2)}) %all-to-all-start.3) | async-done | bytes 1179680 | tf_op jit(solution)/shard_map/all_to_all | solution.py:1088
  172.1 3.5 all-to-all-start.2
  175.6 16.6 %attend.5 = (bf16[4,64,768]{2,1,0:T(8,128)(2,1)}, f32[4,1,768]{2,1,0:T(1,128)}) custom-call(bf16[4,192,768]{2,1,0:T(8,128)(2,1)} %copy-done.2), custom_call_target="tpu_custom_call" | custom-call | flops 9663676416 | bytes 1572864 | tf_op jit(solution)/shard_map/attend/pallas_call | solution.py:395
  192.2 16.2 %all_to_all.57.refs_2_ = bf16[4,64,768]{2,1,0:T(8,128)(2,1)} all-to-all(bf16[4,64,768]{2,1,0:T(8,128)(2,1)} %get-tuple-element.61.o_ref), channel_id=1, replica_groups=mesh['fsdp'=8,'seq'=4] {'seq'}, dimensions={0} | all-to-all | bytes 786432 | tf_op jit(solution)/shard_map/all_to_all | solution.py:1088
  208.4 39.5 %middle.1 = (f32[768,768]{1,0:T(8,128)}, f32[768,768]{1,0:T(8,128)}, f32[8,768]{1,0:T(8,128)}, f32[4,1,768]{2,1,0:T(1,128)}, bf16[3072,768]{1,0:T(8,128)(2,1)}, ...) custom-call(f32[768,768]{1,0:T(8,128)} %bitcast.35, ...), custom_call_target="tpu_custom_call" | custom-call | flops 24461180928 | bytes 28311552 | tf_op jit(solution)/shard_map/middle/pallas_call | solution.py:598
  248.9 13.6 %all_to_all.58.g_ref = bf16[4,64,768]{2,1,0:T(8,128)(2,1)} all-to-all(bf16[4,64,768]{2,1,0:T(8,128)(2,1)S(1)} %copy-done.11), channel_id=1, replica_groups=mesh['fsdp'=8,'seq'=4] {'seq'}, dimensions={0} | all-to-all | bytes 786432 | tf_op jit(solution)/shard_map/all_to_all | solution.py:1088
  262.5 3.5 all-to-all-start.7
  268.9 7.4 %all-to-all-done.7.g_ref = bf16[4,64,768]{2,1,0:T(8,128)(2,1)S(1)} async-done(((bf16[4,64,768]{2,1,0:T(8,128)(2,1)}), bf16[4,64,768]{2,1,0:T(8,128)(2,1)S(1)}, u32[]{:S(2)}, u32[]{:S(2)}) %all-to-all-start.7) | async-done | bytes 393248 | tf_op jit(solution)/shard_map/all_to_all | solution.py:1088
  276.3 3.6 all-to-all-start.5
  279.9 28.4 %attend_back.5 = bf16[4,192,768]{2,1,0:T(8,128)(2,1)} custom-call(bf16[4,192,768]{2,1,0:T(8,128)(2,1)} %copy-done.2, bf16[4,64,768]{2,1,0:T(8,128)(2,1)} %all_to_all.58.g_ref, bf16[4,64,768]{2,1,0:T(8,128)(2,1)} %get-tuple-element.61.o_ref, f32[4,1,768]{2,1,0:T(1,128)} %get-tuple-element.70.lse_ref, f32[4,32,768]{2,1,0:T(8,128)} %get-tuple-element.106.cos_ref, ...), custom_call_target="tpu_custom_call" | custom-call | flops 24159191040 | bytes 3145728 | tf_op jit(solution)/shard_map/attend_back/pallas_call | solution.py:473
  308.3 5.1 %all-to-all-start.10 = ((bf16[4,192,768]{2,1,0:T(8,128)(2,1)}), bf16[4,192,768]{2,1,0:T(8,128)(2,1)S(1)}, u32[]{:S(2)}, u32[]{:S(2)}) async-start(bf16[4,192,768]{2,1,0:T(8,128)(2,1)} %attend_back.5), calls=%async_computation.11 | async-start | bytes 2359296 | tf_op jit(solution)/shard_map/all_to_all | solution.py:1088
  313.4 28.7 %attend_back.3 = bf16[4,192,768]{2,1,0:T(8,128)(2,1)} custom-call(bf16[4,192,768]{2,1,0:T(8,128)(2,1)} %get-tuple-element.56.x_ref, bf16[4,64,768]{2,1,0:T(8,128)(2,1)} %copy-done.10, bf16[4,64,768]{2,1,0:T(8,128)(2,1)} %get-tuple-element.57.o_ref, f32[4,1,768]{2,1,0:T(1,128)} %get-tuple-element.64.lse_ref, f32[4,32,768]{2,1,0:T(8,128)} %get-tuple-element.106.cos_ref, ...), custom_call_target="tpu_custom_call" | custom-call | flops 24159191040 | bytes 3145728 | tf_op jit(solution)/shard_map/attend_back/pallas_call | solution.py:473
  342.2 5.3 %all-to-all-start.6 = ((bf16[4,192,768]{2,1,0:T(8,128)(2,1)}), bf16[4,192,768]{2,1,0:T(8,128)(2,1)}, u32[]{:S(2)}, u32[]{:S(2)}) async-start(bf16[4,192,768]{2,1,0:T(8,128)(2,1)} %attend_back.3), calls=%async_computation.6 | async-start | bytes 2359296 | tf_op jit(solution)/shard_map/all_to_all | solution.py:1088
  347.5 28.3 %attend_back.4 = bf16[4,192,768]{2,1,0:T(8,128)(2,1)} custom-call(bf16[4,192,768]{2,1,0:T(8,128)(2,1)} %all_to_all.56.x_ref, bf16[4,64,768]{2,1,0:T(8,128)(2,1)} %copy-done.8, bf16[4,64,768]{2,1,0:T(8,128)(2,1)} %get-tuple-element.59.o_ref, f32[4,1,768]{2,1,0:T(1,128)} %get-tuple-element.68.lse_ref, f32[4,32,768]{2,1,0:T(8,128)} %get-tuple-element.106.cos_ref, ...), custom_call_target="tpu_custom_call" | custom-call | flops 24159191040 | bytes 3145728 | tf_op jit(solution)/shard_map/attend_back/pallas_call | solution.py:473
  375.9 5.4 %all-to-all-start.8 = ((bf16[4,192,768]{2,1,0:T(8,128)(2,1)}), bf16[4,192,768]{2,1,0:T(8,128)(2,1)}, u32[]{:S(2)}, u32[]{:S(2)}) async-start(bf16[4,192,768]{2,1,0:T(8,128)(2,1)} %attend_back.4), calls=%async_computation.9 | async-start | bytes 2359296 | tf_op jit(solution)/shard_map/all_to_all | solution.py:1088
  384.9 21.6 %all-to-all-done.8.refs_1_ = bf16[4,192,768]{2,1,0:T(8,128)(2,1)} async-done(((bf16[4,192,768]{2,1,0:T(8,128)(2,1)}), bf16[4,192,768]{2,1,0:T(8,128)(2,1)}, u32[]{:S(2)}, u32[]{:S(2)}) %all-to-all-start.8) | async-done | bytes 1179680 | tf_op jit(solution)/shard_map/all_to_all | solution.py:1088
  406.4 65.8 %reduce_all.1 = (f32[768,768]{1,0:T(8,128)}, f32[96,2304]{1,0:T(8,128)}, f32[96,3072]{1,0:T(8,128)}, f32[96,768]{1,0:T(8,128)}, f32[384,768]{1,0:T(8,128)}, /*in...) custom-call(bf16[4,192,768]{2,1,0:T(8,128)(2,1)} %all-to-all-done.6.refs_0_, ...), custom_call_target="tpu_custom_call" | custom-call | flops 5435817984 | bytes 100000000 | tf_op jit(solution)/shard_map/reduce_all/pallas_call | solution.py:993
  479.1 3.3 copy.33
  (72 shorter events, 28.6 us)
Async XLA Ops:
  7.2 201.2 %all-gather.5.cloned.1.call-start = ((), (), s32[]{:S(2)}) async-start(), calls=%async_computation.14 | async-start | bytes 5308416 | tf_op jit(solution)/shard_map/all_gather | solution.py:1067
  7.3 5.9 %copy-start.12 = (f32[96,768]{1,0:T(8,128)S(1)}, f32[96,768]{1,0:T(8,128)}, u32[]{:S(2)}) copy-start(f32[96,768]{1,0:T(8,128)} %param.19) | copy-start | bytes 884740
  9.2 4.0 copy-start.1
  68.2 140.2 %all-gather.3.cloned.1.call-start = ((), (), s32[]{:S(2)}) async-start(), calls=%async_computation.13 | async-start | bytes 6635520 | tf_op jit(solution)/shard_map/all_gather | solution.py:1067
  68.9 38.9 %copy-start.6 = (bf16[4,192,768]{2,1,0:T(8,128)(2,1)S(1)}, bf16[4,192,768]{2,1,0:T(8,128)(2,1)}, u32[]{:S(2)}) copy-start(bf16[4,192,768]{2,1,0:T(8,128)(2,1)} %get-tuple-element.58) | copy-start | bytes 3538948
  140.1 31.9 %all-to-all-start.3 = ((bf16[4,192,768]{2,1,0:T(8,128)(2,1)}), bf16[4,192,768]{2,1,0:T(8,128)(2,1)S(1)}, u32[]{:S(2)}, u32[]{:S(2)}) async-start(bf16[4,192,768]{2,1,0:T(8,128)(2,1)} %get-tuple-element.60), calls=%async_computation.3 | async-start | bytes 2359296 | tf_op jit(solution)/shard_map/all_to_all | solution.py:1088
  172.1 3.5 copy-start.2
  172.1 20.1 %all-to-all-start.2 = ((bf16[4,64,768]{2,1,0:T(8,128)(2,1)}), bf16[4,64,768]{2,1,0:T(8,128)(2,1)S(1)}, u32[]{:S(2)}, u32[]{:S(2)}) async-start(bf16[4,64,768]{2,1,0:T(8,128)(2,1)} %get-tuple-element.59.o_ref), calls=%async_computation.2 | async-start | bytes 786432 | tf_op jit(solution)/shard_map/all_to_all | solution.py:1088
  175.5 166.7 %reduce-scatter.3.cloned.1.call-start = ((), (), s32[]{:S(2)}) async-start(), calls=%async_computation.15 | async-start | bytes 5308416 | tf_op jit(solution)/shard_map/reduce_scatter | solution.py:1104
  192.2 16.2 %copy-start.9 = (bf16[4,64,768]{2,1,0:T(8,128)(2,1)}, bf16[4,64,768]{2,1,0:T(8,128)(2,1)S(1)}, u32[]{:S(2)}) copy-start(bf16[4,64,768]{2,1,0:T(8,128)(2,1)S(1)} %all-to-all-done.2.refs_1_) | copy-start | bytes 1179652
  262.5 13.8 %all-to-all-start.7 = ((bf16[4,64,768]{2,1,0:T(8,128)(2,1)}), bf16[4,64,768]{2,1,0:T(8,128)(2,1)S(1)}, u32[]{:S(2)}, u32[]{:S(2)}) async-start(bf16[4,64,768]{2,1,0:T(8,128)(2,1)} %get-tuple-element.65), calls=%async_computation.7 | async-start | bytes 786432 | tf_op jit(solution)/shard_map/all_to_all | solution.py:1088
  266.0 118.9 %reduce-scatter.5.cloned.1.call-start = ((), (), s32[]{:S(2)}) async-start(), calls=%async_computation.16 | async-start | bytes 6635520 | tf_op jit(solution)/shard_map/reduce_scatter | solution.py:1104
  276.3 32.1 %copy-start.8 = (bf16[4,64,768]{2,1,0:T(8,128)(2,1)}, bf16[4,64,768]{2,1,0:T(8,128)(2,1)S(1)}, u32[]{:S(2)}) copy-start(bf16[4,64,768]{2,1,0:T(8,128)(2,1)S(1)} %all-to-all-done.7.g_ref) | copy-start | bytes 1179652
  276.3 32.1 %all-to-all-start.5 = ((bf16[4,64,768]{2,1,0:T(8,128)(2,1)}), bf16[4,64,768]{2,1,0:T(8,128)(2,1)S(1)}, u32[]{:S(2)}, u32[]{:S(2)}) async-start(bf16[4,64,768]{2,1,0:T(8,128)(2,1)} %get-tuple-element.63), calls=%async_computation.5 | async-start | bytes 786432 | tf_op jit(solution)/shard_map/all_to_all | solution.py:1088
  308.3 5.1 %copy-start.10 = (bf16[4,64,768]{2,1,0:T(8,128)(2,1)}, bf16[4,64,768]{2,1,0:T(8,128)(2,1)S(1)}, u32[]{:S(2)}) copy-start(bf16[4,64,768]{2,1,0:T(8,128)(2,1)S(1)} %all-to-all-done.5.g_ref) | copy-start | bytes 1179652
  308.3 33.9 %all-to-all-start.10 = ((bf16[4,192,768]{2,1,0:T(8,128)(2,1)}), bf16[4,192,768]{2,1,0:T(8,128)(2,1)S(1)}, u32[]{:S(2)}, u32[]{:S(2)}) async-start(bf16[4,192,768]{2,1,0:T(8,128)(2,1)} %attend_back.5), calls=%async_computation.11 | async-start | bytes 2359296 | tf_op jit(solution)/shard_map/all_to_all | solution.py:1088
  342.2 5.3 %copy-start.3 = (bf16[4,192,768]{2,1,0:T(8,128)(2,1)}, bf16[4,192,768]{2,1,0:T(8,128)(2,1)S(1)}, u32[]{:S(2)}) copy-start(bf16[4,192,768]{2,1,0:T(8,128)(2,1)S(1)} %all-to-all-done.10.refs_2_) | copy-start | bytes 3538948
  342.2 33.7 %all-to-all-start.6 = ((bf16[4,192,768]{2,1,0:T(8,128)(2,1)}), bf16[4,192,768]{2,1,0:T(8,128)(2,1)}, u32[]{:S(2)}, u32[]{:S(2)}) async-start(bf16[4,192,768]{2,1,0:T(8,128)(2,1)} %attend_back.3), calls=%async_computation.6 | async-start | bytes 2359296 | tf_op jit(solution)/shard_map/all_to_all | solution.py:1088
  375.9 7.1 %copy-start = (bf16[3,8,96,768]{3,2,1,0:T(8,128)(2,1)S(1)}, bf16[3,8,96,768]{3,2,1,0:T(8,128)(2,1)}, u32[]{:S(2)}) copy-start(bf16[3,8,96,768]{3,2,1,0:T(8,128)(2,1)} %get-tuple-element.73) | copy-start | bytes 10616836
  375.9 30.6 %all-to-all-start.8 = ((bf16[4,192,768]{2,1,0:T(8,128)(2,1)}), bf16[4,192,768]{2,1,0:T(8,128)(2,1)}, u32[]{:S(2)}, u32[]{:S(2)}) async-start(bf16[4,192,768]{2,1,0:T(8,128)(2,1)} %attend_back.4), calls=%async_computation.9 | async-start | bytes 2359296 | tf_op jit(solution)/shard_map/all_to_all | solution.py:1088
  406.4 71.5 %copy-start.14 = (f32[1,128]{1,0:T(1,128)S(1)}, f32[1,128]{1,0:T(1,128)}, u32[]{:S(2)}) copy-start(f32[1,128]{1,0:T(1,128)} %refs_6_.1) | copy-start | bytes 1540
  479.1 3.3 copy-start.7
  482.5 1.8 copy-start.5
  484.3 1.7 copy-start.4
  (2 other events, 2.1 us)
Sparse Core Ops, SparseCore 0:
  68.3 44.2 all-gather.4
  115.0 43.7 all-gather.2
  248.1 50.9 reduce-scatter.2
  302.4 59.6 reduce-scatter.4

commit v5 on v4

--- a/solution.py
+++ b/solution.py
@@ -82,12 +82,24 @@
         mod_b_ref,
         cos_ref,
         sin_ref,
-    ) = refs[:11]
-    refs = refs[11:]
-    heads_ref, rest_refs, refs = refs[0], refs[1:slots], refs[slots:]
-    w_ref, attn_in_ref, vec_ref, bias_ref, cond_out = refs[:5]
+        up_hbm,
+        out_hbm,
+        down_hbm,
+        heads_ref,
+        rest_ref,
+        w_ref,
+        attn_in_ref,
+        vec_ref,
+        bias_ref,
+        cond_out,
+        pack_out,
+        down_out,
+    ) = refs[:23]
     (
         tokens_buf,
+        up_buf,
+        out_buf,
+        down_buf,
         w_own,
         z_send,
         narrow,
@@ -108,7 +120,7 @@
         w_r,
         z_s,
         z_r,
-    ) = refs[5:]
+    ) = refs[23:]
     me = lax.axis_index("fsdp")
     z = lax.axis_index("seq")
     pairs = fs // 2
@@ -119,19 +131,21 @@
     ff = spread.shape[1]
     block = nz * HD
 
-    load = pltpu.make_async_copy(tokens_hbm, tokens_buf, local_s)
-    load.start()
+    fetch = ((tokens_hbm, tokens_buf), (up_hbm, up_buf), (out_hbm, out_buf), (down_hbm, down_buf))
+    loads = [pltpu.make_async_copy(src, dst, local_s.at[i]) for i, (src, dst) in enumerate(fetch)]
+    for load in loads:
+        load.start()
     greet(me, z, fs, nz)
 
     narrow[...] = jnp.zeros_like(narrow)
     for i, piece in enumerate((attn_gain_ref, mlp_gain_ref, down_bias_ref)):
-        narrow[i : i + 1, :shard] = piece[...]
+        narrow[i : i + 1, :shard] = piece[...].reshape(1, -1)
     spread[...] = jnp.zeros_like(spread)
-    spread[0:1, : up_bias_ref.shape[1]] = up_bias_ref[...]
+    spread[0:1, : up_bias_ref.shape[0]] = up_bias_ref[...].reshape(1, -1)
     placed = pltpu.roll(narrow[...], me * shard, 1)
     for i in range(3):
         small_send[:, i * width : (i + 1) * width] = placed[i : i + 1]
-    placed = pltpu.roll(spread[...], me * up_bias_ref.shape[1], 1)
+    placed = pltpu.roll(spread[...], me * up_bias_ref.shape[0], 1)
     small_send[:, 3 * width : 3 * width + ff] = placed[0:1]
     small_send[:, 3 * width + ff :] = cond_ref[...]
     small_all[me] = small_send[...]
@@ -185,7 +199,7 @@
     cond_all = small_all[:, 0, 3 * width + ff :]
     cond_low = (cond_all / (1.0 + jnp.exp(-cond_all))).astype(BF16)
     cond_out[...] = cond_low.astype(F32)
-    own_mod = mm(cond_low, mod_w_ref[...].astype(BF16), 1, 0) + mod_b_ref[...]
+    own_mod = mm(cond_low, mod_w_ref[...].astype(BF16), 1, 1) + mod_b_ref[...].reshape(1, -1)
     mod_wide[...] = jnp.zeros_like(mod_wide)
     mod_wide[:, : own_mod.shape[1]] = own_mod
     placed = pltpu.roll(mod_wide[...], me * own_mod.shape[1], 1)
@@ -208,7 +222,8 @@
     attn_gain, mlp_gain, down_bias = (small_sum[:, i * width : (i + 1) * width] for i in range(3))
     for i in range(ff // width):
         bias_ref[i] = small_sum[:, (3 + i) * width : (4 + i) * width]
-    load.wait()
+    for load in loads:
+        load.wait()
     piece = min(256, tok)
     each(fs - 1, lambda i: mod_arrival(i).wait_recv())
     modulation = jnp.sum(mod_recv[...], axis=0)
@@ -259,8 +274,11 @@
     heads_ref[z] = z_send[z]
     for s in range(1, slots):
         pass_weight(s)
-        project(s, rest_refs[s - 1])
-
+        project(s, rest_ref.at[s - 1])
+
+    pack_out[:, :ff] = up_buf[...].astype(BF16)
+    pack_out[:, ff:] = out_buf[...].astype(BF16)
+    down_out[...] = down_buf[...].astype(BF16)
     each(nz - 1, lambda i: z_arrival(i).wait_recv())
     each(nz - 1, lambda i: z_copy(i).wait_send())
 
@@ -279,12 +297,12 @@
         w_partner(s).wait_send()
 
 
-def start(qkv_weight, tokens, gains, cond, mod_weight, mod_bias, cosine, sine, fs, nz):
+def start(qkv_weight, tokens, gains, cond, mod_weight, mod_bias, cosine, sine, feed, fs, nz):
     slots = H // nz
     tok, width = tokens.shape
     shard = qkv_weight.shape[0]
     pairs = fs // 2
-    row = lambda v: v.reshape(1, -1)
+    up, out, down = feed
     ff = gains[2].shape[0] * fs
     vmem = pl.BlockSpec(memory_space=pltpu.VMEM)
     hbm = pl.BlockSpec(memory_space=pl.ANY)
@@ -294,20 +312,26 @@
     head_shape = (nz, 3 * HD, tok)
     cols = 3 * nz * HD
     small = 3 * width + ff + cond.shape[-1]
-    outs = pl.pallas_call(
+    return pl.pallas_call(
         partial(start_kernel, fs, nz, slots),
-        in_specs=[vmem, hbm] + [vmem] * 9,
-        out_specs=[vmem] * (slots + 5),
-        out_shape=[jax.ShapeDtypeStruct(head_shape, BF16)] * slots
-        + [
+        in_specs=[vmem, hbm] + [vmem] * 9 + [hbm] * 3,
+        out_specs=[vmem] * 9,
+        out_shape=[
+            jax.ShapeDtypeStruct(head_shape, BF16),
+            jax.ShapeDtypeStruct((slots - 1, *head_shape), BF16),
             jax.ShapeDtypeStruct((slots, fs, shard, cols), BF16),
             jax.ShapeDtypeStruct((tok, width), BF16),
             jax.ShapeDtypeStruct((8, width), F32),
             jax.ShapeDtypeStruct((ff // width, 1, width), F32),
             jax.ShapeDtypeStruct((fs, cond.shape[-1]), F32),
+            jax.ShapeDtypeStruct((shard, up.shape[1] + out.shape[1]), BF16),
+            jax.ShapeDtypeStruct(down.shape, BF16),
         ],
         scratch_shapes=[
             wide(tok, width),
+            wide(*up.shape),
+            wide(*out.shape),
+            wide(*down.shape),
             low(slots, shard, cols),
             low(*head_shape),
             wide(8, width),
@@ -318,7 +342,7 @@
             wide(fs, 1, 6 * width),
             wide(fs, 1, 6 * width),
             wide(*((8, 128) if shard % 16 == 0 else (width, cols))),
-            pltpu.SemaphoreType.DMA,
+            dma(4),
             dma(fs - 1),
             dma(fs),
             dma(fs - 1),
@@ -335,33 +359,55 @@
     )(
         qkv_weight,
         tokens,
-        row(gains[0]),
-        row(gains[1]),
-        row(gains[2]),
-        row(gains[3]),
-        cond.reshape(1, -1),
-        mod_weight,
-        row(mod_bias),
+        *gains,
+        cond,
+        mod_weight.T,
+        mod_bias,
         cosine,
         sine,
+        *feed,
     )
-    return outs[:slots], *outs[slots:]
-
-
-def attend_kernel(n, tok, sub, x_ref, o_ref, lse_ref, k_ref):
-    step = pl.program_id(0)
-
-    @pl.when(step == 0)
-    def _():
-        for c in range(n):
-            k_ref[c * tok : (c + 1) * tok, :] = x_ref[c, HD : 2 * HD, :].T
+
+
+def greet_seq(z, nz):
+    barrier = pltpu.get_barrier_semaphore()
+
+    def hello(i):
+        peer = {"seq": lax.rem(z + 1 + i, nz)}
+        pl.semaphore_signal(barrier, inc=1, device_id=peer, device_id_type=MESH)
+
+    each(nz - 1, hello)
+    pl.semaphore_wait(barrier, nz - 1)
+
+
+def attend_kernel(n, slots, tok, sub, first_ref, rest_ref, x_ref, o_ref, mixed_ref, lse_ref, k_ref, x_s, x_r, o_s, o_r):
+    z = lax.axis_index("seq")
+    greet_seq(z, n)
+
+    def x_copy(s, i):
+        peer = lax.rem(z + 1 + i, n)
+        return remote(rest_ref.at[s - 1, peer], x_ref.at[s, z], x_s.at[s - 1, i], x_r.at[s - 1, z], seq=peer)
+
+    def x_arrival(s, i):
+        peer = lax.rem(z + 1 + i, n)
+        return remote(rest_ref.at[s - 1, peer], x_ref.at[s, peer], x_s.at[s - 1, i], x_r.at[s - 1, peer], seq=peer)
+
+    def o_copy(s, i):
+        peer = lax.rem(z + 1 + i, n)
+        return remote(o_ref.at[s, peer], mixed_ref.at[s, z], o_s.at[s, i], o_r.at[s, z], seq=peer)
+
+    def o_arrival(s, i):
+        peer = lax.rem(z + 1 + i, n)
+        return remote(o_ref.at[s, peer], mixed_ref.at[s, peer], o_s.at[s, i], o_r.at[s, peer], seq=peer)
+
+    for s in range(1, slots):
+        each(n - 1, lambda i: x_copy(s, i).start())
+    x_ref[0] = first_ref[...]
+    for s in range(1, slots):
+        x_ref[s, z] = rest_ref[s - 1, z]
 
     scale = LOG2E / math.sqrt(HD)
     width = tok // sub
-
-    def score(i):
-        q = x_ref[step, 0:HD, i * width : (i + 1) * width]
-        return mm(k_ref[...], q, 1, 0)
 
     def soft(s):
         top = jnp.max(s, axis=0, keepdims=True) * scale
@@ -369,63 +415,141 @@
         total = jnp.sum(p, axis=0, keepdims=True)
         return top, total, p.astype(BF16)
 
-    def mix(i, top, total, p):
-        o = None
+    def slot(s):
+        @pl.when(s > 0)
+        def _():
+            each(n - 1, lambda i: x_arrival(s, i).wait_recv())
+
         for c in range(n):
-            part = mm(x_ref[c, 2 * HD : 3 * HD, :], p[c * tok : (c + 1) * tok], 1, 0)
-            o = part if o is None else o + part
-        o_ref[0, :, i * width : (i + 1) * width] = (o / total).astype(BF16)
-        lse_ref[0, :, i * width : (i + 1) * width] = top + jnp.log2(total)
-
-    scores = [score(0)]
-    pending = None
-    for i in range(sub):
-        if i + 1 < sub:
-            scores.append(score(i + 1))
-        done = soft(scores[i])
-        if pending is not None:
-            mix(i - 1, *pending)
-        pending = done
-    mix(sub - 1, *pending)
-
-
-def attend(x):
-    n, _, tok = x.shape
+            k_ref[c * tok : (c + 1) * tok, :] = x_ref[s, c, HD : 2 * HD, :].T
+
+        def shard(i):
+            step = lax.rem(z + 1 + i, n)
+
+            def score(j):
+                q = x_ref[s, step, 0:HD, j * width : (j + 1) * width]
+                return mm(k_ref[...], q, 1, 0)
+
+            def mix(j, top, total, p):
+                o = None
+                for c in range(n):
+                    part = mm(x_ref[s, c, 2 * HD : 3 * HD, :], p[c * tok : (c + 1) * tok], 1, 0)
+                    o = part if o is None else o + part
+                o_ref[s, step, :, j * width : (j + 1) * width] = (o / total).astype(BF16)
+                lse_ref[s, step, :, j * width : (j + 1) * width] = top + jnp.log2(total)
+
+            scores = [score(0)]
+            pending = None
+            for j in range(sub):
+                if j + 1 < sub:
+                    scores.append(score(j + 1))
+                done = soft(scores[j])
+                if pending is not None:
+                    mix(j - 1, *pending)
+                pending = done
+            mix(sub - 1, *pending)
+
+            @pl.when(i < n - 1)
+            def _():
+                o_copy(s, i).start()
+
+        each(n, shard)
+        mixed_ref[s, z] = o_ref[s, z]
+
+    each(slots, slot)
+
+    def drain(s):
+        each(n - 1, lambda i: o_arrival(s, i).wait_recv())
+        each(n - 1, lambda i: o_copy(s, i).wait_send())
+
+    each(slots, drain)
+    for s in range(1, slots):
+        each(n - 1, lambda i: x_copy(s, i).wait_send())
+
+
+def attend(first, rest):
+    n, _, tok = first.shape
+    slots = rest.shape[0] + 1
     length = n * tok
+    vmem = pl.BlockSpec(memory_space=pltpu.VMEM)
+    dma = lambda *shape: pltpu.SemaphoreType.DMA(shape)
+    head_shape = (slots, n, HD, tok)
     return pl.pallas_call(
-        partial(attend_kernel, n, tok, 2),
-        grid=(n,),
-        in_specs=[pl.BlockSpec(x.shape, lambda i: (0, 0, 0))],
-        out_specs=[
-            pl.BlockSpec((1, HD, tok), lambda i: (i, 0, 0)),
-            pl.BlockSpec((1, 1, tok), lambda i: (i, 0, 0)),
+        partial(attend_kernel, n, slots, tok, 2),
+        in_specs=[vmem] * 2,
+        out_specs=[vmem] * 4,
+        out_shape=[
+            jax.ShapeDtypeStruct((slots, n, 3 * HD, tok), BF16),
+            jax.ShapeDtypeStruct(head_shape, BF16),
+            jax.ShapeDtypeStruct(head_shape, BF16),
+            jax.ShapeDtypeStruct((slots, n, 1, tok), F32),
         ],
-        out_shape=[
-            jax.ShapeDtypeStruct((n, HD, tok), BF16),
-            jax.ShapeDtypeStruct((n, 1, tok), F32),
+        scratch_shapes=[
+            pltpu.VMEM((length, HD), BF16),
+            dma(slots - 1, n - 1),
+            dma(slots - 1, n),
+            dma(slots, n - 1),
+            dma(slots, n),
         ],
-        scratch_shapes=[pltpu.VMEM((length, HD), BF16)],
-        compiler_params=pltpu.CompilerParams(vmem_limit_bytes=VMEM_LIMIT),
+        compiler_params=pltpu.CompilerParams(vmem_limit_bytes=VMEM_LIMIT, collective_id=3, has_side_effects=True),
         cost_estimate=pl.CostEstimate(
-            flops=16 * length * length * HD, bytes_accessed=8 * length * HD, transcendentals=length * length
+            flops=16 * slots * length * length * HD, bytes_accessed=10**7, transcendentals=slots * length * length
         ),
         name="attend",
-    )(x)
+    )(first, rest)
 
 
 def attend_back_kernel(
-    n, tok, sub, x_ref, g_ref, o_ref, lse_ref, cos_ref, sin_ref, out_ref, k_ref, v_ref, dk_ref, dv_ref
+    n,
+    slots,
+    tok,
+    sub,
+    x_ref,
+    sent_ref,
+    o_ref,
+    lse_ref,
+    cos_ref,
+    sin_ref,
+    out_ref,
+    g_ref,
+    d_ref,
+    k_ref,
+    v_ref,
+    dk_ref,
+    dv_ref,
+    g_s,
+    g_r,
+    q_s,
+    q_r,
+    kv_s,
+    kv_r,
 ):
-    step = pl.program_id(0)
+    z = lax.axis_index("seq")
     half = HD // 2
-
-    @pl.when(step == 0)
-    def _():
-        for c in range(n):
-            k_ref[c * tok : (c + 1) * tok, :] = x_ref[c, HD : 2 * HD, :].T
-            v_ref[c * tok : (c + 1) * tok, :] = x_ref[c, 2 * HD : 3 * HD, :].T
-        dk_ref[...] = jnp.zeros_like(dk_ref)
-        dv_ref[...] = jnp.zeros_like(dv_ref)
+    greet_seq(z, n)
+
+    def g_copy(s, i):
+        peer = lax.rem(z + 1 + i, n)
+        return remote(sent_ref.at[s, peer], g_ref.at[s, z], g_s.at[s, i], g_r.at[s, z], seq=peer)
+
+    def g_arrival(s, i):
+        peer = lax.rem(z + 1 + i, n)
+        return remote(sent_ref.at[s, peer], g_ref.at[s, peer], g_s.at[s, i], g_r.at[s, peer], seq=peer)
+
+    def part_copy(s, i, rows, send, recv, arrival):
+        peer = lax.rem(z + 1 + i, n)
+        slot = peer if arrival else z
+        return remote(
+            d_ref.at[s, peer, rows], out_ref.at[s, slot, rows], send.at[s, i], recv.at[s, slot], seq=peer
+        )
+
+    q_rows, kv_rows = pl.ds(0, HD), pl.ds(HD, 2 * HD)
+    q_copy = lambda s, i, arrival=False: part_copy(s, i, q_rows, q_s, q_r, arrival)
+    kv_copy = lambda s, i, arrival=False: part_copy(s, i, kv_rows, kv_s, kv_r, arrival)
+
+    for s in range(slots):
+        each(n - 1, lambda i: g_copy(s, i).start())
+        g_ref[s, z] = sent_ref[s, z]
 
     scale = LOG2E / math.sqrt(HD)
     width = tok // sub
@@ -434,57 +558,89 @@
         a, b = grad[:half], grad[half:]
         return (a * cosine + b * sine).astype(BF16), (b * cosine - a * sine).astype(BF16)
 
-    for i in range(sub):
-        cols = slice(i * width, (i + 1) * width)
-        q = x_ref[step, 0:HD, cols]
-        g = g_ref[step, :, cols]
-        o = o_ref[step, :, cols]
-        centre = jnp.sum(g.astype(F32) * o.astype(F32), axis=0, keepdims=True)
-        s = mm(k_ref[...], q, 1, 0)
-        dp = mm(v_ref[...], g, 1, 0)
-        p = jnp.exp2(s * scale - lse_ref[step, :, cols])
-        p_low = p.astype(BF16)
-        ds = (p * (dp - centre)).astype(BF16)
-        dv_ref[...] += mm(g, p_low, 1, 1)
-        dk_ref[...] += mm(q, ds, 1, 1)
-        dq = None
+    def slot(s):
         for c in range(n):
-            part = mm(x_ref[c, HD : 2 * HD, :], ds[c * tok : (c + 1) * tok], 1, 0)
-            dq = part if dq is None else dq + part
-        dq = dq * (1.0 / math.sqrt(HD))
-        a, b = turn_back(dq, cos_ref[step, :, cols], sin_ref[step, :, cols])
-        out_ref[step, 0:half, cols] = a
-        out_ref[step, half:HD, cols] = b
-
-    @pl.when(step == n - 1)
-    def _():
+            k_ref[c * tok : (c + 1) * tok, :] = x_ref[s, c, HD : 2 * HD, :].T
+            v_ref[c * tok : (c + 1) * tok, :] = x_ref[s, c, 2 * HD : 3 * HD, :].T
+        dk_ref[...] = jnp.zeros_like(dk_ref)
+        dv_ref[...] = jnp.zeros_like(dv_ref)
+        each(n - 1, lambda i: g_arrival(s, i).wait_recv())
+
+        def shard(i):
+            step = lax.rem(z + 1 + i, n)
+            for j in range(sub):
+                cols = slice(j * width, (j + 1) * width)
+                q = x_ref[s, step, 0:HD, cols]
+                g = g_ref[s, step, :, cols]
+                o = o_ref[s, step, :, cols]
+                centre = jnp.sum(g.astype(F32) * o.astype(F32), axis=0, keepdims=True)
+                score = mm(k_ref[...], q, 1, 0)
+                dp = mm(v_ref[...], g, 1, 0)
+                p = jnp.exp2(score * scale - lse_ref[s, step, :, cols])
+                p_low = p.astype(BF16)
+                ds = (p * (dp - centre)).astype(BF16)
+                dv_ref[...] += mm(g, p_low, 1, 1)
+                dk_ref[...] += mm(q, ds, 1, 1)
+                dq = None
+                for c in range(n):
+                    part = mm(x_ref[s, c, HD : 2 * HD, :], ds[c * tok : (c + 1) * tok], 1, 0)
+                    dq = part if dq is None else dq + part
+                dq = dq * (1.0 / math.sqrt(HD))
+                a, b = turn_back(dq, cos_ref[step, :, cols], sin_ref[step, :, cols])
+                d_ref[s, step, 0:half, cols] = a
+                d_ref[s, step, half:HD, cols] = b
+
+            @pl.when(i < n - 1)
+            def _():
+                q_copy(s, i).start()
+
+        each(n, shard)
         for c in range(n):
             dk = dk_ref[:, c * tok : (c + 1) * tok] * (1.0 / math.sqrt(HD))
             a, b = turn_back(dk, cos_ref[c], sin_ref[c])
-            out_ref[c, HD : HD + half, :] = a
-            out_ref[c, HD + half : 2 * HD, :] = b
-            out_ref[c, 2 * HD : 3 * HD, :] = dv_ref[:, c * tok : (c + 1) * tok].astype(BF16)
+            d_ref[s, c, HD : HD + half, :] = a
+            d_ref[s, c, HD + half : 2 * HD, :] = b
+            d_ref[s, c, 2 * HD : 3 * HD, :] = dv_ref[:, c * tok : (c + 1) * tok].astype(BF16)
+        each(n - 1, lambda i: kv_copy(s, i).start())
+        out_ref[s, z] = d_ref[s, z]
+
+    each(slots, slot)
+
+    def drain(s):
+        def one(i):
+            q_copy(s, i, True).wait_recv()
+            kv_copy(s, i, True).wait_recv()
+            g_copy(s, i).wait_send()
+            q_copy(s, i).wait_send()
+            kv_copy(s, i).wait_send()
+
+        each(n - 1, one)
+
+    each(slots, drain)
 
 
 def attend_back(x, g, o, lse, cosine, sine):
-    n, _, tok = x.shape
+    slots, n, _, tok = x.shape
     length = n * tok
-    whole = lambda a: pl.BlockSpec(a.shape, lambda i: (0,) * a.ndim)
+    vmem = pl.BlockSpec(memory_space=pltpu.VMEM)
+    dma = lambda *shape: pltpu.SemaphoreType.DMA(shape)
     return pl.pallas_call(
-        partial(attend_back_kernel, n, tok, 2),
-        grid=(n,),
-        in_specs=[whole(a) for a in (x, g, o, lse, cosine, sine)],
-        out_specs=whole(x),
+        partial(attend_back_kernel, n, slots, tok, 2),
+        in_specs=[vmem] * 6,
+        out_specs=vmem,
         out_shape=jax.ShapeDtypeStruct(x.shape, BF16),
         scratch_shapes=[
+            pltpu.VMEM(g.shape, BF16),
+            pltpu.VMEM(x.shape, BF16),
             pltpu.VMEM((length, HD), BF16),
             pltpu.VMEM((length, HD), BF16),
             pltpu.VMEM((HD, length), F32),
             pltpu.VMEM((HD, length), F32),
-        ],
-        compiler_params=pltpu.CompilerParams(vmem_limit_bytes=VMEM_LIMIT),
+        ]
+        + [dma(slots, n - 1), dma(slots, n)] * 3,
+        compiler_params=pltpu.CompilerParams(vmem_limit_bytes=VMEM_LIMIT, collective_id=4, has_side_effects=True),
         cost_estimate=pl.CostEstimate(
-            flops=40 * length * length * HD, bytes_accessed=16 * length * HD, transcendentals=length * length
+            flops=40 * slots * length * length * HD, bytes_accessed=10**7, transcendentals=slots * length * length
         ),
         name="attend_back",
     )(x, g, o, lse, cosine, sine)
@@ -495,8 +651,6 @@
 
 
 def middle_kernel(
-    n,
-    slots,
     blocks,
     tokens_ref,
     cot_ref,
@@ -505,11 +659,19 @@
     up_ref,
     down_ref,
     out_w_ref,
-    *refs,
+    mixed_ref,
+    output_ref,
+    grad_hidden_ref,
+    sums_ref,
+    bias_grad_ref,
+    g_down_ref,
+    g_pack_ref,
+    grad_mixed_ref,
+    attn_out_ref,
+    mlp_in_ref,
+    low_ref,
+    back_ref,
 ):
-    mixed_refs, refs = refs[:slots], refs[slots:]
-    output_ref, grad_hidden_ref, sums_ref, bias_grad_ref, g_down_ref, g_pack_ref, *refs = refs
-    grad_mixed_refs, (mixed_ref, attn_out_ref, mlp_in_ref, low_ref, back_ref) = refs[:slots], refs[slots:]
     j = pl.program_id(0)
     tok, width = tokens_ref.shape
     gate_attn, shift, scale, gate, gain, down_bias = (vec_ref[i : i + 1, :] for i in range(6))
@@ -518,10 +680,6 @@
 
     @pl.when(j == 0)
     def _():
-        for s in range(slots):
-            for c in range(n):
-                head = s * n + c
-                mixed_ref[head * HD : (head + 1) * HD, :] = mixed_refs[s][c]
         attn_out_ref[...] = mm(mixed_ref[...], out_w_ref[...], 0, 0)
 
         def prepare(i, _):
@@ -577,26 +735,19 @@
             sums_ref[i : i + 1, :] = sums[i]
         attn_low = low_ref[...]
         g_pack_ref[...] = mm(mixed_ref[...], attn_low, 1, 0).astype(BF16)
-        grad_mixed = mm(out_w_ref[...], attn_low, 1, 1).astype(BF16)
-        for s in range(slots):
-            for c in range(n):
-                head = s * n + c
-                grad_mixed_refs[s][c] = grad_mixed[head * HD : (head + 1) * HD]
+        grad_mixed_ref[...] = mm(out_w_ref[...], attn_low, 1, 1).astype(BF16)
 
 
 def middle(tokens, cot, vectors, up_bias, w_pack, w_down, mixed):
     tok, width = tokens.shape
     ff = w_down.shape[0]
     blocks = ff // width
-    slots = len(mixed)
-    n = mixed[0].shape[0]
     whole = lambda shape: pl.BlockSpec(shape, lambda j: (0,) * len(shape), pipeline_mode=pl.Buffered(1))
     fixed = lambda shape: pl.BlockSpec(shape, lambda j: (0,) * len(shape))
     last = blocks - 1
-    head_shape = mixed[0].shape
     flops = 2 * tok * width * (6 * ff + 3 * width)
     return pl.pallas_call(
-        partial(middle_kernel, n, slots, blocks),
+        partial(middle_kernel, blocks),
         grid=(blocks + 1,),
         in_specs=[
             whole(tokens.shape),
@@ -607,7 +758,7 @@
             pl.BlockSpec((width, width), lambda j: (jnp.minimum(j, last), 0)),
             pl.BlockSpec((width, width), lambda j: (0, blocks), pipeline_mode=pl.Buffered(1)),
         ]
-        + [whole(head_shape)] * slots,
+        + [whole(mixed.shape)],
         out_specs=[
             fixed((tok, width)),
             fixed((tok, width)),
@@ -616,7 +767,7 @@
             pl.BlockSpec((width, width), lambda j: (jnp.minimum(j, last), 0)),
             pl.BlockSpec((width, width), lambda j: (0, j)),
         ]
-        + [fixed(head_shape)] * slots,
+        + [fixed(mixed.shape)],
         out_shape=[
             jax.ShapeDtypeStruct((tok, width), F32),
             jax.ShapeDtypeStruct((tok, width), F32),
@@ -625,9 +776,8 @@
             jax.ShapeDtypeStruct((ff, width), BF16),
             jax.ShapeDtypeStruct((width, ff + width), BF16),
         ]
-        + [jax.ShapeDtypeStruct(head_shape, BF16)] * slots,
+        + [jax.ShapeDtypeStruct(mixed.shape, BF16)],
         scratch_shapes=[
-            pltpu.VMEM((width, tok), BF16),
             pltpu.VMEM((tok, width), F32),
             pltpu.VMEM((tok, width), BF16),
             pltpu.VMEM((tok, width), BF16),
@@ -636,11 +786,11 @@
         compiler_params=pltpu.CompilerParams(vmem_limit_bytes=VMEM_LIMIT),
         cost_estimate=pl.CostEstimate(flops=flops, bytes_accessed=6 * ff * width * 2, transcendentals=tok * ff),
         name="middle",
-    )(tokens, cot, vectors, up_bias, w_pack, w_down, w_pack, *mixed)
+    )(tokens, cot, vectors, up_bias, w_pack, w_down, w_pack, mixed)
 
 
 def reduce_kernel(fs, nz, slots, counts, lengths, *refs):
-    swapped_refs, w_refs, refs = refs[:slots], refs[slots : 2 * slots], refs[2 * slots :]
+    swapped_ref, w_refs, refs = refs[0], refs[1 : 1 + slots], refs[1 + slots :]
     attn_in_ref, tokens_hbm, hidden_hbm, vec_in_ref, sums_ref, up_bias_ref, *refs = refs
     bulk_refs, (mod_t_ref, cond_ref), refs = refs[:2], refs[2:4], refs[4:]
     inputs_out, qkv_out, up_out, out_out, down_out, total_out, mod_w_out, cond_out = refs[:8]
@@ -783,7 +933,7 @@
         for head in range(nz):
             for p in range(3):
                 base = (p * nz + head) * HD
-                row_buf[s, base : base + HD, :] = swapped_refs[s][head, p * HD : (p + 1) * HD, :]
+                row_buf[s, base : base + HD, :] = swapped_ref[s, head, p * HD : (p + 1) * HD, :]
         grad = mm(attn_in_ref[...], row_buf[s], 0, 1).astype(BF16)
         for i in range(fs):
             g_buf[s, i // 2, i % 2] = grad[i * shard : (i + 1) * shard]
@@ -969,7 +1119,7 @@
 def reduce_all(
     grad_rows, weights, attn_in, tokens, grad_hidden, vectors, sums, up_bias_sum, part_pack, part_down, mod_t, cond, mod_cols, fs, nz
 ):
-    slots = len(grad_rows)
+    slots = grad_rows.shape[0]
     tok, width = tokens.shape
     shard = width // fs
     count = lambda a: 3 if a.shape[0] % 48 == 0 else 1
@@ -989,10 +1139,10 @@
     dma = lambda *shape: pltpu.SemaphoreType.DMA(shape)
     qkv_shape = (slots, shard, width)
     triple = [low(*pack.shape), low(*down.shape), low(*qkv_shape)]
-    cols = grad_rows[0].shape[0] * grad_rows[0].shape[1]
+    cols = grad_rows.shape[1] * grad_rows.shape[2]
     inputs_grad, qkv_sum, up_sum, out_sum, down_sum, total, mod_w, cond_grad = pl.pallas_call(
         partial(reduce_kernel, fs, nz, slots, counts, lengths),
-        in_specs=[vmem] * slots + [hbm] * slots + [vmem, hbm, hbm] + [vmem] * 7,
+        in_specs=[vmem] + [hbm] * slots + [vmem, hbm, hbm] + [vmem] * 7,
         out_specs=[vmem] * 8,
         out_shape=[
             jax.ShapeDtypeStruct((tok, width), F32),
@@ -1034,7 +1184,7 @@
         compiler_params=pltpu.CompilerParams(vmem_limit_bytes=VMEM_LIMIT, collective_id=1, has_side_effects=True),
         cost_estimate=pl.CostEstimate(flops=12 * tok * width * cols, bytes_accessed=10**8, transcendentals=0),
         name="reduce_all",
-    )(*grad_rows, *weights, attn_in, tokens, grad_hidden, vectors, sums, up_bias_sum, pack, down, mod_t, cond)
+    )(grad_rows, *weights, attn_in, tokens, grad_hidden, vectors, sums, up_bias_sum, pack, down, mod_t, cond)
     blocks, place = [], 0
     for v in lengths:
         n = -(-v // fs // 128)
@@ -1073,7 +1223,7 @@
     all_angles = inv_freq[None, :, None] * (positions[None, :] + starts[:, None])[:, None, :]
     cos_all, sin_all = jnp.cos(all_angles), jnp.sin(all_angles)
 
-    sent, qkv_slots, attn_in, vectors, up_bias_full, cond_low_all = start(
+    first, rest, qkv_slots, attn_in, vectors, up_bias_full, cond_low_all, pack_own, down_own = start(
         qkv_weight,
         tokens,
         (attn_gain, mlp_gain, up_bias, down_bias),
@@ -1082,37 +1232,18 @@
         mod_bias,
         jnp.cos(own_angles),
         jnp.sin(own_angles),
+        (up_weight, out_weight, down_weight),
         fs,
         n,
     )
-    swap = lambda a: lax.all_to_all(a, "seq", split_axis=0, concat_axis=0, tiled=True)
-    heads = [sent[0]] + [swap(a) for a in sent[1:]]
-    pack_own = jnp.concatenate([up_weight.astype(BF16), out_weight.astype(BF16)], axis=1)
-    down_own = down_weight.astype(BF16)
-    attn_in, pack_own, down_own = lax.optimization_barrier((attn_in, pack_own, down_own))
-    w_pack, down_full = gather(pack_own), gather(down_own)
-
-    mixed_heads, log_totals, mixed_back = [], [], []
-    for x in heads:
-        o, lse = attend(x)
-        mixed_heads.append(o)
-        log_totals.append(lse)
-        mixed_back.append(swap(o))
-    output, grad_hidden, sums, up_bias_sum, g_down, g_pack, *grad_mixed = middle(
-        tokens, cotangent[0], vectors, up_bias_full, w_pack, down_full, mixed_back
+    down_full, w_pack = gather(down_own), gather(pack_own)
+    x, heads_out, mixed, log_totals = attend(first, rest)
+    output, grad_hidden, sums, up_bias_sum, g_down, g_pack, grad_mixed = middle(
+        tokens, cotangent[0], vectors, up_bias_full, w_pack, down_full, mixed.reshape(width, tok)
     )
     scatter = lambda a: lax.psum_scatter(a, "fsdp", scatter_dimension=0, tiled=True)
-    part_down = scatter(g_down)
-    part_pack = scatter(g_pack)
-
-    grad_slots = []
-    for s in range(slots):
-        g = swap(grad_mixed[s])
-        if s == 1:
-            g, part_down = lax.optimization_barrier((g, part_down))
-        grad_slots.append(swap(attend_back(heads[s], g, mixed_heads[s], log_totals[s], cos_all, sin_all)))
-    grad_slots[-1], part_pack = lax.optimization_barrier((grad_slots[-1], part_pack))
-
+    part_down, part_pack = scatter(g_down), scatter(g_pack)
+    grad_slots = attend_back(x, grad_mixed.reshape(heads_out.shape), heads_out, log_totals, cos_all, sin_all)
     mod_cols = mod_weight.shape[1]
     mod_t = jnp.pad(mod_weight.astype(BF16).T.astype(F32), ((0, -mod_cols % 128), (0, 0)))
     inputs_grad, qkv_weight_grad, up_sum, out_sum, down_sum, blocks, mod_weight_grad, cond_grad = reduce_all(

time: 502 us -> 411 us (0.82)
  blocking collectives: 84.3 us -> 0 us
  Pallas kernels: 293 us -> 365 us
  waiting for transfers between devices: 41.8 us -> 2.06 us
  starting transfers between devices: 30.2 us -> 0.16 us
  local copies, waits for them, and re-layouts: 20.9 us -> 15.4 us
    all_to_all x4 -> x0, blocking collectives: 84.3 us -> none  [per_device(): lax.all_to_all(a, 'seq', split_axis=0, concat_axis=0, tiled=True)]
    pallas_call x7 -> x3, Pallas kernels: 175 us -> 239 us  [the longest x1 109 us: attend_back(): pl.pallas_call(partial(attend_back_kernel, n, slots, tok, 2), in_specs=[v...]
    all_to_all x7 -> x0, waiting for transfers between devices: 40.5 us -> none  [per_device(): lax.all_to_all(a, 'seq', split_axis=0, concat_axis=0, tiled=True)]
    all_to_all x7 -> x0, starting transfers between devices: 30.1 us -> none  [per_device(): lax.all_to_all(a, 'seq', split_axis=0, concat_axis=0, tiled=True)]
    pallas_call x1, Pallas kernels: 65.8 us -> 73.1 us  [reduce_all(): pl.pallas_call(partial(reduce_kernel, fs, nz, slots, counts, lengths), in...]
    unnamed x37 -> x18, local copies, waits for them, and re-layouts: 12.6 us -> 9.7 us
  transfers between devices with their start and end apart: 11 -> 4, of which waited for: 3 -> 1; matrix products, arithmetic and copies ran while one was open for 1% -> 2% of each run, Pallas kernels for 27% -> 49%
where the time goes in v5:
time: 411 us; the launch traced here: 403 us
  Pallas kernels  365 us (89%)
  local copies, waits for them, and re-layouts  15.4 us (4%)
  between operations  14.3 us (3%)
  other arithmetic  6.88 us (2%)
    pallas_call x1, Pallas kernels, attend_back(): pl.pallas_call(partial(attend_back_kernel, n, slots, tok, 2), in_specs=[v...  109 us
    pallas_call x1, Pallas kernels, attend(): pl.pallas_call(partial(attend_kernel, n, slots, tok, 2), in_specs=[vmem]...  90.3 us
    pallas_call x1, Pallas kernels, reduce_all(): pl.pallas_call(partial(reduce_kernel, fs, nz, slots, counts, lengths), in...  73.1 us
    pallas_call x1, Pallas kernels, start(): pl.pallas_call(partial(start_kernel, fs, nz, slots), in_specs=[vmem, hbm]...  52.5 us
    pallas_call x1, Pallas kernels, middle(): pl.pallas_call(partial(middle_kernel, blocks), grid=(blocks + 1,), in_spe...  39.7 us
    unnamed x18, local copies, waits for them, and re-layouts  9.7 us
  transfers between devices with their start and end apart: 4, of which 1 were waited for; matrix products, arithmetic and copies ran while one was open for 2% of the time, Pallas kernels for 49%

profile of v5, /device:TPU:0, one launch (start us, length us, event | category | flops | bytes accessed | tf_op | source)
XLA Modules:
  0.0 403.4 jit_solution(3435571454981842831)
XLA Ops:
  7.3 1.1 multiply_sine_fusion.1
  8.4 52.5 %start.1 = (bf16[4,192,768]{2,1,0:T(8,128)(2,1)}, bf16[2,4,192,768]{3,2,1,0:T(8,128)(2,1)}, bf16[3,8,96,768]{3,2,1,0:T(8,128)(2,1)}, bf16[768,768]{1,0:T(8,128)(...) custom-call(f32[96,2304]{1,0:T(8,128)} %refs_0_.1, ...), custom_call_target="tpu_custom_call" | custom-call | flops 2717908992 | bytes 100000000 | tf_op jit(solution)/shard_map/start/pallas_call | solution.py:315
  61.0 0.7 all-gather.3.cloned.1.call-update
  61.7 90.3 %attend.1 = (bf16[3,4,192,768]{3,2,1,0:T(8,128)(2,1)}, bf16[3,4,64,768]{3,2,1,0:T(8,128)(2,1)}, bf16[3,4,64,768]{3,2,1,0:T(8,128)(2,1)}, f32[3,4,1,768]{3,2,1,0:T(1,128)}) custom-call(bf16[4,192,768]{2,1,0:T(8,128)(2,1)} %get-tuple-element.45.first_ref, bf16[2,4,192,768]{3,2,1,0:T(8,128)(2,1)} %get-tuple-element.46.rest_ref), custom_call_target="tpu_custom_call" | custom-call | flops 28991029248 | bytes 10000000 | tf_op jit(solution)/shard_map/attend/pallas_call | solution.py:477
  152.1 39.7 %middle.1 = (f32[768,768]{1,0:T(8,128)}, f32[768,768]{1,0:T(8,128)}, f32[8,768]{1,0:T(8,128)}, f32[4,1,768]{2,1,0:T(1,128)}, bf16[3072,768]{1,0:T(8,128)(2,1)}, ...) custom-call(f32[768,768]{1,0:T(8,128)} %bitcast.36, f32[768,768]{1,0:T(8,128)} %bitcast.34, ...), custom_call_target="tpu_custom_call" | custom-call | flops 24461180928 | bytes 28311552 | tf_op jit(solution)/shard_map/middle/pallas_call | solution.py:749
  191.9 0.5 reduce-scatter.3.cloned.1.call-update
  192.4 1.2 convert_bitcast_fusion
  193.7 0.8 convert.4.refs_12_
  194.5 2.5 multiply_sine_fusion
  197.0 1.9 fusion.2
  198.9 108.9 %attend_back.1.refs_0_ = bf16[3,4,192,768]{3,2,1,0:T(8,128)(2,1)} custom-call(bf16[3,4,192,768]{3,2,1,0:T(8,128)(2,1)} %get-tuple-element.49.x_ref, bf16[3,4,64,768]{3,2,1,0:T(8,128)(2,1)} %bitcast.41, bf16[3,4,64,768]{3,2,1,0:T(8,128)(2,1)} %get-tuple-element.51.o_ref, f32[3,4,1,768]{3,2,1,0:T(1,128)} %get-tuple-element.52.lse_ref, ...), custom_call_target="tpu_custom_call" | custom-call | flops 72477573120 | bytes 10000000 | tf_op jit(solution)/shard_map/attend_back/pallas_call | solution.py:627
  307.8 0.8 reduce-scatter.3.cloned.1.call-done
  308.6 73.1 %reduce_all.1 = (f32[768,768]{1,0:T(8,128)}, f32[96,2304]{1,0:T(8,128)}, f32[96,3072]{1,0:T(8,128)}, f32[96,768]{1,0:T(8,128)}, f32[384,768]{1,0:T(8,128)}, /*in...) custom-call(bf16[3,4,192,768]{3,2,1,0:T(8,128)(2,1)} %attend_back.1.refs_0_, bf16[768,768]{1,0:T(8,128)(2,1)} %bitcast.30, ...), custom_call_target="tpu_custom_call" | custom-call | flops 5435817984 | bytes 100000000 | tf_op jit(solution)/shard_map/reduce_all/pallas_call | solution.py:1143
  381.7 1.3 slice_bitcast_fusion
  382.9 1.3 slice_bitcast_fusion.1
  384.2 1.3 slice_bitcast_fusion.2
  385.5 1.8 copy.26
  387.3 1.2 fusion.1
  388.5 3.3 copy.32
  391.9 0.9 copy.33
  393.0 0.7 copy.34
  393.7 1.0 copy.35
  394.7 0.7 copy-done.1
  395.4 1.0 copy.36
  (25 shorter events, 0.6 us)
Async XLA Ops:
  7.2 144.9 %all-gather.5.cloned.1.call-start = ((), (), s32[]{:S(2)}) async-start(), calls=%async_computation.3 | async-start | bytes 5308416 | tf_op jit(solution)/shard_map/all_gather | solution.py:1217
  60.9 91.1 %all-gather.3.cloned.1.call-start = ((), (), s32[]{:S(2)}) async-start(), calls=%async_computation.2 | async-start | bytes 6635520 | tf_op jit(solution)/shard_map/all_gather | solution.py:1217
  61.7 246.1 %reduce-scatter.5.cloned.1.call-start = ((), (), s32[]{:S(2)}) async-start(), calls=%async_computation.5 | async-start | bytes 5308416 | tf_op jit(solution)/shard_map/reduce_scatter | solution.py:1244
  191.8 116.7 %reduce-scatter.3.cloned.1.call-start = ((), (), s32[]{:S(2)}) async-start(), calls=%async_computation.4 | async-start | bytes 6635520 | tf_op jit(solution)/shard_map/reduce_scatter | solution.py:1244
  191.9 5.1 %copy-start = (bf16[3,8,96,768]{3,2,1,0:T(8,128)(2,1)S(1)}, bf16[3,8,96,768]{3,2,1,0:T(8,128)(2,1)}, u32[]{:S(2)}) copy-start(bf16[3,8,96,768]{3,2,1,0:T(8,128)(2,1)} %get-tuple-element.53) | copy-start | bytes 10616836
  308.6 78.8 %copy-start.5 = (f32[1,128]{1,0:T(1,128)S(1)}, f32[1,128]{1,0:T(1,128)}, u32[]{:S(2)}) copy-start(f32[1,128]{1,0:T(1,128)} %refs_6_.1) | copy-start | bytes 1540
  388.5 3.3 copy-start.3
  391.8 1.1 copy-start.4
  391.9 1.8 copy-start.2
  393.7 1.7 copy-start.1
Sparse Core Ops, SparseCore 0:
  61.0 44.2 all-gather.4
  107.2 43.7 all-gather.2
  192.0 53.5 reduce-scatter.4
  248.8 59.6 reduce-scatter.2

commit v6 on v5

--- a/solution.py
+++ b/solution.py
@@ -191,8 +191,6 @@
         each(pairs - 1, step)
 
     send_weight(0)
-    for s in range(1, slots - 1):
-        send_weight(s)
 
     each(fs - 1, lambda i: small_arrival(i).wait_recv())
     small_sum = jnp.sum(small_all[:, :, : 3 * width + ff], axis=0)
@@ -216,7 +214,8 @@
         return remote(mod_send.at[peer], mod_recv.at[peer], mod_s.at[i], mod_r.at[peer], fsdp=peer)
 
     each(fs - 1, lambda i: mod_copy(i).start())
-    send_weight(slots - 1)
+    for s in range(1, slots):
+        send_weight(s)
     pass_weight(0)
 
     attn_gain, mlp_gain, down_bias = (small_sum[:, i * width : (i + 1) * width] for i in range(3))
@@ -272,9 +271,12 @@
     project(0, z_send)
     each(nz - 1, lambda i: z_copy(i).start())
     heads_ref[z] = z_send[z]
-    for s in range(1, slots):
-        pass_weight(s)
-        project(s, rest_ref.at[s - 1])
+
+    def later(i):
+        pass_weight(i + 1)
+        project(i + 1, rest_ref.at[i])
+
+    each(slots - 1, later)
 
     pack_out[:, :ff] = up_buf[...].astype(BF16)
     pack_out[:, ff:] = out_buf[...].astype(BF16)
@@ -790,8 +792,7 @@
 
 
 def reduce_kernel(fs, nz, slots, counts, lengths, *refs):
-    swapped_ref, w_refs, refs = refs[0], refs[1 : 1 + slots], refs[1 + slots :]
-    attn_in_ref, tokens_hbm, hidden_hbm, vec_in_ref, sums_ref, up_bias_ref, *refs = refs
+    swapped_ref, w_hbm, attn_in_ref, tokens_hbm, hidden_hbm, vec_in_ref, sums_ref, up_bias_ref, *refs = refs
     bulk_refs, (mod_t_ref, cond_ref), refs = refs[:2], refs[2:4], refs[4:]
     inputs_out, qkv_out, up_out, out_out, down_out, total_out, mod_w_out, cond_out = refs[:8]
     (
@@ -853,9 +854,8 @@
     shard = g_buf.shape[3]
     groups = width // 128
 
-    loads = [pltpu.make_async_copy(w_refs[s], w_buf.at[s], local_s.at[s]) for s in range(slots)]
-    loads.append(pltpu.make_async_copy(tokens_hbm, tokens_buf, local_s.at[slots]))
-    loads.append(pltpu.make_async_copy(hidden_hbm, hidden_buf, local_s.at[slots + 1]))
+    fetch = ((w_hbm, w_buf), (tokens_hbm, tokens_buf), (hidden_hbm, hidden_buf))
+    loads = [pltpu.make_async_copy(src, dst, local_s.at[i]) for i, (src, dst) in enumerate(fetch)]
     for load in loads:
         load.start()
     greet(me, z, fs, nz)
@@ -913,11 +913,9 @@
                 for step, (n, item) in todo:
                     step(n, item)
 
-    half = len(early) // 2
-
     @pl.when(outer)
     def _():
-        for n, item in early[:half]:
+        for n, item in early:
             up_copy(n, item).start()
 
     def pair_copy(s, j):
@@ -929,7 +927,7 @@
     def peer_arrival(s, j):
         return remote(sum_buf.at[s, j], recv_buf.at[s, j], peer_s.at[s, j], peer_r.at[s, j], fsdp=2 * j + c)
 
-    for s in range(slots):
+    def project_grad(s):
         for head in range(nz):
             for p in range(3):
                 base = (p * nz + head) * HD
@@ -939,6 +937,8 @@
             g_buf[s, i // 2, i % 2] = grad[i * shard : (i + 1) * shard]
         each(pairs, lambda i: pair_copy(s, lax.rem(k + 1 + i, pairs)).start())
 
+    each(slots, project_grad)
+
     advance(1)
 
     def forward(i):
@@ -955,9 +955,10 @@
     scale_mlp, gate_mlp, mlp_gain = (vec_in_ref[i : i + 1, :] for i in (2, 3, 4))
     attn_gain, scale_attn = (vec_in_ref[i : i + 1, :] for i in (6, 7))
     piece = min(256, tok)
-    back_sum = hat_sum = jnp.zeros((1, width), F32)
-    for i in range(tok // piece):
-        rows = slice(i * piece, (i + 1) * piece)
+
+    def norm_piece(i, kept):
+        back_sum, hat_sum = kept
+        rows = pl.ds(pl.multiple_of(i * piece, piece), piece)
         grad = None
         for s in range(slots):
             part = mm(row_buf[s, :, rows], w_buf[s], 0, 1)
@@ -967,7 +968,10 @@
         inputs_out[rows, :] = hidden_buf[rows, :] + norm_back(scaled, hat, inv)
         back_sum = back_sum + jnp.sum(grad, axis=0, keepdims=True)
         hat_sum = hat_sum + jnp.sum(grad * hat, axis=0, keepdims=True)
-        advance(2)
+        return back_sum, hat_sum
+
+    zero = jnp.zeros((1, width), F32)
+    back_sum, hat_sum = lax.fori_loop(0, tok // piece, norm_piece, (zero, zero))
 
     sums = [sums_ref[i : i + 1, :] for i in range(5)]
     vectors = [back_sum, hat_sum * attn_gain, sums[0], sums[1], sums[2] * mlp_gain, sums[3]]
@@ -990,12 +994,23 @@
 
     each(nz - 1, lambda i: vecz_copy(i).start())
 
-    @pl.when(outer)
-    def _():
-        for n, item in early[half:]:
-            up_copy(n, item).start()
-
-    advance(2)
+    advance(len(steps))
+    for s in range(slots):
+        pair_copy(s, k).wait_recv()
+        own = g_buf[s, k, c].astype(F32) + pair_buf[s, k].astype(F32)
+
+        def gather_in(i, acc):
+            j = lax.rem(k + 1 + i, pairs)
+            peer_arrival(s, j).wait_recv()
+            return acc + recv_buf[s, j].astype(F32)
+
+        own_buf[s] = lax.fori_loop(0, pairs - 1, gather_in, own).astype(BF16)
+
+        @pl.when(outer)
+        def _():
+            up_copy(*late[s]).start()
+
+    steps.extend(plan(late))
     each(nz - 1, lambda i: vecz_arrival(i).wait_recv())
     summed = vec_z[0]
     for i in range(1, nz):
@@ -1011,22 +1026,7 @@
         return remote(vec_own, vec_all.at[peer], vec_s.at[i], vec_r.at[peer], fsdp=peer)
 
     each(fs - 1, lambda i: vec_copy(i).start())
-    advance(len(steps))
-
-    for s in range(slots):
-        pair_copy(s, k).wait_recv()
-        own = g_buf[s, k, c].astype(F32) + pair_buf[s, k].astype(F32)
-
-        def gather_in(i, acc):
-            j = lax.rem(k + 1 + i, pairs)
-            peer_arrival(s, j).wait_recv()
-            return acc + recv_buf[s, j].astype(F32)
-
-        own_buf[s] = lax.fori_loop(0, pairs - 1, gather_in, own).astype(BF16)
-
-        @pl.when(outer)
-        def _():
-            up_copy(*late[s]).start()
+    advance(3)
 
     each(fs - 1, lambda i: vec_arrival(i).wait_recv())
     lane_from = lax.broadcasted_iota(jnp.int32, (256, 128), 0)
@@ -1046,15 +1046,17 @@
             place += 1
             if which > 0:
                 continue
+            wide = min(128, block - i * 128)
+            columns = slice(i * 128, i * 128 + wide)
+            mod_rows = mod_t_ref[columns, :].astype(BF16).astype(F32)
             share = lax.dot_general(
-                rows, mod_t_ref[i], (((1,), (0,)), ((), ())), precision=HIGHEST, preferred_element_type=F32
+                rows[:, :wide], mod_rows, (((1,), (0,)), ((), ())), precision=HIGHEST, preferred_element_type=F32
             )
             part = share if part is None else part + share
             outer_product = lax.dot_general(
-                cond_ref[...], rows, (((0,), (0,)), ((), ())), precision=HIGHEST, preferred_element_type=F32
+                rows, cond_ref[...], (((0,), (0,)), ((), ())), precision=HIGHEST, preferred_element_type=F32
             )
-            wide = min(128, block - i * 128)
-            mod_w_out[:, i * 128 : i * 128 + wide] = outer_product[:, :wide]
+            mod_w_out[columns, :] = outer_product[:wide]
         first += length // 128
     cond_send[...] = jnp.broadcast_to(part[:, None, :], cond_send.shape)
 
@@ -1067,7 +1069,6 @@
         return remote(cond_send.at[peer], cond_recv.at[peer], cond_s.at[i], cond_r.at[peer], fsdp=peer)
 
     each(fs - 1, lambda i: cond_copy(i).start())
-    steps.extend(plan(late))
     advance(len(steps))
     cond_recv[me] = cond_send[me]
     each(fs - 1, lambda i: cond_arrival(i).wait_recv())
@@ -1081,12 +1082,17 @@
 
     block = nz * HD
     ff = up_out.shape[1]
-    for i in range(counts[0]):
-        rows = slice(i * tot_pack.shape[1], (i + 1) * tot_pack.shape[1])
+
+    def write_pack(i):
+        rows = pl.ds(i * tot_pack.shape[1], tot_pack.shape[1])
         up_out[rows, :] = tot_pack[i, :, :ff].astype(F32)
         out_out[rows, :] = tot_pack[i, :, ff:].astype(F32)
-    for i in range(counts[1]):
-        down_out[i * tot_down.shape[1] : (i + 1) * tot_down.shape[1], :] = tot_down[i].astype(F32)
+
+    def write_down(i):
+        down_out[pl.ds(i * tot_down.shape[1], tot_down.shape[1]), :] = tot_down[i].astype(F32)
+
+    each(counts[0], write_pack)
+    each(counts[1], write_down)
     for s in range(slots):
         for p in range(3):
             columns = slice(p * width + s * block, p * width + (s + 1) * block)
@@ -1117,7 +1123,7 @@
 
 
 def reduce_all(
-    grad_rows, weights, attn_in, tokens, grad_hidden, vectors, sums, up_bias_sum, part_pack, part_down, mod_t, cond, mod_cols, fs, nz
+    grad_rows, weights, attn_in, tokens, grad_hidden, vectors, sums, up_bias_sum, part_pack, part_down, mod_t, cond, fs, nz
 ):
     slots = grad_rows.shape[0]
     tok, width = tokens.shape
@@ -1142,7 +1148,7 @@
     cols = grad_rows.shape[1] * grad_rows.shape[2]
     inputs_grad, qkv_sum, up_sum, out_sum, down_sum, total, mod_w, cond_grad = pl.pallas_call(
         partial(reduce_kernel, fs, nz, slots, counts, lengths),
-        in_specs=[vmem] + [hbm] * slots + [vmem, hbm, hbm] + [vmem] * 7,
+        in_specs=[vmem, hbm, vmem, hbm, hbm] + [vmem] * 7,
         out_specs=[vmem] * 8,
         out_shape=[
             jax.ShapeDtypeStruct((tok, width), F32),
@@ -1151,7 +1157,7 @@
             jax.ShapeDtypeStruct((shard, part_pack.shape[1] - ff), F32),
             jax.ShapeDtypeStruct(part_down.shape, F32),
             jax.ShapeDtypeStruct((places, 128), F32),
-            jax.ShapeDtypeStruct((cond.shape[1], mod_cols), F32),
+            jax.ShapeDtypeStruct(mod_t.shape, F32),
             jax.ShapeDtypeStruct((8, 128), F32),
         ],
         scratch_shapes=[
@@ -1173,7 +1179,7 @@
             wide(fs, rows, 128),
             wide(fs, 8, 128),
             wide(fs, 8, 128),
-            dma(slots + 2),
+            dma(3),
             dma(slots, pairs),
             dma(slots, pairs),
             dma(slots, pairs),
@@ -1184,13 +1190,13 @@
         compiler_params=pltpu.CompilerParams(vmem_limit_bytes=VMEM_LIMIT, collective_id=1, has_side_effects=True),
         cost_estimate=pl.CostEstimate(flops=12 * tok * width * cols, bytes_accessed=10**8, transcendentals=0),
         name="reduce_all",
-    )(grad_rows, *weights, attn_in, tokens, grad_hidden, vectors, sums, up_bias_sum, pack, down, mod_t, cond)
+    )(grad_rows, weights, attn_in, tokens, grad_hidden, vectors, sums, up_bias_sum, pack, down, mod_t, cond)
     blocks, place = [], 0
     for v in lengths:
         n = -(-v // fs // 128)
         blocks.append(total[place : place + n].reshape(-1)[: v // fs])
         place += n
-    return inputs_grad, qkv_sum, up_sum, out_sum, down_sum, blocks, mod_w, cond_grad
+    return inputs_grad, qkv_sum, up_sum, out_sum, down_sum, blocks, mod_w.T, cond_grad
 
 
 def per_device(
@@ -1244,11 +1250,9 @@
     scatter = lambda a: lax.psum_scatter(a, "fsdp", scatter_dimension=0, tiled=True)
     part_down, part_pack = scatter(g_down), scatter(g_pack)
     grad_slots = attend_back(x, grad_mixed.reshape(heads_out.shape), heads_out, log_totals, cos_all, sin_all)
-    mod_cols = mod_weight.shape[1]
-    mod_t = jnp.pad(mod_weight.astype(BF16).T.astype(F32), ((0, -mod_cols % 128), (0, 0)))
     inputs_grad, qkv_weight_grad, up_sum, out_sum, down_sum, blocks, mod_weight_grad, cond_grad = reduce_all(
         grad_slots,
-        [qkv_slots[s].reshape(width, -1) for s in range(slots)],
+        qkv_slots.reshape(slots, width, -1),
         attn_in,
         tokens,
         grad_hidden,
@@ -1257,9 +1261,8 @@
         up_bias_sum,
         part_pack,
         part_down,
-        mod_t.reshape(-1, 128, mod_weight.shape[0]),
+        mod_weight.T,
         cond_low_all,
-        mod_cols,
         fs,
         n,
     )

time: 411 us -> 391 us (0.951); the launches traced: 403 us -> 390 us
  Pallas kernels: 365 us -> 353 us
  waiting for transfers between devices: 2.06 us -> 6.42 us
    pallas_call x1, Pallas kernels: 52.5 us -> 46.2 us  [start(): pl.pallas_call(partial(start_kernel, fs, nz, slots), in_specs=[vmem, hbm]...]
    reduce_scatter x2, waiting for transfers between devices: 0.78 us -> 5.13 us  [per_device(): lax.psum_scatter(a, 'fsdp', scatter_dimension=0, tiled=True)]
    pallas_call x1, Pallas kernels: 73.1 us -> 68.9 us  [reduce_all(): pl.pallas_call(partial(reduce_kernel, fs, nz, slots, counts, lengths), in...]
  transfers between devices with their start and end apart: 4 -> 4, of which waited for: 1 -> 1; matrix products, arithmetic and copies ran while one was open for 2% -> 1% of each run, Pallas kernels for 49% -> 51%
where the time goes in v6:
time: 391 us; the launch traced here: 390 us
  Pallas kernels  353 us (90%)
  between operations  13.9 us (4%)
  local copies, waits for them, and re-layouts  11.6 us (3%)
  waiting for transfers between devices  6.42 us (2%)
  other arithmetic  4.87 us (1%)
    pallas_call x1, Pallas kernels, attend_back(): pl.pallas_call(partial(attend_back_kernel, n, slots, tok, 2), in_specs=[v...  108 us
    pallas_call x1, Pallas kernels, attend(): pl.pallas_call(partial(attend_kernel, n, slots, tok, 2), in_specs=[vmem]...  90.2 us
    pallas_call x1, Pallas kernels, reduce_all(): pl.pallas_call(partial(reduce_kernel, fs, nz, slots, counts, lengths), in...  68.9 us
    pallas_call x1, Pallas kernels, start(): pl.pallas_call(partial(start_kernel, fs, nz, slots), in_specs=[vmem, hbm]...  46.2 us
    pallas_call x1, Pallas kernels, middle(): pl.pallas_call(partial(middle_kernel, blocks), grid=(blocks + 1,), in_spe...  39.7 us
  transfers between devices with their start and end apart: 4, of which 1 were waited for; matrix products, arithmetic and copies ran while one was open for 1% of the time, Pallas kernels for 51%

profile of v6, /device:TPU:0, one launch (start us, length us, event | category | flops | bytes accessed | tf_op | source)
XLA Modules:
  0.0 390.3 jit_solution(1328606868848628298)
XLA Ops:
  7.3 1.1 multiply_sine_fusion.1
  8.4 46.2 %start.1 = (bf16[4,192,768]{2,1,0:T(8,128)(2,1)}, bf16[2,4,192,768]{3,2,1,0:T(8,128)(2,1)}, bf16[3,8,96,768]{3,2,1,0:T(8,128)(2,1)}, bf16[768,768]{1,0:T(8,128)(...) custom-call(f32[96,2304]{1,0:T(8,128)} %refs_0_.1, ...), custom_call_target="tpu_custom_call" | custom-call | flops 2717908992 | bytes 100000000 | tf_op jit(solution)/shard_map/start/pallas_call | solution.py:317
  54.6 0.0 all-gather.3.cloned.1.call-start
  54.6 0.7 all-gather.3.cloned.1.call-update
  55.3 0.0 reduce-scatter.5.cloned.1.call-start
  55.4 90.2 %attend.1 = (bf16[3,4,192,768]{3,2,1,0:T(8,128)(2,1)}, bf16[3,4,64,768]{3,2,1,0:T(8,128)(2,1)}, bf16[3,4,64,768]{3,2,1,0:T(8,128)(2,1)}, f32[3,4,1,768]{3,2,1,0:T(1,128)}) custom-call(bf16[4,192,768]{2,1,0:T(8,128)(2,1)} %get-tuple-element.45.first_ref, bf16[2,4,192,768]{3,2,1,0:T(8,128)(2,1)} %get-tuple-element.46.rest_ref), custom_call_target="tpu_custom_call" | custom-call | flops 28991029248 | bytes 10000000 | tf_op jit(solution)/shard_map/attend/pallas_call | solution.py:479
  145.6 39.7 %middle.1 = (f32[768,768]{1,0:T(8,128)}, f32[768,768]{1,0:T(8,128)}, f32[8,768]{1,0:T(8,128)}, f32[4,1,768]{2,1,0:T(1,128)}, bf16[3072,768]{1,0:T(8,128)(2,1)}, ...) custom-call(f32[768,768]{1,0:T(8,128)} %bitcast.27, f32[768,768]{1,0:T(8,128)} %bitcast.25, ...), custom_call_target="tpu_custom_call" | custom-call | flops 24461180928 | bytes 28311552 | tf_op jit(solution)/shard_map/middle/pallas_call | solution.py:751
  185.4 0.0 reduce-scatter.3.cloned.1.call-start
  185.4 0.5 reduce-scatter.3.cloned.1.call-update
  186.0 0.1 iota_add_fusion
  186.1 2.5 multiply_sine_fusion
  188.5 108.5 %attend_back.1.refs_0_ = bf16[3,4,192,768]{3,2,1,0:T(8,128)(2,1)} custom-call(bf16[3,4,192,768]{3,2,1,0:T(8,128)(2,1)} %get-tuple-element.49.x_ref, bf16[3,4,64,768]{3,2,1,0:T(8,128)(2,1)} %bitcast.35, bf16[3,4,64,768]{3,2,1,0:T(8,128)(2,1)} %get-tuple-element.51.o_ref, f32[3,4,1,768]{3,2,1,0:T(1,128)} %get-tuple-element.52.lse_ref, ...), custom_call_target="tpu_custom_call" | custom-call | flops 72477573120 | bytes 10000000 | tf_op jit(solution)/shard_map/attend_back/pallas_call | solution.py:629
  297.0 5.1 %reduce-scatter.3.cloned.1.call-done = bf16[96,3840]{1,0:T(8,128)(2,1)} async-done(((bf16[768,3840]{1,0:T(8,128)(2,1)}), bf16[96,3840]{1,0:T(8,128)(2,1)}) %reduce-scatter.3.cloned.1.call-update) | async-done | bytes 737296 | tf_op jit(solution)/shard_map/reduce_scatter | solution.py:1250
  302.1 68.9 %reduce_all.1 = (f32[768,768]{1,0:T(8,128)}, f32[96,2304]{1,0:T(8,128)}, f32[96,3072]{1,0:T(8,128)}, f32[96,768]{1,0:T(8,128)}, f32[384,768]{1,0:T(8,128)}, /*in...) custom-call(bf16[3,4,192,768]{3,2,1,0:T(8,128)(2,1)} %attend_back.1.refs_0_, bf16[3,768,768]{2,1,0:T(8,128)(2,1)} %bitcast.33, ...), custom_call_target="tpu_custom_call" | custom-call | flops 5435817984 | bytes 100000000 | tf_op jit(solution)/shard_map/reduce_all/pallas_call | solution.py:1149
  371.0 1.3 slice_bitcast_fusion
  372.3 1.3 slice_bitcast_fusion.1
  373.5 1.3 slice_bitcast_fusion.2
  374.8 1.2 fusion.1
  376.0 3.4 copy.32
  379.4 0.9 copy.33
  380.3 0.7 copy.34
  381.0 1.0 copy.35
  382.0 1.0 copy.36
  383.1 0.7 copy.37
  (21 shorter events, 0.2 us)
Async XLA Ops:
  7.2 138.4 %all-gather.5.cloned.1.call-start = ((), (), s32[]{:S(2)}) async-start(), calls=%async_computation.3 | async-start | bytes 5308416 | tf_op jit(solution)/shard_map/all_gather | solution.py:1223
  54.6 91.0 %all-gather.3.cloned.1.call-start = ((), (), s32[]{:S(2)}) async-start(), calls=%async_computation.2 | async-start | bytes 6635520 | tf_op jit(solution)/shard_map/all_gather | solution.py:1223
  55.3 241.7 %reduce-scatter.5.cloned.1.call-start = ((), (), s32[]{:S(2)}) async-start(), calls=%async_computation.5 | async-start | bytes 5308416 | tf_op jit(solution)/shard_map/reduce_scatter | solution.py:1250
  185.4 116.7 %reduce-scatter.3.cloned.1.call-start = ((), (), s32[]{:S(2)}) async-start(), calls=%async_computation.4 | async-start | bytes 6635520 | tf_op jit(solution)/shard_map/reduce_scatter | solution.py:1250
  302.1 72.7 %copy-start.5 = (f32[1,128]{1,0:T(1,128)S(1)}, f32[1,128]{1,0:T(1,128)}, u32[]{:S(2)}) copy-start(f32[1,128]{1,0:T(1,128)} %refs_6_.1) | copy-start | bytes 1540
  376.0 3.4 copy-start.2
  376.0 4.3 %copy-start.4 = (f32[96,768]{1,0:T(8,128)S(1)}, f32[96,768]{1,0:T(8,128)}, u32[]{:S(2)}) copy-start(f32[96,768]{1,0:T(8,128)} %get-tuple-element.95) | copy-start | bytes 884740
  376.0 5.0 %copy-start.1 = (f32[96,3072]{1,0:T(8,128)S(1)}, f32[96,3072]{1,0:T(8,128)}, u32[]{:S(2)}) copy-start(f32[96,3072]{1,0:T(8,128)} %get-tuple-element.96) | copy-start | bytes 3538948
  379.4 2.7 copy-start
  381.0 2.0 copy-start.3
Sparse Core Ops, SparseCore 0:
  54.7 44.1 all-gather.4
  100.8 43.7 all-gather.2
  185.5 53.5 reduce-scatter.4
  242.5 59.6 reduce-scatter.2

commit v7 on v6

--- a/solution.py
+++ b/solution.py
@@ -69,7 +69,7 @@
     pl.semaphore_wait(barrier, fs + nz - 2)
 
 
-def start_kernel(fs, nz, slots, *refs):
+def forward_kernel(fs, nz, slots, sub, *refs):
     (
         qkv_ref,
         tokens_hbm,
@@ -85,16 +85,18 @@
         up_hbm,
         out_hbm,
         down_hbm,
-        heads_ref,
-        rest_ref,
+        x_ref,
+        o_ref,
+        mixed_ref,
+        lse_ref,
         w_ref,
         attn_in_ref,
         vec_ref,
         bias_ref,
         cond_out,
-        pack_out,
-        down_out,
-    ) = refs[:23]
+        pack_hbm,
+        feed_hbm,
+    ) = refs[:25]
     (
         tokens_buf,
         up_buf,
@@ -118,9 +120,18 @@
         w_s,
         w_f,
         w_r,
-        z_s,
-        z_r,
-    ) = refs[23:]
+        pack_own,
+        feed_own,
+        k_ref,
+        x_s,
+        x_r,
+        o_s,
+        o_r,
+        p_s,
+        p_f,
+        p_r,
+        own_s,
+    ) = refs[25:]
     me = lax.axis_index("fsdp")
     z = lax.axis_index("seq")
     pairs = fs // 2
@@ -260,29 +271,140 @@
                     out_ref[shard_of, part * HD : part * HD + half, :] = (a * cosine - b * sine).astype(BF16)
                     out_ref[shard_of, part * HD + half : (part + 1) * HD, :] = (b * cosine + a * sine).astype(BF16)
 
-    def z_copy(i):
+    def x_copy(s, i):
         peer = lax.rem(z + 1 + i, nz)
-        return remote(z_send.at[peer], heads_ref.at[z], z_s.at[i], z_r.at[z], seq=peer)
-
-    def z_arrival(i):
+        return remote(z_send.at[s, peer], x_ref.at[s, z], x_s.at[s, i], x_r.at[s, z], seq=peer)
+
+    def x_arrival(s, i):
         peer = lax.rem(z + 1 + i, nz)
-        return remote(z_send.at[peer], heads_ref.at[peer], z_s.at[i], z_r.at[peer], seq=peer)
-
-    project(0, z_send)
-    each(nz - 1, lambda i: z_copy(i).start())
-    heads_ref[z] = z_send[z]
+        return remote(z_send.at[s, peer], x_ref.at[s, peer], x_s.at[s, i], x_r.at[s, peer], seq=peer)
+
+    def o_copy(s, i):
+        peer = lax.rem(z + 1 + i, nz)
+        return remote(o_ref.at[s, peer], mixed_ref.at[s, z], o_s.at[s, i], o_r.at[s, z], seq=peer)
+
+    def o_arrival(s, i):
+        peer = lax.rem(z + 1 + i, nz)
+        return remote(o_ref.at[s, peer], mixed_ref.at[s, peer], o_s.at[s, i], o_r.at[s, peer], seq=peer)
+
+    def send_slot(s):
+        project(s, z_send.at[s])
+        each(nz - 1, lambda i: x_copy(s, i).start())
+        x_ref[s, z] = z_send[s, z]
+
+    send_slot(0)
 
     def later(i):
         pass_weight(i + 1)
-        project(i + 1, rest_ref.at[i])
+        send_slot(i + 1)
 
     each(slots - 1, later)
 
-    pack_out[:, :ff] = up_buf[...].astype(BF16)
-    pack_out[:, ff:] = out_buf[...].astype(BF16)
-    down_out[...] = down_buf[...].astype(BF16)
-    each(nz - 1, lambda i: z_arrival(i).wait_recv())
-    each(nz - 1, lambda i: z_copy(i).wait_send())
+    pack_own[:, :ff] = up_buf[...].astype(BF16)
+    pack_own[:, ff:] = out_buf[...].astype(BF16)
+    feed_own[...] = down_buf[...].astype(BF16)
+    bulk = ((pack_own, pack_hbm), (feed_own, feed_hbm))
+
+    def p_peer(a, i):
+        j = lax.rem(k + 1 + i, pairs)
+        own, whole = bulk[a]
+        return remote(own, whole.at[me], p_s.at[a, i], p_r.at[a, me], fsdp=2 * j + c)
+
+    def p_partner(a):
+        own, whole = bulk[a]
+        return remote(own, whole.at[me], p_s.at[a, pairs - 1], p_r.at[a, me], fsdp=partner)
+
+    def p_arrival(a, j):
+        own, whole = bulk[a]
+        return remote(own, whole.at[j], p_s.at[a, 0], p_r.at[a, j], fsdp=partner)
+
+    def p_pass(a, i):
+        j = 2 * lax.rem(k + 1 + i, pairs) + c
+        whole = bulk[a][1]
+        return remote(whole.at[j], whole.at[j], p_f.at[a, i], p_r.at[a, j], fsdp=partner)
+
+    def p_own(a):
+        own, whole = bulk[a]
+        return pltpu.make_async_copy(own, whole.at[me], own_s.at[a])
+
+    for a in range(2):
+        each(pairs - 1, lambda i: p_peer(a, i).start())
+        p_partner(a).start()
+        p_own(a).start()
+
+    def pass_bulk(a):
+        def step(i):
+            p_arrival(a, 2 * lax.rem(k + 1 + i, pairs) + c).wait_recv()
+            p_pass(a, i).start()
+
+        each(pairs - 1, step)
+
+    scale = LOG2E / math.sqrt(HD)
+    part_width = tok // sub
+
+    def soft(s):
+        top = jnp.max(s, axis=0, keepdims=True) * scale
+        p = jnp.exp2(s * scale - top)
+        total = jnp.sum(p, axis=0, keepdims=True)
+        return top, total, p.astype(BF16)
+
+    def slot(s):
+        each(nz - 1, lambda i: x_arrival(s, i).wait_recv())
+        for shard_of in range(nz):
+            k_ref[shard_of * tok : (shard_of + 1) * tok, :] = x_ref[s, shard_of, HD : 2 * HD, :].T
+
+        def one_shard(i):
+            step = lax.rem(z + 1 + i, nz)
+
+            def score(j):
+                q = x_ref[s, step, 0:HD, j * part_width : (j + 1) * part_width]
+                return mm(k_ref[...], q, 1, 0)
+
+            def mix(j, top, total, p):
+                o = None
+                for shard_of in range(nz):
+                    part = mm(x_ref[s, shard_of, 2 * HD : 3 * HD, :], p[shard_of * tok : (shard_of + 1) * tok], 1, 0)
+                    o = part if o is None else o + part
+                o_ref[s, step, :, j * part_width : (j + 1) * part_width] = (o / total).astype(BF16)
+                lse_ref[s, step, :, j * part_width : (j + 1) * part_width] = top + jnp.log2(total)
+
+            scores = [score(0)]
+            pending = None
+            for j in range(sub):
+                if j + 1 < sub:
+                    scores.append(score(j + 1))
+                done = soft(scores[j])
+                if pending is not None:
+                    mix(j - 1, *pending)
+                pending = done
+            mix(sub - 1, *pending)
+
+            @pl.when(i < nz - 1)
+            def _():
+                o_copy(s, i).start()
+
+        each(nz, one_shard)
+        mixed_ref[s, z] = o_ref[s, z]
+
+        @pl.when(s == slots - 2)
+        def _():
+            pass_bulk(0)
+
+    each(slots, slot)
+    pass_bulk(1)
+
+    def drain_slots(s):
+        each(nz - 1, lambda i: o_arrival(s, i).wait_recv())
+        each(nz - 1, lambda i: o_copy(s, i).wait_send())
+        each(nz - 1, lambda i: x_copy(s, i).wait_send())
+
+    each(slots, drain_slots)
+    for a in range(2):
+        each(pairs, lambda j: p_arrival(a, 2 * j + 1 - c).wait_recv())
+        each(pairs - 1, lambda i: p_peer(a, i).wait_send())
+        each(pairs - 1, lambda i: p_pass(a, i).wait_send())
+        p_partner(a).wait_send()
+        p_own(a).wait()
 
     def drain_peers(i):
         small_copy(i).wait_send()
@@ -299,7 +421,7 @@
         w_partner(s).wait_send()
 
 
-def start(qkv_weight, tokens, gains, cond, mod_weight, mod_bias, cosine, sine, feed, fs, nz):
+def forward(qkv_weight, tokens, gains, cond, mod_weight, mod_bias, cosine, sine, feed, fs, nz):
     slots = H // nz
     tok, width = tokens.shape
     shard = qkv_weight.shape[0]
@@ -311,23 +433,27 @@
     low = lambda *shape: pltpu.VMEM(shape, BF16)
     wide = lambda *shape: pltpu.VMEM(shape, F32)
     dma = lambda *shape: pltpu.SemaphoreType.DMA(shape)
-    head_shape = (nz, 3 * HD, tok)
+    head_shape = (slots, nz, 3 * HD, tok)
+    pack_shape = (shard, up.shape[1] + out.shape[1])
+    length = nz * tok
     cols = 3 * nz * HD
     small = 3 * width + ff + cond.shape[-1]
     return pl.pallas_call(
-        partial(start_kernel, fs, nz, slots),
+        partial(forward_kernel, fs, nz, slots, 2),
         in_specs=[vmem, hbm] + [vmem] * 9 + [hbm] * 3,
-        out_specs=[vmem] * 9,
+        out_specs=[vmem] * 9 + [hbm] * 2,
         out_shape=[
             jax.ShapeDtypeStruct(head_shape, BF16),
-            jax.ShapeDtypeStruct((slots - 1, *head_shape), BF16),
+            jax.ShapeDtypeStruct((slots, nz, HD, tok), BF16),
+            jax.ShapeDtypeStruct((slots, nz, HD, tok), BF16),
+            jax.ShapeDtypeStruct((slots, nz, 1, tok), F32),
             jax.ShapeDtypeStruct((slots, fs, shard, cols), BF16),
             jax.ShapeDtypeStruct((tok, width), BF16),
             jax.ShapeDtypeStruct((8, width), F32),
             jax.ShapeDtypeStruct((ff // width, 1, width), F32),
             jax.ShapeDtypeStruct((fs, cond.shape[-1]), F32),
-            jax.ShapeDtypeStruct((shard, up.shape[1] + out.shape[1]), BF16),
-            jax.ShapeDtypeStruct(down.shape, BF16),
+            jax.ShapeDtypeStruct((fs, *pack_shape), BF16),
+            jax.ShapeDtypeStruct((fs, *down.shape), BF16),
         ],
         scratch_shapes=[
             wide(tok, width),
@@ -352,12 +478,23 @@
             dma(slots, pairs),
             dma(slots, pairs),
             dma(slots, fs),
-            dma(nz - 1),
-            dma(nz),
+            low(*pack_shape),
+            low(*down.shape),
+            low(length, HD),
+            dma(slots, nz - 1),
+            dma(slots, nz),
+            dma(slots, nz - 1),
+            dma(slots, nz),
+            dma(2, pairs),
+            dma(2, pairs),
+            dma(2, fs),
+            dma(2),
         ],
         compiler_params=pltpu.CompilerParams(vmem_limit_bytes=VMEM_LIMIT, collective_id=2, has_side_effects=True),
-        cost_estimate=pl.CostEstimate(flops=6 * tok * width * cols, bytes_accessed=10**8, transcendentals=0),
-        name="start",
+        cost_estimate=pl.CostEstimate(
+            flops=16 * slots * length * length * HD, bytes_accessed=10**7, transcendentals=slots * length * length
+        ),
+        name="forward",
     )(
         qkv_weight,
         tokens,
@@ -380,125 +517,6 @@
 
     each(nz - 1, hello)
     pl.semaphore_wait(barrier, nz - 1)
-
-
-def attend_kernel(n, slots, tok, sub, first_ref, rest_ref, x_ref, o_ref, mixed_ref, lse_ref, k_ref, x_s, x_r, o_s, o_r):
-    z = lax.axis_index("seq")
-    greet_seq(z, n)
-
-    def x_copy(s, i):
-        peer = lax.rem(z + 1 + i, n)
-        return remote(rest_ref.at[s - 1, peer], x_ref.at[s, z], x_s.at[s - 1, i], x_r.at[s - 1, z], seq=peer)
-
-    def x_arrival(s, i):
-        peer = lax.rem(z + 1 + i, n)
-        return remote(rest_ref.at[s - 1, peer], x_ref.at[s, peer], x_s.at[s - 1, i], x_r.at[s - 1, peer], seq=peer)
-
-    def o_copy(s, i):
-        peer = lax.rem(z + 1 + i, n)
-        return remote(o_ref.at[s, peer], mixed_ref.at[s, z], o_s.at[s, i], o_r.at[s, z], seq=peer)
-
-    def o_arrival(s, i):
-        peer = lax.rem(z + 1 + i, n)
-        return remote(o_ref.at[s, peer], mixed_ref.at[s, peer], o_s.at[s, i], o_r.at[s, peer], seq=peer)
-
-    for s in range(1, slots):
-        each(n - 1, lambda i: x_copy(s, i).start())
-    x_ref[0] = first_ref[...]
-    for s in range(1, slots):
-        x_ref[s, z] = rest_ref[s - 1, z]
-
-    scale = LOG2E / math.sqrt(HD)
-    width = tok // sub
-
-    def soft(s):
-        top = jnp.max(s, axis=0, keepdims=True) * scale
-        p = jnp.exp2(s * scale - top)
-        total = jnp.sum(p, axis=0, keepdims=True)
-        return top, total, p.astype(BF16)
-
-    def slot(s):
-        @pl.when(s > 0)
-        def _():
-            each(n - 1, lambda i: x_arrival(s, i).wait_recv())
-
-        for c in range(n):
-            k_ref[c * tok : (c + 1) * tok, :] = x_ref[s, c, HD : 2 * HD, :].T
-
-        def shard(i):
-            step = lax.rem(z + 1 + i, n)
-
-            def score(j):
-                q = x_ref[s, step, 0:HD, j * width : (j + 1) * width]
-                return mm(k_ref[...], q, 1, 0)
-
-            def mix(j, top, total, p):
-                o = None
-                for c in range(n):
-                    part = mm(x_ref[s, c, 2 * HD : 3 * HD, :], p[c * tok : (c + 1) * tok], 1, 0)
-                    o = part if o is None else o + part
-                o_ref[s, step, :, j * width : (j + 1) * width] = (o / total).astype(BF16)
-                lse_ref[s, step, :, j * width : (j + 1) * width] = top + jnp.log2(total)
-
-            scores = [score(0)]
-            pending = None
-            for j in range(sub):
-                if j + 1 < sub:
-                    scores.append(score(j + 1))
-                done = soft(scores[j])
-                if pending is not None:
-                    mix(j - 1, *pending)
-                pending = done
-            mix(sub - 1, *pending)
-
-            @pl.when(i < n - 1)
-            def _():
-                o_copy(s, i).start()
-
-        each(n, shard)
-        mixed_ref[s, z] = o_ref[s, z]
-
-    each(slots, slot)
-
-    def drain(s):
-        each(n - 1, lambda i: o_arrival(s, i).wait_recv())
-        each(n - 1, lambda i: o_copy(s, i).wait_send())
-
-    each(slots, drain)
-    for s in range(1, slots):
-        each(n - 1, lambda i: x_copy(s, i).wait_send())
-
-
-def attend(first, rest):
-    n, _, tok = first.shape
-    slots = rest.shape[0] + 1
-    length = n * tok
-    vmem = pl.BlockSpec(memory_space=pltpu.VMEM)
-    dma = lambda *shape: pltpu.SemaphoreType.DMA(shape)
-    head_shape = (slots, n, HD, tok)
-    return pl.pallas_call(
-        partial(attend_kernel, n, slots, tok, 2),
-        in_specs=[vmem] * 2,
-        out_specs=[vmem] * 4,
-        out_shape=[
-            jax.ShapeDtypeStruct((slots, n, 3 * HD, tok), BF16),
-            jax.ShapeDtypeStruct(head_shape, BF16),
-            jax.ShapeDtypeStruct(head_shape, BF16),
-            jax.ShapeDtypeStruct((slots, n, 1, tok), F32),
-        ],
-        scratch_shapes=[
-            pltpu.VMEM((length, HD), BF16),
-            dma(slots - 1, n - 1),
-            dma(slots - 1, n),
-            dma(slots, n - 1),
-            dma(slots, n),
-        ],
-        compiler_params=pltpu.CompilerParams(vmem_limit_bytes=VMEM_LIMIT, collective_id=3, has_side_effects=True),
-        cost_estimate=pl.CostEstimate(
-            flops=16 * slots * length * length * HD, bytes_accessed=10**7, transcendentals=slots * length * length
-        ),
-        name="attend",
-    )(first, rest)
 
 
 def attend_back_kernel(
@@ -792,10 +810,13 @@
 
 
 def reduce_kernel(fs, nz, slots, counts, lengths, *refs):
-    swapped_ref, w_hbm, attn_in_ref, tokens_hbm, hidden_hbm, vec_in_ref, sums_ref, up_bias_ref, *refs = refs
+    swapped_hbm, w_hbm, attn_in_hbm, tokens_hbm, hidden_hbm, vec_in_ref, sums_ref, up_bias_ref, *refs = refs
     bulk_refs, (mod_t_ref, cond_ref), refs = refs[:2], refs[2:4], refs[4:]
     inputs_out, qkv_out, up_out, out_out, down_out, total_out, mod_w_out, cond_out = refs[:8]
     (
+        swapped_ref,
+        attn_in_ref,
+        swap_s,
         row_buf,
         w_buf,
         tokens_buf,
@@ -854,6 +875,13 @@
     shard = g_buf.shape[3]
     groups = width // 128
 
+    def swap_load(s):
+        return pltpu.make_async_copy(swapped_hbm.at[s], swapped_ref.at[s], swap_s.at[s])
+
+    first_load = pltpu.make_async_copy(attn_in_hbm, attn_in_ref, local_s.at[3])
+    first_load.start()
+    for s in range(slots):
+        swap_load(s).start()
     fetch = ((w_hbm, w_buf), (tokens_hbm, tokens_buf), (hidden_hbm, hidden_buf))
     loads = [pltpu.make_async_copy(src, dst, local_s.at[i]) for i, (src, dst) in enumerate(fetch)]
     for load in loads:
@@ -927,7 +955,10 @@
     def peer_arrival(s, j):
         return remote(sum_buf.at[s, j], recv_buf.at[s, j], peer_s.at[s, j], peer_r.at[s, j], fsdp=2 * j + c)
 
+    first_load.wait()
+
     def project_grad(s):
+        swap_load(s).wait()
         for head in range(nz):
             for p in range(3):
                 base = (p * nz + head) * HD
@@ -937,18 +968,24 @@
             g_buf[s, i // 2, i % 2] = grad[i * shard : (i + 1) * shard]
         each(pairs, lambda i: pair_copy(s, lax.rem(k + 1 + i, pairs)).start())
 
-    each(slots, project_grad)
-
+
+    def forward(s, i):
+        j = lax.rem(k + 1 + i, pairs)
+        pair_copy(s, j).wait_recv()
+        sum_buf[s, j] = add_low(g_buf[s, j, c], pair_buf[s, j])
+        peer_copy(s, j).start()
+
+    def stage(s):
+        @pl.when(s < slots)
+        def _():
+            project_grad(s)
+
+        @pl.when(s > 0)
+        def _():
+            each(pairs - 1, lambda i: forward(s - 1, i))
+
+    each(slots + 1, stage)
     advance(1)
-
-    def forward(i):
-        j = lax.rem(k + 1 + i, pairs)
-        for s in range(slots):
-            pair_copy(s, j).wait_recv()
-            sum_buf[s, j] = add_low(g_buf[s, j, c], pair_buf[s, j])
-            peer_copy(s, j).start()
-
-    each(pairs - 1, forward)
     for load in loads:
         load.wait()
 
@@ -1148,7 +1185,7 @@
     cols = grad_rows.shape[1] * grad_rows.shape[2]
     inputs_grad, qkv_sum, up_sum, out_sum, down_sum, total, mod_w, cond_grad = pl.pallas_call(
         partial(reduce_kernel, fs, nz, slots, counts, lengths),
-        in_specs=[vmem, hbm, vmem, hbm, hbm] + [vmem] * 7,
+        in_specs=[hbm] * 5 + [vmem] * 7,
         out_specs=[vmem] * 8,
         out_shape=[
             jax.ShapeDtypeStruct((tok, width), F32),
@@ -1161,6 +1198,9 @@
             jax.ShapeDtypeStruct((8, 128), F32),
         ],
         scratch_shapes=[
+            low(*grad_rows.shape),
+            low(tok, width),
+            dma(slots),
             low(slots, cols, tok),
             low(slots, width, cols),
             wide(tok, width),
@@ -1179,7 +1219,7 @@
             wide(fs, rows, 128),
             wide(fs, 8, 128),
             wide(fs, 8, 128),
-            dma(3),
+            dma(4),
             dma(slots, pairs),
             dma(slots, pairs),
             dma(slots, pairs),
@@ -1220,7 +1260,6 @@
     tokens = inputs[0]
     tok, width = tokens.shape
     slots = H // n
-    gather = lambda a: lax.all_gather(a, "fsdp", axis=0, tiled=True)
 
     inv_freq = jnp.exp(-math.log(10000.0) * jnp.arange(HD // 2, dtype=F32) * (2.0 / HD))
     positions = jnp.arange(tok, dtype=F32)
@@ -1229,7 +1268,7 @@
     all_angles = inv_freq[None, :, None] * (positions[None, :] + starts[:, None])[:, None, :]
     cos_all, sin_all = jnp.cos(all_angles), jnp.sin(all_angles)
 
-    first, rest, qkv_slots, attn_in, vectors, up_bias_full, cond_low_all, pack_own, down_own = start(
+    x, heads_out, mixed, log_totals, qkv_slots, attn_in, vectors, up_bias_full, cond_low_all, pack, down = forward(
         qkv_weight,
         tokens,
         (attn_gain, mlp_gain, up_bias, down_bias),
@@ -1242,8 +1281,7 @@
         fs,
         n,
     )
-    down_full, w_pack = gather(down_own), gather(pack_own)
-    x, heads_out, mixed, log_totals = attend(first, rest)
+    w_pack, down_full = pack.reshape(width, -1), down.reshape(-1, width)
     output, grad_hidden, sums, up_bias_sum, g_down, g_pack, grad_mixed = middle(
         tokens, cotangent[0], vectors, up_bias_full, w_pack, down_full, mixed.reshape(width, tok)
     )

time: 391 us -> 388 us (level)
    pallas_call x1, Pallas kernels: 108 us -> 117 us  [attend_back(): pl.pallas_call(partial(attend_back_kernel, n, slots, tok, 2), in_specs=[v...]
    pallas_call x2 -> x1, Pallas kernels: 136 us -> 129 us  [forward(): pl.pallas_call(partial(forward_kernel, fs, nz, slots, 2), in_specs=[vmem,...]
  transfers between devices with their start and end apart: 4 -> 2, of which waited for: 1 -> 1; matrix products, arithmetic and copies ran while one was open for 1% -> 1% of each run, Pallas kernels for 51% -> 30%
where the time goes in v7:
time: 388 us
  Pallas kernels  353 us (91%)
  between operations  14.1 us (4%)
  local copies, waits for them, and re-layouts  11.6 us (3%)
  other arithmetic  4.87 us (1%)
  waiting for transfers between devices  4.71 us (1%)
    pallas_call x1, Pallas kernels, forward(): pl.pallas_call(partial(forward_kernel, fs, nz, slots, 2), in_specs=[vmem,...  129 us
    pallas_call x1, Pallas kernels, attend_back(): pl.pallas_call(partial(attend_back_kernel, n, slots, tok, 2), in_specs=[v...  117 us
    pallas_call x1, Pallas kernels, reduce_all(): pl.pallas_call(partial(reduce_kernel, fs, nz, slots, counts, lengths), in...  67.5 us
    pallas_call x1, Pallas kernels, middle(): pl.pallas_call(partial(middle_kernel, blocks), grid=(blocks + 1,), in_spe...  39.7 us
  transfers between devices with their start and end apart: 2, of which 1 were waited for; matrix products, arithmetic and copies ran while one was open for 1% of the time, Pallas kernels for 30%

profile of v7, /device:TPU:0, one launch (start us, length us, event | category | flops | bytes accessed | tf_op | source)
XLA Modules:
  0.0 387.9 jit_solution(14201882942737261277)
XLA Ops:
  7.2 0.0 reduce-scatter.5.cloned.1.call-start
  7.3 1.1 multiply_sine_fusion.1
  8.4 128.7 %forward.1 = (bf16[3,4,192,768]{3,2,1,0:T(8,128)(2,1)}, bf16[3,4,64,768]{3,2,1,0:T(8,128)(2,1)}, bf16[3,4,64,768]{3,2,1,0:T(8,128)(2,1)}, f32[3,4,1,768]{3,2,1,0...) custom-call(f32[96,2304]{1,0:T(8,128)} %refs_0_.1, ...), custom_call_target="tpu_custom_call" | custom-call | flops 28991029248 | bytes 10000000 | tf_op jit(solution)/shard_map/forward/pallas_call | solution.py:441
  137.1 39.7 %middle.1 = (f32[768,768]{1,0:T(8,128)}, f32[768,768]{1,0:T(8,128)}, f32[8,768]{1,0:T(8,128)}, f32[4,1,768]{2,1,0:T(1,128)}, bf16[3072,768]{1,0:T(8,128)(2,1)}, ...) custom-call(f32[768,768]{1,0:T(8,128)} %bitcast.29, f32[768,768]{1,0:T(8,128)} %bitcast.27, ...), custom_call_target="tpu_custom_call" | custom-call | flops 24461180928 | bytes 28311552 | tf_op jit(solution)/shard_map/middle/pallas_call | solution.py:769
  176.8 0.0 reduce-scatter.5.cloned.1.call-update
  176.8 0.0 reduce-scatter.3.cloned.1.call-start
  176.9 0.7 reduce-scatter.3.cloned.1.call-update
  177.6 0.1 iota_add_fusion
  177.7 2.5 multiply_sine_fusion
  180.1 116.7 %attend_back.1.refs_0_ = bf16[3,4,192,768]{3,2,1,0:T(8,128)(2,1)} custom-call(bf16[3,4,192,768]{3,2,1,0:T(8,128)(2,1)} %get-tuple-element.45.x_ref, bf16[3,4,64,768]{3,2,1,0:T(8,128)(2,1)} %bitcast.40, bf16[3,4,64,768]{3,2,1,0:T(8,128)(2,1)} %get-tuple-element.47.o_ref, f32[3,4,1,768]{3,2,1,0:T(1,128)} %get-tuple-element.48.lse_ref, ...), custom_call_target="tpu_custom_call" | custom-call | flops 72477573120 | bytes 10000000 | tf_op jit(solution)/shard_map/attend_back/pallas_call | solution.py:647
  296.8 0.0 reduce-scatter.5.cloned.1.call-done
  296.8 4.0 %reduce-scatter.3.cloned.1.call-done = bf16[96,3840]{1,0:T(8,128)(2,1)} async-done(((bf16[768,3840]{1,0:T(8,128)(2,1)}), bf16[96,3840]{1,0:T(8,128)(2,1)}) %reduce-scatter.3.cloned.1.call-update) | async-done | bytes 737296 | tf_op jit(solution)/shard_map/reduce_scatter | solution.py:1288
  300.8 67.5 %reduce_all.1 = (f32[768,768]{1,0:T(8,128)}, f32[96,2304]{1,0:T(8,128)}, f32[96,3072]{1,0:T(8,128)}, f32[96,768]{1,0:T(8,128)}, f32[384,768]{1,0:T(8,128)}, /*in...) custom-call(bf16[3,4,192,768]{3,2,1,0:T(8,128)(2,1)} %attend_back.1.refs_0_, bf16[3,768,768]{2,1,0:T(8,128)(2,1)} %bitcast.38, ...), custom_call_target="tpu_custom_call" | custom-call | flops 5435817984 | bytes 100000000 | tf_op jit(solution)/shard_map/reduce_all/pallas_call | solution.py:1186
  368.3 1.3 slice_bitcast_fusion
  369.6 1.3 slice_bitcast_fusion.1
  370.9 1.3 slice_bitcast_fusion.2
  372.1 0.0 copy-done.5
  372.1 1.2 fusion.1
  373.3 3.4 copy.32
  376.7 0.9 copy.33
  377.6 0.7 copy.34
  378.4 1.0 copy.35
  379.4 1.0 copy.36
  380.4 0.7 copy.37
  (14 shorter events, 0.0 us)
Async XLA Ops:
  7.2 289.7 %reduce-scatter.5.cloned.1.call-start = ((), (), s32[]{:S(2)}) async-start(), calls=%async_computation.3 | async-start | bytes 5308416 | tf_op jit(solution)/shard_map/reduce_scatter | solution.py:1288
  176.8 124.0 %reduce-scatter.3.cloned.1.call-start = ((), (), s32[]{:S(2)}) async-start(), calls=%async_computation.2 | async-start | bytes 6635520 | tf_op jit(solution)/shard_map/reduce_scatter | solution.py:1288
  300.8 71.3 %copy-start.5 = (f32[1,128]{1,0:T(1,128)S(1)}, f32[1,128]{1,0:T(1,128)}, u32[]{:S(2)}) copy-start(f32[1,128]{1,0:T(1,128)} %refs_6_.1) | copy-start | bytes 1540
  373.3 3.4 copy-start.2
  373.3 4.3 %copy-start.4 = (f32[96,768]{1,0:T(8,128)S(1)}, f32[96,768]{1,0:T(8,128)}, u32[]{:S(2)}) copy-start(f32[96,768]{1,0:T(8,128)} %get-tuple-element.91) | copy-start | bytes 884740
  373.3 5.0 %copy-start.1 = (f32[96,3072]{1,0:T(8,128)S(1)}, f32[96,3072]{1,0:T(8,128)}, u32[]{:S(2)}) copy-start(f32[96,3072]{1,0:T(8,128)} %get-tuple-element.92) | copy-start | bytes 3538948
  376.7 2.7 copy-start
  378.4 2.0 copy-start.3
Sparse Core Ops, SparseCore 0:
  177.0 60.7 reduce-scatter.4
  241.2 59.5 reduce-scatter.2

commit v8 on v7

--- a/solution.py
+++ b/solution.py
@@ -292,13 +292,14 @@
         each(nz - 1, lambda i: x_copy(s, i).start())
         x_ref[s, z] = z_send[s, z]
 
-    send_slot(0)
-
-    def later(i):
-        pass_weight(i + 1)
-        send_slot(i + 1)
-
-    each(slots - 1, later)
+    def next_slot(s):
+        @pl.when(s > 0)
+        def _():
+            pass_weight(s)
+
+        send_slot(s)
+
+    each(slots, next_slot)
 
     pack_own[:, :ff] = up_buf[...].astype(BF16)
     pack_own[:, ff:] = out_buf[...].astype(BF16)
@@ -508,18 +509,8 @@
     )
 
 
-def greet_seq(z, nz):
-    barrier = pltpu.get_barrier_semaphore()
-
-    def hello(i):
-        peer = {"seq": lax.rem(z + 1 + i, nz)}
-        pl.semaphore_signal(barrier, inc=1, device_id=peer, device_id_type=MESH)
-
-    each(nz - 1, hello)
-    pl.semaphore_wait(barrier, nz - 1)
-
-
 def attend_back_kernel(
+    fs,
     n,
     slots,
     tok,
@@ -530,13 +521,31 @@
     lse_ref,
     cos_ref,
     sin_ref,
+    pack_hbm,
+    down_hbm,
     out_ref,
+    part_pack,
+    part_down,
+    own_pack,
+    own_down,
+    pair_pack,
+    pair_down,
+    recv_pack,
+    recv_down,
+    own_s,
+    pair_s,
+    pair_r,
+    peer_s,
+    peer_r,
     g_ref,
     d_ref,
     k_ref,
     v_ref,
-    dk_ref,
-    dv_ref,
+    q_all,
+    g_all,
+    lse_all,
+    centre_all,
+    dq_ref,
     g_s,
     g_r,
     q_s,
@@ -546,7 +555,60 @@
 ):
     z = lax.axis_index("seq")
     half = HD // 2
-    greet_seq(z, n)
+    me = lax.axis_index("fsdp")
+    pairs = fs // 2
+    k, c = me // 2, lax.rem(me, 2)
+    partner = me + 1 - 2 * c
+    bulk = ((pack_hbm, own_pack, pair_pack, recv_pack, part_pack), (down_hbm, own_down, pair_down, recv_down, part_down))
+
+    def own_load(a, j):
+        return pltpu.make_async_copy(bulk[a][0].at[j, c], bulk[a][1].at[j], own_s.at[a, j])
+
+    def pair_copy(a, j):
+        return remote(bulk[a][0].at[j, 1 - c], bulk[a][2].at[j], pair_s.at[a, j], pair_r.at[a, j], fsdp=partner)
+
+    def peer_copy(a, j):
+        return remote(bulk[a][1].at[j], bulk[a][3].at[k], peer_s.at[a, j], peer_r.at[a, k], fsdp=2 * j + c)
+
+    def peer_arrival(a, j):
+        return remote(bulk[a][1].at[j], bulk[a][3].at[j], peer_s.at[a, j], peer_r.at[a, j], fsdp=2 * j + c)
+
+    def forward_bulk(a):
+        own, pair = bulk[a][1:3]
+
+        def one(i):
+            j = lax.rem(k + 1 + i, pairs)
+            own_load(a, j).wait()
+            pair_copy(a, j).wait_recv()
+            own[j] = add_low(own[j], pair[j])
+            peer_copy(a, j).start()
+
+        each(pairs - 1, one)
+
+    def finish_bulk(a):
+        _, own, pair, recv, part = bulk[a]
+        own_load(a, k).wait()
+        pair_copy(a, k).wait_recv()
+        each(pairs - 1, lambda i: peer_arrival(a, lax.rem(k + 1 + i, pairs)).wait_recv())
+        height = part.shape[0]
+        block = 32 if height % 32 == 0 else height
+
+        def one(b):
+            rows = pl.ds(b * block, block)
+            total = own[k, rows].astype(F32) + pair[k, rows].astype(F32)
+            for i in range(pairs - 1):
+                total = total + recv[lax.rem(k + 1 + i, pairs), rows].astype(F32)
+            part[rows, :] = total.astype(BF16)
+
+        each(height // block, one)
+
+    def drain_bulk(a):
+        each(pairs, lambda j: pair_copy(a, j).wait_send())
+        each(pairs - 1, lambda i: peer_copy(a, lax.rem(k + 1 + i, pairs)).wait_send())
+
+    for a in range(2):
+        each(pairs, lambda j: own_load(a, j).start())
+    greet(me, z, fs, n)
 
     def g_copy(s, i):
         peer = lax.rem(z + 1 + i, n)
@@ -570,6 +632,8 @@
     for s in range(slots):
         each(n - 1, lambda i: g_copy(s, i).start())
         g_ref[s, z] = sent_ref[s, z]
+    for a in range(2):
+        each(pairs, lambda i: pair_copy(a, lax.rem(k + 1 + i, pairs)).start())
 
     scale = LOG2E / math.sqrt(HD)
     width = tok // sub
@@ -579,52 +643,60 @@
         return (a * cosine + b * sine).astype(BF16), (b * cosine - a * sine).astype(BF16)
 
     def slot(s):
-        for c in range(n):
-            k_ref[c * tok : (c + 1) * tok, :] = x_ref[s, c, HD : 2 * HD, :].T
-            v_ref[c * tok : (c + 1) * tok, :] = x_ref[s, c, 2 * HD : 3 * HD, :].T
-        dk_ref[...] = jnp.zeros_like(dk_ref)
-        dv_ref[...] = jnp.zeros_like(dv_ref)
+        for owner in range(n):
+            cols = slice(owner * tok, (owner + 1) * tok)
+            k_ref[cols, :] = x_ref[s, owner, HD : 2 * HD, :].T
+            v_ref[cols, :] = x_ref[s, owner, 2 * HD : 3 * HD, :].T
+            q_all[:, cols] = x_ref[s, owner, 0:HD, :]
+            lse_all[:, cols] = lse_ref[s, owner]
         each(n - 1, lambda i: g_arrival(s, i).wait_recv())
+        for owner in range(n):
+            cols = slice(owner * tok, (owner + 1) * tok)
+            g = g_ref[s, owner]
+            g_all[:, cols] = g
+            centre_all[:, cols] = jnp.sum(g.astype(F32) * o_ref[s, owner].astype(F32), axis=0, keepdims=True)
+        dq_ref[...] = jnp.zeros_like(dq_ref)
 
         def shard(i):
             step = lax.rem(z + 1 + i, n)
             for j in range(sub):
                 cols = slice(j * width, (j + 1) * width)
-                q = x_ref[s, step, 0:HD, cols]
-                g = g_ref[s, step, :, cols]
-                o = o_ref[s, step, :, cols]
-                centre = jnp.sum(g.astype(F32) * o.astype(F32), axis=0, keepdims=True)
-                score = mm(k_ref[...], q, 1, 0)
-                dp = mm(v_ref[...], g, 1, 0)
-                p = jnp.exp2(score * scale - lse_ref[s, step, :, cols])
+                rows = pl.ds(pl.multiple_of(step * tok + j * width, width), width)
+                score = mm(k_ref[rows, :], q_all[...], 1, 0)
+                dp = mm(v_ref[rows, :], g_all[...], 1, 0)
+                p = jnp.exp2(score * scale - lse_all[...])
                 p_low = p.astype(BF16)
-                ds = (p * (dp - centre)).astype(BF16)
-                dv_ref[...] += mm(g, p_low, 1, 1)
-                dk_ref[...] += mm(q, ds, 1, 1)
-                dq = None
-                for c in range(n):
-                    part = mm(x_ref[s, c, HD : 2 * HD, :], ds[c * tok : (c + 1) * tok], 1, 0)
-                    dq = part if dq is None else dq + part
-                dq = dq * (1.0 / math.sqrt(HD))
-                a, b = turn_back(dq, cos_ref[step, :, cols], sin_ref[step, :, cols])
-                d_ref[s, step, 0:half, cols] = a
-                d_ref[s, step, half:HD, cols] = b
+                ds = (p * (dp - centre_all[...])).astype(BF16)
+                dv = mm(g_all[...], p_low, 1, 1)
+                dk = mm(q_all[...], ds, 1, 1) * (1.0 / math.sqrt(HD))
+                dq_ref[...] += mm(x_ref[s, step, HD : 2 * HD, cols], ds, 1, 0)
+                a, b = turn_back(dk, cos_ref[step, :, cols], sin_ref[step, :, cols])
+                d_ref[s, step, HD : HD + half, cols] = a
+                d_ref[s, step, HD + half : 2 * HD, cols] = b
+                d_ref[s, step, 2 * HD : 3 * HD, cols] = dv.astype(BF16)
 
             @pl.when(i < n - 1)
             def _():
-                q_copy(s, i).start()
+                kv_copy(s, i).start()
 
         each(n, shard)
-        for c in range(n):
-            dk = dk_ref[:, c * tok : (c + 1) * tok] * (1.0 / math.sqrt(HD))
-            a, b = turn_back(dk, cos_ref[c], sin_ref[c])
-            d_ref[s, c, HD : HD + half, :] = a
-            d_ref[s, c, HD + half : 2 * HD, :] = b
-            d_ref[s, c, 2 * HD : 3 * HD, :] = dv_ref[:, c * tok : (c + 1) * tok].astype(BF16)
-        each(n - 1, lambda i: kv_copy(s, i).start())
+        for owner in range(n):
+            dq = dq_ref[:, owner * tok : (owner + 1) * tok] * (1.0 / math.sqrt(HD))
+            a, b = turn_back(dq, cos_ref[owner], sin_ref[owner])
+            d_ref[s, owner, 0:half, :] = a
+            d_ref[s, owner, half:HD, :] = b
+        each(n - 1, lambda i: q_copy(s, i).start())
         out_ref[s, z] = d_ref[s, z]
 
+        @pl.when(s == 0)
+        def _():
+            for a in range(2):
+                forward_bulk(a)
+
     each(slots, slot)
+    for a in range(2):
+        finish_bulk(a)
+        drain_bulk(a)
 
     def drain(s):
         def one(i):
@@ -639,22 +711,34 @@
     each(slots, drain)
 
 
-def attend_back(x, g, o, lse, cosine, sine):
+def attend_back(x, g, o, lse, cosine, sine, g_pack, g_down, fs):
     slots, n, _, tok = x.shape
     length = n * tok
     vmem = pl.BlockSpec(memory_space=pltpu.VMEM)
     dma = lambda *shape: pltpu.SemaphoreType.DMA(shape)
+    pairs = fs // 2
+    shards = [(v.shape[0] // fs, v.shape[1]) for v in (g_pack, g_down)]
+    split = lambda v: v.reshape(pairs, 2, v.shape[0] // fs, v.shape[1])
     return pl.pallas_call(
-        partial(attend_back_kernel, n, slots, tok, 2),
-        in_specs=[vmem] * 6,
-        out_specs=vmem,
-        out_shape=jax.ShapeDtypeStruct(x.shape, BF16),
-        scratch_shapes=[
+        partial(attend_back_kernel, fs, n, slots, tok, 2),
+        in_specs=[vmem] * 6 + [pl.BlockSpec(memory_space=pl.ANY)] * 2,
+        out_specs=[vmem] * 3,
+        out_shape=[
+            jax.ShapeDtypeStruct(x.shape, BF16),
+            jax.ShapeDtypeStruct(shards[0], BF16),
+            jax.ShapeDtypeStruct(shards[1], BF16),
+        ],
+        scratch_shapes=[pltpu.VMEM((pairs, *shard), BF16) for shard in shards * 3]
+        + [dma(2, pairs)] * 5
+        + [
             pltpu.VMEM(g.shape, BF16),
             pltpu.VMEM(x.shape, BF16),
             pltpu.VMEM((length, HD), BF16),
             pltpu.VMEM((length, HD), BF16),
-            pltpu.VMEM((HD, length), F32),
+            pltpu.VMEM((HD, length), BF16),
+            pltpu.VMEM((HD, length), BF16),
+            pltpu.VMEM((1, length), F32),
+            pltpu.VMEM((1, length), F32),
             pltpu.VMEM((HD, length), F32),
         ]
         + [dma(slots, n - 1), dma(slots, n)] * 3,
@@ -663,7 +747,7 @@
             flops=40 * slots * length * length * HD, bytes_accessed=10**7, transcendentals=slots * length * length
         ),
         name="attend_back",
-    )(x, g, o, lse, cosine, sine)
+    )(x, g, o, lse, cosine, sine, split(g_pack), split(g_down))
 
 
 GELU_C = math.sqrt(2.0 / math.pi)
@@ -941,9 +1025,11 @@
                 for step, (n, item) in todo:
                     step(n, item)
 
+    half = len(early) - 2
+
     @pl.when(outer)
     def _():
-        for n, item in early:
+        for n, item in early[:half]:
             up_copy(n, item).start()
 
     def pair_copy(s, j):
@@ -1008,7 +1094,9 @@
         return back_sum, hat_sum
 
     zero = jnp.zeros((1, width), F32)
-    back_sum, hat_sum = lax.fori_loop(0, tok // piece, norm_piece, (zero, zero))
+    kept = lax.fori_loop(0, tok // piece - 1, norm_piece, (zero, zero))
+    advance(2)
+    back_sum, hat_sum = norm_piece(tok // piece - 1, kept)
 
     sums = [sums_ref[i : i + 1, :] for i in range(5)]
     vectors = [back_sum, hat_sum * attn_gain, sums[0], sums[1], sums[2] * mlp_gain, sums[3]]
@@ -1031,23 +1119,12 @@
 
     each(nz - 1, lambda i: vecz_copy(i).start())
 
-    advance(len(steps))
-    for s in range(slots):
-        pair_copy(s, k).wait_recv()
-        own = g_buf[s, k, c].astype(F32) + pair_buf[s, k].astype(F32)
-
-        def gather_in(i, acc):
-            j = lax.rem(k + 1 + i, pairs)
-            peer_arrival(s, j).wait_recv()
-            return acc + recv_buf[s, j].astype(F32)
-
-        own_buf[s] = lax.fori_loop(0, pairs - 1, gather_in, own).astype(BF16)
-
-        @pl.when(outer)
-        def _():
-            up_copy(*late[s]).start()
-
-    steps.extend(plan(late))
+    @pl.when(outer)
+    def _():
+        for n, item in early[half:]:
+            up_copy(n, item).start()
+
+    advance(max(0, len(steps) - 3))
     each(nz - 1, lambda i: vecz_arrival(i).wait_recv())
     summed = vec_z[0]
     for i in range(1, nz):
@@ -1063,7 +1140,26 @@
         return remote(vec_own, vec_all.at[peer], vec_s.at[i], vec_r.at[peer], fsdp=peer)
 
     each(fs - 1, lambda i: vec_copy(i).start())
-    advance(3)
+
+    def gather_slot(s):
+        pair_copy(s, k).wait_recv()
+        own = g_buf[s, k, c].astype(F32) + pair_buf[s, k].astype(F32)
+
+        def gather_in(i, acc):
+            j = lax.rem(k + 1 + i, pairs)
+            peer_arrival(s, j).wait_recv()
+            return acc + recv_buf[s, j].astype(F32)
+
+        own_buf[s] = lax.fori_loop(0, pairs - 1, gather_in, own).astype(BF16)
+
+        @pl.when(outer)
+        def _():
+            up = remote(own_buf.at[s], up_qkv.at[s], up_s.at[len(early) + s], up_r.at[len(early) + s], seq=mate)
+            up.start()
+
+    each(slots, gather_slot)
+    advance(len(steps))
+    steps.extend(plan(late))
 
     each(fs - 1, lambda i: vec_arrival(i).wait_recv())
     lane_from = lax.broadcasted_iota(jnp.int32, (256, 128), 0)
@@ -1106,6 +1202,24 @@
         return remote(cond_send.at[peer], cond_recv.at[peer], cond_s.at[i], cond_r.at[peer], fsdp=peer)
 
     each(fs - 1, lambda i: cond_copy(i).start())
+    advance(3)
+    ff = up_out.shape[1]
+
+    def write_pack(i):
+        rows = pl.ds(i * tot_pack.shape[1], tot_pack.shape[1])
+        up_out[rows, :] = tot_pack[i, :, :ff].astype(F32)
+        out_out[rows, :] = tot_pack[i, :, ff:].astype(F32)
+
+    def write_down(i):
+        down_out[pl.ds(i * tot_down.shape[1], tot_down.shape[1]), :] = tot_down[i].astype(F32)
+
+    @pl.when(outer)
+    def _():
+        for n, item in early:
+            tot_copy(n, item).wait_recv()
+
+    each(counts[0], write_pack)
+    each(counts[1], write_down)
     advance(len(steps))
     cond_recv[me] = cond_send[me]
     each(fs - 1, lambda i: cond_arrival(i).wait_recv())
@@ -1113,23 +1227,12 @@
 
     @pl.when(outer)
     def _():
+        for n, item in late:
+            tot_copy(n, item).wait_recv()
         for n, item in chain:
-            tot_copy(n, item).wait_recv()
             up_copy(n, item).wait_send()
 
     block = nz * HD
-    ff = up_out.shape[1]
-
-    def write_pack(i):
-        rows = pl.ds(i * tot_pack.shape[1], tot_pack.shape[1])
-        up_out[rows, :] = tot_pack[i, :, :ff].astype(F32)
-        out_out[rows, :] = tot_pack[i, :, ff:].astype(F32)
-
-    def write_down(i):
-        down_out[pl.ds(i * tot_down.shape[1], tot_down.shape[1]), :] = tot_down[i].astype(F32)
-
-    each(counts[0], write_pack)
-    each(counts[1], write_down)
     for s in range(slots):
         for p in range(3):
             columns = slice(p * width + s * block, p * width + (s + 1) * block)
@@ -1285,9 +1388,9 @@
     output, grad_hidden, sums, up_bias_sum, g_down, g_pack, grad_mixed = middle(
         tokens, cotangent[0], vectors, up_bias_full, w_pack, down_full, mixed.reshape(width, tok)
     )
-    scatter = lambda a: lax.psum_scatter(a, "fsdp", scatter_dimension=0, tiled=True)
-    part_down, part_pack = scatter(g_down), scatter(g_pack)
-    grad_slots = attend_back(x, grad_mixed.reshape(heads_out.shape), heads_out, log_totals, cos_all, sin_all)
+    grad_slots, part_pack, part_down = attend_back(
+        x, grad_mixed.reshape(heads_out.shape), heads_out, log_totals, cos_all, sin_all, g_pack, g_down, fs
+    )
     inputs_grad, qkv_weight_grad, up_sum, out_sum, down_sum, blocks, mod_weight_grad, cond_grad = reduce_all(
         grad_slots,
         qkv_slots.reshape(slots, width, -1),

time: 388 us -> 372 us (0.959)
  between operations: 14.1 us -> 0.71 us
  waiting for transfers between devices: 4.71 us -> 0 us
    reduce_scatter x2 -> x0, waiting for transfers between devices: 4 us -> none  [per_device(): lax.psum_scatter(a, 'fsdp', scatter_dimension=0, tiled=True)]
  transfers between devices with their start and end apart: 2 -> 0, of which waited for: 1 -> 0; matrix products, arithmetic and copies ran while one was open for 1% -> 0% of each run, Pallas kernels for 30% -> 0%
where the time goes in v8:
time: 372 us
  Pallas kernels  355 us (95%)
  local copies, waits for them, and re-layouts  11.6 us (3%)
  other arithmetic  4.68 us (1%)
    pallas_call x1, Pallas kernels, forward(): pl.pallas_call(partial(forward_kernel, fs, nz, slots, 2), in_specs=[vmem,...  129 us
    pallas_call x1, Pallas kernels, attend_back(): pl.pallas_call(partial(attend_back_kernel, fs, n, slots, tok, 2), in_spec...  120 us
    pallas_call x1, Pallas kernels, reduce_all(): pl.pallas_call(partial(reduce_kernel, fs, nz, slots, counts, lengths), in...  66.6 us
    pallas_call x1, Pallas kernels, middle(): pl.pallas_call(partial(middle_kernel, blocks), grid=(blocks + 1,), in_spe...  39.7 us
    unnamed x18, local copies, waits for them, and re-layouts  7.76 us

profile of v8, /device:TPU:0, one launch (start us, length us, event | category | flops | bytes accessed | tf_op | source)
XLA Modules:
  0.0 371.7 jit_solution(12576339726539164493)
XLA Ops:
  0.7 1.1 multiply_sine_fusion.1
  1.8 128.7 %forward.1 = (bf16[3,4,192,768]{3,2,1,0:T(8,128)(2,1)}, bf16[3,4,64,768]{3,2,1,0:T(8,128)(2,1)}, bf16[3,4,64,768]{3,2,1,0:T(8,128)(2,1)}, f32[3,4,1,768]{3,2,1,0...) custom-call(f32[96,2304]{1,0:T(8,128)} %refs_0_.1, ...), custom_call_target="tpu_custom_call" | custom-call | flops 28991029248 | bytes 10000000 | tf_op jit(solution)/shard_map/forward/pallas_call | solution.py:442
  130.5 39.7 %middle.1 = (f32[768,768]{1,0:T(8,128)}, f32[768,768]{1,0:T(8,128)}, f32[8,768]{1,0:T(8,128)}, f32[4,1,768]{2,1,0:T(1,128)}, bf16[3072,768]{1,0:T(8,128)(2,1)}, ...) custom-call(f32[768,768]{1,0:T(8,128)} %bitcast.31, f32[768,768]{1,0:T(8,128)} %bitcast.29, ...), custom_call_target="tpu_custom_call" | custom-call | flops 24461180928 | bytes 28311552 | tf_op jit(solution)/shard_map/middle/pallas_call | solution.py:853
  170.3 0.1 iota_add_fusion
  170.4 2.3 multiply_sine_fusion
  172.6 119.7 %attend_back.1 = (bf16[3,4,192,768]{3,2,1,0:T(8,128)(2,1)}, bf16[96,3840]{1,0:T(8,128)(2,1)}, bf16[384,768]{1,0:T(8,128)(2,1)}) custom-call(bf16[3,4,192,768]{3,2,1,0:T(8,128)(2,1)} %get-tuple-element.48.x_ref, bf16[3,4,64,768]{3,2,1,0:T(8,128)(2,1)} %bitcast.42, bf16[3,4,64,768]{3,2,1,0:T(8,128)(2,1)} %get-tuple-element.50.o_ref, ...), custom_call_target="tpu_custom_call" | custom-call | flops 72477573120 | bytes 10000000 | tf_op jit(solution)/shard_map/attend_back/pallas_call | solution.py:722
  292.3 0.0 copy-start.5
  292.3 66.6 %reduce_all.1 = (f32[768,768]{1,0:T(8,128)}, f32[96,2304]{1,0:T(8,128)}, f32[96,3072]{1,0:T(8,128)}, f32[96,768]{1,0:T(8,128)}, f32[384,768]{1,0:T(8,128)}, /*in...) custom-call(bf16[3,4,192,768]{3,2,1,0:T(8,128)(2,1)} %get-tuple-element.54.refs_0_, ...), custom_call_target="tpu_custom_call" | custom-call | flops 5435817984 | bytes 100000000 | tf_op jit(solution)/shard_map/reduce_all/pallas_call | solution.py:1289
  358.9 1.3 slice_bitcast_fusion
  360.2 1.3 slice_bitcast_fusion.1
  361.5 1.3 slice_bitcast_fusion.2
  362.8 0.0 copy-done.5
  362.8 1.2 fusion.1
  364.0 3.4 copy.32
  367.4 0.0 copy-done.2
  367.4 0.9 copy.33
  368.3 0.0 copy-done.4
  368.3 0.7 copy.34
  369.0 0.0 copy-done.1
  369.0 1.0 copy.35
  370.0 0.0 copy-done
  370.0 1.0 copy.36
  371.0 0.0 copy-done.3
  371.0 0.7 copy.37
  (8 shorter events, 0.0 us)
Async XLA Ops:
  292.3 70.5 %copy-start.5 = (f32[1,128]{1,0:T(1,128)S(1)}, f32[1,128]{1,0:T(1,128)}, u32[]{:S(2)}) copy-start(f32[1,128]{1,0:T(1,128)} %refs_6_.1) | copy-start | bytes 1540
  364.0 3.4 copy-start.2
  364.0 4.3 %copy-start.4 = (f32[96,768]{1,0:T(8,128)S(1)}, f32[96,768]{1,0:T(8,128)}, u32[]{:S(2)}) copy-start(f32[96,768]{1,0:T(8,128)} %get-tuple-element.97) | copy-start | bytes 884740
  364.0 5.0 %copy-start.1 = (f32[96,3072]{1,0:T(8,128)S(1)}, f32[96,3072]{1,0:T(8,128)}, u32[]{:S(2)}) copy-start(f32[96,3072]{1,0:T(8,128)} %get-tuple-element.98) | copy-start | bytes 3538948
  367.4 2.7 copy-start
  369.0 2.0 copy-start.3

commit v9 on v8

--- a/solution.py
+++ b/solution.py
@@ -85,12 +85,12 @@
         up_hbm,
         out_hbm,
         down_hbm,
-        x_ref,
-        o_ref,
+        x_hbm,
+        o_hbm,
         mixed_ref,
         lse_ref,
-        w_ref,
-        attn_in_ref,
+        w_hbm,
+        attn_in_hbm,
         vec_ref,
         bias_ref,
         cond_out,
@@ -98,6 +98,11 @@
         feed_hbm,
     ) = refs[:25]
     (
+        x_ref,
+        o_ref,
+        w_ref,
+        attn_in_ref,
+        store_s,
         tokens_buf,
         up_buf,
         out_buf,
@@ -300,6 +305,10 @@
         send_slot(s)
 
     each(slots, next_slot)
+    results = ((w_ref, w_hbm), (attn_in_ref, attn_in_hbm), (x_ref, x_hbm), (o_ref, o_hbm))
+    stores = [pltpu.make_async_copy(src, dst, store_s.at[i]) for i, (src, dst) in enumerate(results)]
+    for store in stores[:2]:
+        store.start()
 
     pack_own[:, :ff] = up_buf[...].astype(BF16)
     pack_own[:, ff:] = out_buf[...].astype(BF16)
@@ -392,6 +401,8 @@
             pass_bulk(0)
 
     each(slots, slot)
+    for store in stores[2:]:
+        store.start()
     pass_bulk(1)
 
     def drain_slots(s):
@@ -406,6 +417,8 @@
         each(pairs - 1, lambda i: p_pass(a, i).wait_send())
         p_partner(a).wait_send()
         p_own(a).wait()
+    for store in stores:
+        store.wait()
 
     def drain_peers(i):
         small_copy(i).wait_send()
@@ -442,7 +455,7 @@
     return pl.pallas_call(
         partial(forward_kernel, fs, nz, slots, 2),
         in_specs=[vmem, hbm] + [vmem] * 9 + [hbm] * 3,
-        out_specs=[vmem] * 9 + [hbm] * 2,
+        out_specs=[hbm, hbm, vmem, vmem, hbm, hbm, vmem, vmem, vmem, hbm, hbm],
         out_shape=[
             jax.ShapeDtypeStruct(head_shape, BF16),
             jax.ShapeDtypeStruct((slots, nz, HD, tok), BF16),
@@ -457,6 +470,11 @@
             jax.ShapeDtypeStruct((fs, *down.shape), BF16),
         ],
         scratch_shapes=[
+            low(*head_shape),
+            low(slots, nz, HD, tok),
+            low(slots, fs, shard, cols),
+            low(tok, width),
+            dma(4),
             wide(tok, width),
             wide(*up.shape),
             wide(*out.shape),
@@ -515,17 +533,22 @@
     slots,
     tok,
     sub,
-    x_ref,
+    x_hbm,
     sent_ref,
-    o_ref,
+    o_hbm,
     lse_ref,
-    cos_ref,
-    sin_ref,
+    cos_hbm,
+    sin_hbm,
     pack_hbm,
     down_hbm,
     out_ref,
     part_pack,
     part_down,
+    x_ref,
+    o_ref,
+    cos_ref,
+    sin_ref,
+    load_s,
     own_pack,
     own_down,
     pair_pack,
@@ -606,6 +629,10 @@
         each(pairs, lambda j: pair_copy(a, j).wait_send())
         each(pairs - 1, lambda i: peer_copy(a, lax.rem(k + 1 + i, pairs)).wait_send())
 
+    fetch = ((x_hbm, x_ref), (o_hbm, o_ref), (cos_hbm, cos_ref), (sin_hbm, sin_ref))
+    loads = [pltpu.make_async_copy(src, dst, load_s.at[i]) for i, (src, dst) in enumerate(fetch)]
+    for load in loads:
+        load.start()
     for a in range(2):
         each(pairs, lambda j: own_load(a, j).start())
     greet(me, z, fs, n)
@@ -693,6 +720,8 @@
             for a in range(2):
                 forward_bulk(a)
 
+    for load in loads:
+        load.wait()
     each(slots, slot)
     for a in range(2):
         finish_bulk(a)
@@ -714,21 +743,24 @@
 def attend_back(x, g, o, lse, cosine, sine, g_pack, g_down, fs):
     slots, n, _, tok = x.shape
     length = n * tok
-    vmem = pl.BlockSpec(memory_space=pltpu.VMEM)
+    vmem, hbm = pl.BlockSpec(memory_space=pltpu.VMEM), pl.BlockSpec(memory_space=pl.ANY)
     dma = lambda *shape: pltpu.SemaphoreType.DMA(shape)
     pairs = fs // 2
     shards = [(v.shape[0] // fs, v.shape[1]) for v in (g_pack, g_down)]
     split = lambda v: v.reshape(pairs, 2, v.shape[0] // fs, v.shape[1])
     return pl.pallas_call(
         partial(attend_back_kernel, fs, n, slots, tok, 2),
-        in_specs=[vmem] * 6 + [pl.BlockSpec(memory_space=pl.ANY)] * 2,
+        in_specs=[hbm, vmem, hbm, vmem] + [hbm] * 4,
         out_specs=[vmem] * 3,
         out_shape=[
             jax.ShapeDtypeStruct(x.shape, BF16),
             jax.ShapeDtypeStruct(shards[0], BF16),
             jax.ShapeDtypeStruct(shards[1], BF16),
         ],
-        scratch_shapes=[pltpu.VMEM((pairs, *shard), BF16) for shard in shards * 3]
+        scratch_shapes=[pltpu.VMEM(x.shape, BF16), pltpu.VMEM(o.shape, BF16)]
+        + [pltpu.VMEM(cosine.shape, F32)] * 2
+        + [dma(4)]
+        + [pltpu.VMEM((pairs, *shard), BF16) for shard in shards * 3]
         + [dma(2, pairs)] * 5
         + [
             pltpu.VMEM(g.shape, BF16),
@@ -896,8 +928,13 @@
 def reduce_kernel(fs, nz, slots, counts, lengths, *refs):
     swapped_hbm, w_hbm, attn_in_hbm, tokens_hbm, hidden_hbm, vec_in_ref, sums_ref, up_bias_ref, *refs = refs
     bulk_refs, (mod_t_ref, cond_ref), refs = refs[:2], refs[2:4], refs[4:]
-    inputs_out, qkv_out, up_out, out_out, down_out, total_out, mod_w_out, cond_out = refs[:8]
+    inputs_hbm, qkv_out, up_hbm, out_hbm, down_hbm, total_out, mod_w_out, cond_out = refs[:8]
     (
+        inputs_out,
+        up_out,
+        out_out,
+        down_out,
+        store_s,
         swapped_ref,
         attn_in_ref,
         swap_s,
@@ -980,7 +1017,8 @@
         )
         for i in range(count)
     ]
-    last = [(own_buf, up_qkv, part_qkv, twin_qkv, tot_qkv, s) for s in range(slots)]
+    halves = own_buf.shape[0] // slots
+    last = [(own_buf, up_qkv, part_qkv, twin_qkv, tot_qkv, i) for i in range(slots * halves)]
     chain = list(enumerate(bulk + last))
     early, late = chain[: len(bulk)], chain[len(bulk) :]
 
@@ -1009,10 +1047,11 @@
         tot_copy(n, item).start()
 
     def plan(items):
-        steps = [(chain_in, items[0])]
-        for before, item in zip(items[:-1], items[1:]):
+        ahead = 2
+        steps = [(chain_in, item) for item in items[:ahead]]
+        for before, item in zip(items, items[ahead:]):
             steps += [(chain_in, item), (chain_out, before)]
-        return steps + [(chain_out, items[-1])]
+        return steps + [(chain_out, item) for item in items[-ahead:]]
 
     steps = plan(early)
 
@@ -1025,7 +1064,7 @@
                 for step, (n, item) in todo:
                     step(n, item)
 
-    half = len(early) - 2
+    half = len(early) - len(early) // 3
 
     @pl.when(outer)
     def _():
@@ -1071,7 +1110,7 @@
             each(pairs - 1, lambda i: forward(s - 1, i))
 
     each(slots + 1, stage)
-    advance(1)
+    advance(3)
     for load in loads:
         load.wait()
 
@@ -1094,9 +1133,14 @@
         return back_sum, hat_sum
 
     zero = jnp.zeros((1, width), F32)
-    kept = lax.fori_loop(0, tok // piece - 1, norm_piece, (zero, zero))
-    advance(2)
-    back_sum, hat_sum = norm_piece(tok // piece - 1, kept)
+    kept = (zero, zero)
+    for i in range(tok // piece):
+        kept = norm_piece(i, kept)
+        advance(4)
+    back_sum, hat_sum = kept
+    results = ((inputs_out, inputs_hbm), (up_out, up_hbm), (out_out, out_hbm), (down_out, down_hbm))
+    stores = [pltpu.make_async_copy(src, dst, store_s.at[i]) for i, (src, dst) in enumerate(results)]
+    stores[0].start()
 
     sums = [sums_ref[i : i + 1, :] for i in range(5)]
     vectors = [back_sum, hat_sum * attn_gain, sums[0], sums[1], sums[2] * mlp_gain, sums[3]]
@@ -1124,7 +1168,7 @@
         for n, item in early[half:]:
             up_copy(n, item).start()
 
-    advance(max(0, len(steps) - 3))
+    advance(max(0, len(steps) - 5))
     each(nz - 1, lambda i: vecz_arrival(i).wait_recv())
     summed = vec_z[0]
     for i in range(1, nz):
@@ -1150,12 +1194,15 @@
             peer_arrival(s, j).wait_recv()
             return acc + recv_buf[s, j].astype(F32)
 
-        own_buf[s] = lax.fori_loop(0, pairs - 1, gather_in, own).astype(BF16)
-
-        @pl.when(outer)
-        def _():
-            up = remote(own_buf.at[s], up_qkv.at[s], up_s.at[len(early) + s], up_r.at[len(early) + s], seq=mate)
-            up.start()
+        own = lax.fori_loop(0, pairs - 1, gather_in, own).astype(BF16)
+        for h in range(halves):
+            i, n = halves * s + h, len(early) + halves * s + h
+            own_buf[i] = own[h * own_buf.shape[1] : (h + 1) * own_buf.shape[1]]
+            up = remote(own_buf.at[i], up_qkv.at[i], up_s.at[n], up_r.at[n], seq=mate)
+
+            @pl.when(outer)
+            def _(up=up):
+                up.start()
 
     each(slots, gather_slot)
     advance(len(steps))
@@ -1220,6 +1267,8 @@
 
     each(counts[0], write_pack)
     each(counts[1], write_down)
+    for store in stores[1:]:
+        store.start()
     advance(len(steps))
     cond_recv[me] = cond_send[me]
     each(fs - 1, lambda i: cond_arrival(i).wait_recv())
@@ -1233,10 +1282,12 @@
             up_copy(n, item).wait_send()
 
     block = nz * HD
-    for s in range(slots):
+    for i in range(slots * halves):
+        s, h = i // halves, i % halves
+        rows = slice(h * tot_qkv.shape[1], (h + 1) * tot_qkv.shape[1])
         for p in range(3):
             columns = slice(p * width + s * block, p * width + (s + 1) * block)
-            qkv_out[:, columns] = tot_qkv[s, :, p * block : (p + 1) * block].astype(F32)
+            qkv_out[rows, columns] = tot_qkv[i, :, p * block : (p + 1) * block].astype(F32)
 
     @pl.when(inner)
     def _():
@@ -1260,6 +1311,8 @@
     each(pairs, drain_pairs)
     each(pairs - 1, drain_sums)
     each(nz - 1, lambda i: vecz_copy(i).wait_send())
+    for store in stores:
+        store.wait()
 
 
 def reduce_all(
@@ -1268,12 +1321,13 @@
     slots = grad_rows.shape[0]
     tok, width = tokens.shape
     shard = width // fs
-    count = lambda a: 3 if a.shape[0] % 48 == 0 else 1
+    count = lambda a: 6 if a.shape[0] % 96 == 0 else 1
     counts = (count(part_pack), count(part_down))
     split = lambda a, n: a.reshape(n, a.shape[0] // n, a.shape[1])
     pack, down = split(part_pack, counts[0]), split(part_down, counts[1])
     pairs = fs // 2
-    items = sum(counts) + slots
+    halves = 2 if shard % 32 == 0 else 1
+    items = sum(counts) + slots * halves
     ff = up_bias_sum.size
     lengths = (6 * width, width, width, ff, width)
     rows = sum(lengths) // 128 + 2
@@ -1283,13 +1337,13 @@
     low = lambda *shape: pltpu.VMEM(shape, BF16)
     wide = lambda *shape: pltpu.VMEM(shape, F32)
     dma = lambda *shape: pltpu.SemaphoreType.DMA(shape)
-    qkv_shape = (slots, shard, width)
+    qkv_shape = (slots * halves, shard // halves, width)
     triple = [low(*pack.shape), low(*down.shape), low(*qkv_shape)]
     cols = grad_rows.shape[1] * grad_rows.shape[2]
     inputs_grad, qkv_sum, up_sum, out_sum, down_sum, total, mod_w, cond_grad = pl.pallas_call(
         partial(reduce_kernel, fs, nz, slots, counts, lengths),
         in_specs=[hbm] * 5 + [vmem] * 7,
-        out_specs=[vmem] * 8,
+        out_specs=[hbm, vmem, hbm, hbm, hbm, vmem, vmem, vmem],
         out_shape=[
             jax.ShapeDtypeStruct((tok, width), F32),
             jax.ShapeDtypeStruct((shard, 3 * width), F32),
@@ -1301,6 +1355,11 @@
             jax.ShapeDtypeStruct((8, 128), F32),
         ],
         scratch_shapes=[
+            wide(tok, width),
+            wide(shard, ff),
+            wide(shard, part_pack.shape[1] - ff),
+            wide(*part_down.shape),
+            dma(4),
             low(*grad_rows.shape),
             low(tok, width),
             dma(slots),

time: 372 us -> 365 us (0.981)
  Pallas kernels: 355 us -> 348 us
where the time goes in v9:
time: 365 us
  Pallas kernels  348 us (95%)
  local copies, waits for them, and re-layouts  11.6 us (3%)
  other arithmetic  4.68 us (1%)
    pallas_call x1, Pallas kernels, forward(): pl.pallas_call(partial(forward_kernel, fs, nz, slots, 2), in_specs=[vmem,...  126 us
    pallas_call x1, Pallas kernels, attend_back(): pl.pallas_call(partial(attend_back_kernel, fs, n, slots, tok, 2), in_spec...  118 us
    pallas_call x1, Pallas kernels, reduce_all(): pl.pallas_call(partial(reduce_kernel, fs, nz, slots, counts, lengths), in...  63.7 us
    pallas_call x1, Pallas kernels, middle(): pl.pallas_call(partial(middle_kernel, blocks), grid=(blocks + 1,), in_spe...  39.7 us
    unnamed x18, local copies, waits for them, and re-layouts  7.76 us

profile of v9, /device:TPU:0, one launch (start us, length us, event | category | flops | bytes accessed | tf_op | source)
XLA Modules:
  0.0 364.6 jit_solution(14194608054082735376)
XLA Ops:
  0.7 1.1 multiply_sine_fusion.1
  1.8 125.9 %forward.1 = (bf16[3,4,192,768]{3,2,1,0:T(8,128)(2,1)}, bf16[3,4,64,768]{3,2,1,0:T(8,128)(2,1)}, bf16[3,4,64,768]{3,2,1,0:T(8,128)(2,1)}, f32[3,4,1,768]{3,2,1,0...) custom-call(f32[96,2304]{1,0:T(8,128)} %refs_0_.1, ...), custom_call_target="tpu_custom_call" | custom-call | flops 28991029248 | bytes 10000000 | tf_op jit(solution)/shard_map/forward/pallas_call | solution.py:455
  127.6 39.7 %middle.1 = (f32[768,768]{1,0:T(8,128)}, f32[768,768]{1,0:T(8,128)}, f32[8,768]{1,0:T(8,128)}, f32[4,1,768]{2,1,0:T(1,128)}, bf16[3072,768]{1,0:T(8,128)(2,1)}, ...) custom-call(f32[768,768]{1,0:T(8,128)} %bitcast.31, f32[768,768]{1,0:T(8,128)} %bitcast.29, ...), custom_call_target="tpu_custom_call" | custom-call | flops 24461180928 | bytes 28311552 | tf_op jit(solution)/shard_map/middle/pallas_call | solution.py:885
  167.4 0.1 iota_add_fusion
  167.5 2.3 multiply_sine_fusion
  169.7 118.3 %attend_back.1 = (bf16[3,4,192,768]{3,2,1,0:T(8,128)(2,1)}, bf16[96,3840]{1,0:T(8,128)(2,1)}, bf16[384,768]{1,0:T(8,128)(2,1)}) custom-call(bf16[3,4,192,768]{3,2,1,0:T(8,128)(2,1)} %get-tuple-element.48.x_hbm, bf16[3,4,64,768]{3,2,1,0:T(8,128)(2,1)} %bitcast.42, bf16[3,4,64,768]{3,2,1,0:T(8,128)(2,1)} %get-tuple-element.50.o_hbm, ...), custom_call_target="tpu_custom_call" | custom-call | flops 72477573120 | bytes 10000000 | tf_op jit(solution)/shard_map/attend_back/pallas_call | solution.py:751
  288.1 0.0 copy-start.5
  288.1 63.7 %reduce_all.1 = (f32[768,768]{1,0:T(8,128)}, f32[96,2304]{1,0:T(8,128)}, f32[96,3072]{1,0:T(8,128)}, f32[96,768]{1,0:T(8,128)}, f32[384,768]{1,0:T(8,128)}, /*in...) custom-call(bf16[3,4,192,768]{3,2,1,0:T(8,128)(2,1)} %get-tuple-element.54.refs_0_, ...), custom_call_target="tpu_custom_call" | custom-call | flops 5435817984 | bytes 100000000 | tf_op jit(solution)/shard_map/reduce_all/pallas_call | solution.py:1343
  351.8 1.3 slice_bitcast_fusion
  353.1 1.3 slice_bitcast_fusion.1
  354.4 1.3 slice_bitcast_fusion.2
  355.7 0.0 copy-done.5
  355.7 1.2 fusion.1
  356.9 3.4 copy.32
  360.2 0.0 copy-done.2
  360.2 0.9 copy.33
  361.2 0.0 copy-done.4
  361.2 0.7 copy.34
  361.9 0.0 copy-done.1
  361.9 1.0 copy.35
  362.9 0.0 copy-done
  362.9 1.0 copy.36
  363.9 0.0 copy-done.3
  363.9 0.7 copy.37
  (8 shorter events, 0.0 us)
Async XLA Ops:
  288.1 67.6 %copy-start.5 = (f32[1,128]{1,0:T(1,128)S(1)}, f32[1,128]{1,0:T(1,128)}, u32[]{:S(2)}) copy-start(f32[1,128]{1,0:T(1,128)} %refs_6_.1) | copy-start | bytes 1540
  356.9 3.4 copy-start.2
  356.9 4.3 %copy-start.4 = (f32[96,768]{1,0:T(8,128)S(1)}, f32[96,768]{1,0:T(8,128)}, u32[]{:S(2)}) copy-start(f32[96,768]{1,0:T(8,128)} %get-tuple-element.97) | copy-start | bytes 884740
  356.9 5.0 %copy-start.1 = (f32[96,3072]{1,0:T(8,128)S(1)}, f32[96,3072]{1,0:T(8,128)}, u32[]{:S(2)}) copy-start(f32[96,3072]{1,0:T(8,128)} %get-tuple-element.98) | copy-start | bytes 3538948
  360.2 2.7 copy-start
  361.9 2.0 copy-start.3

commit v10 on v9

--- a/solution.py
+++ b/solution.py
@@ -232,7 +232,6 @@
     each(fs - 1, lambda i: mod_copy(i).start())
     for s in range(1, slots):
         send_weight(s)
-    pass_weight(0)
 
     attn_gain, mlp_gain, down_bias = (small_sum[:, i * width : (i + 1) * width] for i in range(3))
     for i in range(ff // width):
@@ -240,6 +239,13 @@
     for load in loads:
         load.wait()
     piece = min(256, tok)
+
+    def normed_piece(i):
+        rows = pl.ds(pl.multiple_of(i * piece, piece), piece)
+        tokens_buf[rows, :] = normalize(tokens_buf[rows, :])[0] * attn_gain
+
+    each(tok // piece, normed_piece)
+    pass_weight(0)
     each(fs - 1, lambda i: mod_arrival(i).wait_recv())
     modulation = jnp.sum(mod_recv[...], axis=0)
     shift_attn, scale_attn, gate_attn, shift_mlp, scale_mlp, gate_mlp = (
@@ -250,8 +256,7 @@
         vec_ref[i : i + 1, :] = v
     for i in range(tok // piece):
         rows = slice(i * piece, (i + 1) * piece)
-        hat, _ = normalize(tokens_buf[rows, :])
-        attn_in_ref[rows, :] = (hat * attn_gain * (1.0 + scale_attn) + shift_attn).astype(BF16)
+        attn_in_ref[rows, :] = (tokens_buf[rows, :] * (1.0 + scale_attn) + shift_attn).astype(BF16)
 
     cosine, sine = cos_ref[...], sin_ref[...]
     half = HD // 2
@@ -788,16 +793,16 @@
 
 def middle_kernel(
     blocks,
-    tokens_ref,
-    cot_ref,
+    tokens_hbm,
+    cot_hbm,
     vec_ref,
     bias_ref,
     up_ref,
     down_ref,
     out_w_ref,
     mixed_ref,
-    output_ref,
-    grad_hidden_ref,
+    output_hbm,
+    grad_hidden_hbm,
     sums_ref,
     bias_grad_ref,
     g_down_ref,
@@ -807,6 +812,11 @@
     mlp_in_ref,
     low_ref,
     back_ref,
+    tokens_ref,
+    cot_ref,
+    output_ref,
+    grad_hidden_ref,
+    copy_s,
 ):
     j = pl.program_id(0)
     tok, width = tokens_ref.shape
@@ -816,7 +826,13 @@
 
     @pl.when(j == 0)
     def _():
+        fetch = ((tokens_hbm, tokens_ref), (cot_hbm, cot_ref))
+        loads = [pltpu.make_async_copy(src, dst, copy_s.at[i]) for i, (src, dst) in enumerate(fetch)]
+        for load in loads:
+            load.start()
         attn_out_ref[...] = mm(mixed_ref[...], out_w_ref[...], 0, 0)
+        for load in loads:
+            load.wait()
 
         def prepare(i, _):
             rows = pl.ds(pl.multiple_of(i * piece, piece), piece)
@@ -869,9 +885,15 @@
         sums = lax.fori_loop(0, pieces, finish, (zero,) * 5)
         for i in range(5):
             sums_ref[i : i + 1, :] = sums[i]
+        results = ((output_ref, output_hbm), (grad_hidden_ref, grad_hidden_hbm))
+        stores = [pltpu.make_async_copy(src, dst, copy_s.at[2 + i]) for i, (src, dst) in enumerate(results)]
+        for store in stores:
+            store.start()
         attn_low = low_ref[...]
         g_pack_ref[...] = mm(mixed_ref[...], attn_low, 1, 0).astype(BF16)
         grad_mixed_ref[...] = mm(out_w_ref[...], attn_low, 1, 1).astype(BF16)
+        for store in stores:
+            store.wait()
 
 
 def middle(tokens, cot, vectors, up_bias, w_pack, w_down, mixed):
@@ -882,12 +904,13 @@
     fixed = lambda shape: pl.BlockSpec(shape, lambda j: (0,) * len(shape))
     last = blocks - 1
     flops = 2 * tok * width * (6 * ff + 3 * width)
+    hbm = pl.BlockSpec(memory_space=pl.ANY)
     return pl.pallas_call(
         partial(middle_kernel, blocks),
         grid=(blocks + 1,),
         in_specs=[
-            whole(tokens.shape),
-            whole(cot.shape),
+            hbm,
+            hbm,
             whole(vectors.shape),
             pl.BlockSpec((1, 1, width), lambda j: (jnp.minimum(j, last), 0, 0)),
             pl.BlockSpec((width, width), lambda j: (0, jnp.minimum(j, last))),
@@ -896,8 +919,8 @@
         ]
         + [whole(mixed.shape)],
         out_specs=[
-            fixed((tok, width)),
-            fixed((tok, width)),
+            hbm,
+            hbm,
             fixed((8, width)),
             pl.BlockSpec((1, 1, width), lambda j: (jnp.minimum(j, last), 0, 0)),
             pl.BlockSpec((width, width), lambda j: (jnp.minimum(j, last), 0)),
@@ -918,7 +941,9 @@
             pltpu.VMEM((tok, width), BF16),
             pltpu.VMEM((tok, width), BF16),
             pltpu.VMEM((tok, width), F32),
-        ],
+        ]
+        + [pltpu.VMEM((tok, width), F32)] * 4
+        + [pltpu.SemaphoreType.DMA((4,))],
         compiler_params=pltpu.CompilerParams(vmem_limit_bytes=VMEM_LIMIT),
         cost_estimate=pl.CostEstimate(flops=flops, bytes_accessed=6 * ff * width * 2, transcendentals=tok * ff),
         name="middle",

time: 365 us -> 363 us (level)
  no operation moved by 1% of the time
where the time goes in v10:
time: 363 us; the launch traced here: 362 us
  Pallas kernels  345 us (95%)
  local copies, waits for them, and re-layouts  11.6 us (3%)
  other arithmetic  4.68 us (1%)
    pallas_call x1, Pallas kernels, forward(): pl.pallas_call(partial(forward_kernel, fs, nz, slots, 2), in_specs=[vmem,...  125 us
    pallas_call x1, Pallas kernels, attend_back(): pl.pallas_call(partial(attend_back_kernel, fs, n, slots, tok, 2), in_spec...  118 us
    pallas_call x1, Pallas kernels, reduce_all(): pl.pallas_call(partial(reduce_kernel, fs, nz, slots, counts, lengths), in...  63.7 us
    pallas_call x1, Pallas kernels, middle(): pl.pallas_call(partial(middle_kernel, blocks), grid=(blocks + 1,), in_spe...  38.1 us
    unnamed x18, local copies, waits for them, and re-layouts  7.76 us

profile of v10, /device:TPU:0, one launch (start us, length us, event | category | flops | bytes accessed | tf_op | source)
XLA Modules:
  0.0 362.4 jit_solution(16790322544778014305)
XLA Ops:
  0.7 1.1 multiply_sine_fusion.1
  1.8 125.2 %forward.1 = (bf16[3,4,192,768]{3,2,1,0:T(8,128)(2,1)}, bf16[3,4,64,768]{3,2,1,0:T(8,128)(2,1)}, bf16[3,4,64,768]{3,2,1,0:T(8,128)(2,1)}, f32[3,4,1,768]{3,2,1,0...) custom-call(f32[96,2304]{1,0:T(8,128)} %refs_0_.1, ...), custom_call_target="tpu_custom_call" | custom-call | flops 28991029248 | bytes 10000000 | tf_op jit(solution)/shard_map/forward/pallas_call | solution.py:460
  127.0 38.1 %middle.1 = (f32[768,768]{1,0:T(8,128)}, f32[768,768]{1,0:T(8,128)}, f32[8,768]{1,0:T(8,128)}, f32[4,1,768]{2,1,0:T(1,128)}, bf16[3072,768]{1,0:T(8,128)(2,1)}, ...) custom-call(f32[768,768]{1,0:T(8,128)} %bitcast.31, f32[768,768]{1,0:T(8,128)} %bitcast.29, ...), custom_call_target="tpu_custom_call" | custom-call | flops 24461180928 | bytes 28311552 | tf_op jit(solution)/shard_map/middle/pallas_call | solution.py:908
  165.1 0.1 iota_add_fusion
  165.2 2.3 multiply_sine_fusion
  167.4 118.4 %attend_back.1 = (bf16[3,4,192,768]{3,2,1,0:T(8,128)(2,1)}, bf16[96,3840]{1,0:T(8,128)(2,1)}, bf16[384,768]{1,0:T(8,128)(2,1)}) custom-call(bf16[3,4,192,768]{3,2,1,0:T(8,128)(2,1)} %get-tuple-element.48.x_hbm, bf16[3,4,64,768]{3,2,1,0:T(8,128)(2,1)} %bitcast.42, bf16[3,4,64,768]{3,2,1,0:T(8,128)(2,1)} %get-tuple-element.50.o_hbm, ...), custom_call_target="tpu_custom_call" | custom-call | flops 72477573120 | bytes 10000000 | tf_op jit(solution)/shard_map/attend_back/pallas_call | solution.py:756
  285.8 0.0 copy-start.5
  285.9 63.7 %reduce_all.1 = (f32[768,768]{1,0:T(8,128)}, f32[96,2304]{1,0:T(8,128)}, f32[96,3072]{1,0:T(8,128)}, f32[96,768]{1,0:T(8,128)}, f32[384,768]{1,0:T(8,128)}, /*in...) custom-call(bf16[3,4,192,768]{3,2,1,0:T(8,128)(2,1)} %get-tuple-element.54.refs_0_, ...), custom_call_target="tpu_custom_call" | custom-call | flops 5435817984 | bytes 100000000 | tf_op jit(solution)/shard_map/reduce_all/pallas_call | solution.py:1368
  349.6 1.3 slice_bitcast_fusion
  350.9 1.3 slice_bitcast_fusion.1
  352.2 1.3 slice_bitcast_fusion.2
  353.4 0.0 copy-done.5
  353.4 1.2 fusion.1
  354.7 3.4 copy.32
  358.0 0.0 copy-done.2
  358.0 0.9 copy.33
  358.9 0.0 copy-done.4
  358.9 0.7 copy.34
  359.7 0.0 copy-done.1
  359.7 1.0 copy.35
  360.7 0.0 copy-done
  360.7 1.0 copy.36
  361.7 0.0 copy-done.3
  361.7 0.7 copy.37
  (8 shorter events, 0.0 us)
Async XLA Ops:
  285.8 67.6 %copy-start.5 = (f32[1,128]{1,0:T(1,128)S(1)}, f32[1,128]{1,0:T(1,128)}, u32[]{:S(2)}) copy-start(f32[1,128]{1,0:T(1,128)} %refs_6_.1) | copy-start | bytes 1540
  354.6 3.4 copy-start.2
  354.6 4.3 %copy-start.4 = (f32[96,768]{1,0:T(8,128)S(1)}, f32[96,768]{1,0:T(8,128)}, u32[]{:S(2)}) copy-start(f32[96,768]{1,0:T(8,128)} %get-tuple-element.97) | copy-start | bytes 884740
  354.6 5.0 %copy-start.1 = (f32[96,3072]{1,0:T(8,128)S(1)}, f32[96,3072]{1,0:T(8,128)}, u32[]{:S(2)}) copy-start(f32[96,3072]{1,0:T(8,128)} %get-tuple-element.98) | copy-start | bytes 3538948
  358.0 2.7 copy-start
  359.7 2.0 copy-start.3

commit v11 on v10

--- a/solution.py
+++ b/solution.py
@@ -1089,7 +1089,7 @@
                 for step, (n, item) in todo:
                     step(n, item)
 
-    half = len(early) - len(early) // 3
+    half = len(early) - 1
 
     @pl.when(outer)
     def _():

time: 363 us -> 363 us (level)
  no operation moved by 1% of the time
where the time goes in v11:
time: 363 us
  Pallas kernels  346 us (95%)
  local copies, waits for them, and re-layouts  11.6 us (3%)
  other arithmetic  4.68 us (1%)
    pallas_call x1, Pallas kernels, forward(): pl.pallas_call(partial(forward_kernel, fs, nz, slots, 2), in_specs=[vmem,...  125 us
    pallas_call x1, Pallas kernels, attend_back(): pl.pallas_call(partial(attend_back_kernel, fs, n, slots, tok, 2), in_spec...  118 us
    pallas_call x1, Pallas kernels, reduce_all(): pl.pallas_call(partial(reduce_kernel, fs, nz, slots, counts, lengths), in...  64.3 us
    pallas_call x1, Pallas kernels, middle(): pl.pallas_call(partial(middle_kernel, blocks), grid=(blocks + 1,), in_spe...  38.1 us
    unnamed x18, local copies, waits for them, and re-layouts  7.76 us

profile of v11, /device:TPU:0, one launch (start us, length us, event | category | flops | bytes accessed | tf_op | source)
XLA Modules:
  0.0 363.0 jit_solution(18375226260165833035)
XLA Ops:
  0.7 1.1 multiply_sine_fusion.1
  1.8 125.2 %forward.1 = (bf16[3,4,192,768]{3,2,1,0:T(8,128)(2,1)}, bf16[3,4,64,768]{3,2,1,0:T(8,128)(2,1)}, bf16[3,4,64,768]{3,2,1,0:T(8,128)(2,1)}, f32[3,4,1,768]{3,2,1,0...) custom-call(f32[96,2304]{1,0:T(8,128)} %refs_0_.1, ...), custom_call_target="tpu_custom_call" | custom-call | flops 28991029248 | bytes 10000000 | tf_op jit(solution)/shard_map/forward/pallas_call | solution.py:460
  127.0 38.1 %middle.1 = (f32[768,768]{1,0:T(8,128)}, f32[768,768]{1,0:T(8,128)}, f32[8,768]{1,0:T(8,128)}, f32[4,1,768]{2,1,0:T(1,128)}, bf16[3072,768]{1,0:T(8,128)(2,1)}, ...) custom-call(f32[768,768]{1,0:T(8,128)} %bitcast.31, f32[768,768]{1,0:T(8,128)} %bitcast.29, ...), custom_call_target="tpu_custom_call" | custom-call | flops 24461180928 | bytes 28311552 | tf_op jit(solution)/shard_map/middle/pallas_call | solution.py:908
  165.1 0.1 iota_add_fusion
  165.2 2.3 multiply_sine_fusion
  167.4 118.4 %attend_back.1 = (bf16[3,4,192,768]{3,2,1,0:T(8,128)(2,1)}, bf16[96,3840]{1,0:T(8,128)(2,1)}, bf16[384,768]{1,0:T(8,128)(2,1)}) custom-call(bf16[3,4,192,768]{3,2,1,0:T(8,128)(2,1)} %get-tuple-element.48.x_hbm, bf16[3,4,64,768]{3,2,1,0:T(8,128)(2,1)} %bitcast.42, bf16[3,4,64,768]{3,2,1,0:T(8,128)(2,1)} %get-tuple-element.50.o_hbm, ...), custom_call_target="tpu_custom_call" | custom-call | flops 72477573120 | bytes 10000000 | tf_op jit(solution)/shard_map/attend_back/pallas_call | solution.py:756
  285.8 0.0 copy-start.5
  285.9 64.3 %reduce_all.1 = (f32[768,768]{1,0:T(8,128)}, f32[96,2304]{1,0:T(8,128)}, f32[96,3072]{1,0:T(8,128)}, f32[96,768]{1,0:T(8,128)}, f32[384,768]{1,0:T(8,128)}, /*in...) custom-call(bf16[3,4,192,768]{3,2,1,0:T(8,128)(2,1)} %get-tuple-element.54.refs_0_, ...), custom_call_target="tpu_custom_call" | custom-call | flops 5435817984 | bytes 100000000 | tf_op jit(solution)/shard_map/reduce_all/pallas_call | solution.py:1368
  350.2 1.3 slice_bitcast_fusion
  351.5 1.3 slice_bitcast_fusion.1
  352.7 1.3 slice_bitcast_fusion.2
  354.0 0.0 copy-done.5
  354.0 1.2 fusion.1
  355.2 3.4 copy.32
  358.6 0.0 copy-done.2
  358.6 0.9 copy.33
  359.5 0.0 copy-done.4
  359.5 0.7 copy.34
  360.2 0.0 copy-done.1
  360.2 1.0 copy.35
  361.3 0.0 copy-done
  361.3 1.0 copy.36
  362.3 0.0 copy-done.3
  362.3 0.7 copy.37
  (8 shorter events, 0.0 us)
Async XLA Ops:
  285.8 68.2 %copy-start.5 = (f32[1,128]{1,0:T(1,128)S(1)}, f32[1,128]{1,0:T(1,128)}, u32[]{:S(2)}) copy-start(f32[1,128]{1,0:T(1,128)} %refs_6_.1) | copy-start | bytes 1540
  355.2 3.4 copy-start.2
  355.2 4.3 %copy-start.4 = (f32[96,768]{1,0:T(8,128)S(1)}, f32[96,768]{1,0:T(8,128)}, u32[]{:S(2)}) copy-start(f32[96,768]{1,0:T(8,128)} %get-tuple-element.97) | copy-start | bytes 884740
  355.2 5.0 %copy-start.1 = (f32[96,3072]{1,0:T(8,128)S(1)}, f32[96,3072]{1,0:T(8,128)}, u32[]{:S(2)}) copy-start(f32[96,3072]{1,0:T(8,128)} %get-tuple-element.98) | copy-start | bytes 3538948
  358.6 2.7 copy-start
  360.2 2.0 copy-start.3
